TPU v7x, 128 devices: a whole 4x4x4 slice. The times are simulated.
128 devices in a mesh: row: 4 (over y_hi, core), blk: 32 (over y_lo, z, x).
Axes of the slice: x: 4, y: 4 (y_hi: 2, y_lo: 2; y = y_hi * 2 + y_lo), z: 4, core: 2. Of those that a mesh axis runs over, the one named last changes fastest.
Arguments:
- coarse_cluster_means: bfloat16 [131072, 1024], P('blk', 'row'), may hold values from -16 to 16
- fine_cluster_means: bfloat16 [16384, 1024], P(('blk', 'row')), may hold values from -6 to 6
- block_panel_candidates: int32 [1024, 8], P(('blk', 'row')), may hold values from 0 to 31, all different within a row; in each aligned block of 8 rows (0 to 7, 8 to 15, ...) at most 4 rows name the same one
- softmax_heat: float32 [1], replicated, may hold values from 0.5 to 1
Outputs:
- revised_centroids: bfloat16 [16384, 1024], P(('blk', 'row'))
- log_norm: float32 [131072], P(('blk', 'row'))
Inputs may be any that keep to these rules, and one draw needn't show every extreme that they name: `block_panel_candidates`: each row names 8 different panels; within the rows of one device no panel is named by more than 4 rows, and in some device one panel is named by exactly 4 rows.
All inputs are finite; a program needn't handle non-finite values.
Results may differ from a plain program's by a relative error of at most 0.013.
Values may be sent and summed in bfloat16 or wider, within the bound.
No kernel may reach another device: no remote copies, remote signals or barrier semaphores. Data moves between devices by JAX's collectives and lax.ppermute only.
A program may use at most 128 MiB of HBM per device.

v0:
```python
import math

import jax
import jax.numpy as jnp
from jax import lax
from jax.sharding import PartitionSpec as P


def passed_along(shard, axis, by):
    peers = lax.axis_size(axis)
    return lax.ppermute(shard, axis, [(i, (i + by) % peers) for i in range(peers)])


def shards(coarse_cluster_means, fine_cluster_means, block_panel_candidates, softmax_heat):
    points = lax.all_to_all(coarse_cluster_means, "row", split_axis=0, concat_axis=1, tiled=True)
    rows_dev, vector_dimension = points.shape
    block_count, pair_count = block_panel_candidates.shape
    block_rows = rows_dev // block_count
    panel_rows = fine_cluster_means.shape[0]
    panels = lax.axis_size("blk")
    here = lax.axis_index("blk")
    slots = max(2, min(block_count, 2 * block_count * pair_count // panels))
    normalizing_multiplier = 1.0 / (softmax_heat[0] * math.sqrt(vector_dimension))
    blocks = points.reshape(block_count, block_rows, vector_dimension)
    block_ids = jnp.arange(block_count, dtype=jnp.int32)
    slot_ids = jnp.arange(slots, dtype=jnp.int32)

    def pick(owner):
        hits = jnp.any(block_panel_candidates == owner, axis=1)
        order = jnp.cumsum(hits.astype(jnp.int32)) - 1
        table = (order[None, :] == slot_ids[:, None]) & hits[None, :]
        index = jnp.sum(jnp.where(table, block_ids[None, :], 0), axis=1)
        valid = jnp.any(table, axis=1)
        chosen = jnp.take(blocks, index, axis=0).reshape(slots * block_rows, vector_dimension)
        return (hits, table, index, valid, chosen)

    def scores(chosen, panel):
        sqnorm = jnp.sum(jnp.square(panel.astype(jnp.float32)), axis=1)
        dots = jnp.einsum("rd,pd->rp", chosen, panel, preferred_element_type=jnp.float32)
        logit = (2.0 * dots - sqnorm[None, :]) * normalizing_multiplier
        return logit.reshape(slots, block_rows, panel_rows)

    def scout(state, panel, step):
        run_max, run_sum = state
        owner = (here - step) % panels
        hits, table, index, valid, chosen = pick(owner)
        logit = scores(chosen, panel)
        top = jnp.max(logit, axis=2)
        total = jnp.sum(jnp.exp(logit - top[:, :, None]), axis=2)
        spread = table.astype(jnp.float32)[:, :, None]
        top_back = jnp.sum(spread * top[:, None, :], axis=0)
        total_back = jnp.sum(spread * total[:, None, :], axis=0)
        newer = jnp.maximum(run_max, top_back)
        merged = run_sum * jnp.exp(run_max - newer) + total_back * jnp.exp(top_back - newer)
        chosen_rows = hits[:, None]
        return (jnp.where(chosen_rows, newer, run_max), jnp.where(chosen_rows, merged, run_sum))

    stash = jnp.zeros((1,), fine_cluster_means.dtype)
    start = (
        jnp.full((block_count, block_rows), -1e30, jnp.float32),
        jnp.zeros((block_count, block_rows), jnp.float32),
    )
    state = scout(start, fine_cluster_means, 0)

    def scout_turn(step, carry):
        panel, state, stash = carry
        panel = passed_along(panel, "blk", 1)
        return (panel, scout(state, panel, step), stash)

    outcome = lax.fori_loop(1, panels, scout_turn, (fine_cluster_means, state, stash))
    run_max, run_sum = outcome[1]
    stash = outcome[2]
    log_norm = run_max + jnp.log(run_sum)

    def weighted(panel, step):
        owner = (here - step) % panels
        hits, table, index, valid, chosen = pick(owner)
        logit = scores(chosen, panel)
        norm_rows = jnp.take(log_norm, index, axis=0)
        assign_weight = jnp.exp(logit - norm_rows[:, :, None])
        assign_weight = jnp.where(valid[:, None, None], assign_weight, 0.0).astype(jnp.bfloat16)
        flat = assign_weight.reshape(slots * block_rows, panel_rows)
        sums = lax.dot_general(
            flat, chosen, (((0,), (0,)), ((), ())), preferred_element_type=jnp.float32
        )
        mass = jnp.sum(flat.astype(jnp.float32), axis=0)
        return (sums, mass)

    def next_panel(panel):
        return passed_along(panel, "blk", 1)

    def add_sums(totals, added):
        moved = passed_along(totals, "blk", 1)
        return (moved[0] + added[0], moved[1] + added[1])

    totals = weighted(fine_cluster_means, 0)

    def sum_turn(step, carry):
        panel, totals = carry
        panel = next_panel(panel)
        return (panel, add_sums(totals, weighted(panel, step)))

    totals = lax.fori_loop(1, panels, sum_turn, (fine_cluster_means, totals))[1]
    sums, mass = passed_along((totals[0], totals[1]), "blk", 1)
    updated = ((sums + fine_cluster_means.astype(jnp.float32)) / (mass[:, None] + 1.0)).astype(
        jnp.bfloat16
    )
    return (updated, log_norm.reshape(rows_dev))


def solution(mesh):
    return jax.shard_map(
        shards,
        mesh=mesh,
        in_specs=(P("blk", "row"), P(("blk", "row"), None), P(("blk", "row"), None), P()),
        out_specs=(P(("blk", "row"), None), P(("blk", "row"))),
        check_vma=False,
    )
```

profile of v0, /device:TPU:16, one launch (start us, length us, event | category | flops | bytes accessed | tf_op | source)
XLA Modules:
  0.0 1092.8 jit_solution(599605015159850631)
XLA Ops:
  7.1 22.5 %all-to-all-done = bf16[4,1024,256]{2,1,0:T(8,128)(2,1)S(1)} async-done(((bf16[4,1024,256]{2,1,0:T(8,128)(2,1)}), bf16[4,1024,256]{2,1,0:T(8,128)(2,1)S(1)}, u32[]{:S(2)}, u32[]{:S(2)}) %all-to-all-start) | async-done | bytes 2097184 | tf_op jit(solution)/shard_map/all_to_all | solution.py:15
  40.3 381.9 %while.40 = (s32[]{:T(128)}, bf16[128,1024]{1,0:T(8,128)(2,1)S(1)}, f32[8,128]{1,0:T(8,128)S(1)}, f32[8,128]{1,0:T(8,128)S(1)}, s32[]{:T(128)}, /*index=5*/s32[8...) while((s32[]{:T(128)}, bf16[128,1024]{1,0:T(8,128)(2,1)S(1)}, ...), condition=%wide.region_18.20_spmd.clone, body=%wide.region_9.19_spmd.clone.sunk | while | flops 135551312 | bytes 7913618 | solution.py:70
  44.7 9.0 collective-permute-done
  57.5 8.9 collective-permute-done
  70.3 8.0 collective-permute-done
  82.1 7.7 collective-permute-done
  93.7 7.7 collective-permute-done
  105.2 7.7 collective-permute-done
  116.8 7.7 collective-permute-done
  128.4 8.1 collective-permute-done
  140.3 9.2 collective-permute-done
  153.3 10.3 collective-permute-done
  167.5 9.6 collective-permute-done
  181.0 8.8 collective-permute-done
  193.7 7.9 collective-permute-done
  205.5 7.7 collective-permute-done
  217.0 7.7 collective-permute-done
  228.6 7.7 collective-permute-done
  240.1 7.7 collective-permute-done
  251.7 8.2 collective-permute-done
  263.7 9.3 collective-permute-done
  276.9 10.4 collective-permute-done
  291.2 9.6 collective-permute-done
  304.7 8.8 collective-permute-done
  317.3 7.9 collective-permute-done
  329.1 7.7 collective-permute-done
  340.7 7.7 collective-permute-done
  352.2 7.7 collective-permute-done
  363.8 7.7 collective-permute-done
  375.3 8.2 collective-permute-done
  387.4 7.7 collective-permute-done
  398.9 7.9 collective-permute-done
  410.7 10.6 collective-permute-done
  424.4 652.9 %while.41 = (s32[]{:T(128)}, bf16[128,1024]{1,0:T(8,128)(2,1)S(1)}, f32[128,1024]{1,0:T(8,128)}, f32[128]{0:T(128)S(1)}, s32[]{:T(128)}, /*index=5*/s32[8,8]{1,0...) while((s32[]{:T(128)}, bf16[128,1024]{1,0:T(8,128)(2,1)S(1)}, ...), condition=%wide.region_27.30_spmd.clone, body=%wide.region_20.0_spmd.clone.sunk | while | flops 270207296 | bytes 12610566 | solution.py:103
  428.3 9.5 collective-permute-done.1
  438.5 9.7 collective-permute-done.3
  453.2 9.7 collective-permute-done.1
  463.7 8.8 collective-permute-done.3
  477.4 9.7 collective-permute-done.1
  487.8 7.8 collective-permute-done.3
  500.5 9.7 collective-permute-done.1
  522.7 9.7 collective-permute-done.1
  543.9 9.6 collective-permute-done.1
  564.1 8.6 collective-permute-done.1
  646.4 7.8 collective-permute-done.3
  666.7 8.9 collective-permute-done.3
  688.1 10.0 collective-permute-done.3
  711.1 10.5 collective-permute-done.3
  726.6 8.4 collective-permute-done.1
  735.8 10.5 collective-permute-done.3
  751.2 9.6 collective-permute-done.1
  761.6 10.5 collective-permute-done.3
  777.1 9.6 collective-permute-done.1
  787.4 9.6 collective-permute-done.3
  802.0 9.7 collective-permute-done.1
  812.5 8.6 collective-permute-done.3
  826.0 9.7 collective-permute-done.1
  849.1 9.7 collective-permute-done.1
  871.1 9.7 collective-permute-done.1
  892.2 9.4 collective-permute-done.1
  912.3 8.5 collective-permute-done.1
  994.6 7.9 collective-permute-done.3
  1015.1 8.8 collective-permute-done.3
  1077.3 13.7 %collective-permute-done.5 = f32[128]{0:T(128)S(1)} collective-permute-done((f32[128]{0:T(128)S(1)}, f32[128]{0:T(128)S(1)}, u32[]{:S(2)}, u32[]{:S(2)}) %collective-permute-start.5) | collective-permute-done | bytes 544 | tf_op jit(solution)/shard_map/ppermute | solution.py:11
  (1409 shorter events, 519.4 us)
Async XLA Ops:
  0.7 29.0 %all-to-all-start = ((bf16[4,1024,256]{2,1,0:T(8,128)(2,1)}), bf16[4,1024,256]{2,1,0:T(8,128)(2,1)S(1)}, u32[]{:S(2)}, u32[]{:S(2)}) async-start(bf16[4,1024,256]{2,1,0:T(8,128)(2,1)} %bitcast.88), calls=%async_computation | async-start | bytes 4194304 | tf_op jit(solution)/shard_map/all_to_all | solution.py:15
  424.4 23.9 %collective-permute-start.2 = (f32[128,1024]{1,0:T(8,128)}, f32[128,1024]{1,0:T(8,128)S(1)}, u32[]{:S(2)}, u32[]{:S(2)}) collective-permute-start(f32[128,1024]{1,0:T(8,128)} %get-tuple-element.832), channel_id=1, source_target_pairs={{0,1},{1,2},{2,3},{3,4},{4,5},{5,6},{6,7},{7,8},{8,9},{9,10},{10,1... | collective-permute-start | bytes 1572872 | tf_op jit(solution)/shard_map/while/body/eval_jaxpr/ppermute | solution.py:11
  424.4 23.9 %collective-permute-start.3 = (f32[128]{0:T(128)S(1)}, f32[128]{0:T(128)S(1)}, u32[]{:S(2)}, u32[]{:S(2)}) collective-permute-start(f32[128]{0:T(128)S(1)} %get-tuple-element.833), channel_id=1, source_target_pairs={{0,1},{1,2},{2,3},{3,4},{4,5},{5,6},{6,7},{7,8},{8,9},{9,10},{10,1... | collective-permute-start | bytes 1544 | tf_op jit(solution)/shard_map/while/body/eval_jaxpr/ppermute | solution.py:11
  449.4 23.0 %collective-permute-start.2 = (f32[128,1024]{1,0:T(8,128)}, f32[128,1024]{1,0:T(8,128)S(1)}, u32[]{:S(2)}, u32[]{:S(2)}) collective-permute-start(f32[128,1024]{1,0:T(8,128)} %get-tuple-element.832), channel_id=1, source_target_pairs={{0,1},{1,2},{2,3},{3,4},{4,5},{5,6},{6,7},{7,8},{8,9},{9,10},{10,1... | collective-permute-start | bytes 1572872 | tf_op jit(solution)/shard_map/while/body/eval_jaxpr/ppermute | solution.py:11
  449.4 23.0 %collective-permute-start.3 = (f32[128]{0:T(128)S(1)}, f32[128]{0:T(128)S(1)}, u32[]{:S(2)}, u32[]{:S(2)}) collective-permute-start(f32[128]{0:T(128)S(1)} %get-tuple-element.833), channel_id=1, source_target_pairs={{0,1},{1,2},{2,3},{3,4},{4,5},{5,6},{6,7},{7,8},{8,9},{9,10},{10,1... | collective-permute-start | bytes 1544 | tf_op jit(solution)/shard_map/while/body/eval_jaxpr/ppermute | solution.py:11
  473.6 22.0 %collective-permute-start.2 = (f32[128,1024]{1,0:T(8,128)}, f32[128,1024]{1,0:T(8,128)S(1)}, u32[]{:S(2)}, u32[]{:S(2)}) collective-permute-start(f32[128,1024]{1,0:T(8,128)} %get-tuple-element.832), channel_id=1, source_target_pairs={{0,1},{1,2},{2,3},{3,4},{4,5},{5,6},{6,7},{7,8},{8,9},{9,10},{10,1... | collective-permute-start | bytes 1572872 | tf_op jit(solution)/shard_map/while/body/eval_jaxpr/ppermute | solution.py:11
  473.6 22.0 %collective-permute-start.3 = (f32[128]{0:T(128)S(1)}, f32[128]{0:T(128)S(1)}, u32[]{:S(2)}, u32[]{:S(2)}) collective-permute-start(f32[128]{0:T(128)S(1)} %get-tuple-element.833), channel_id=1, source_target_pairs={{0,1},{1,2},{2,3},{3,4},{4,5},{5,6},{6,7},{7,8},{8,9},{9,10},{10,1... | collective-permute-start | bytes 1544 | tf_op jit(solution)/shard_map/while/body/eval_jaxpr/ppermute | solution.py:11
  496.7 21.0 %collective-permute-start.2 = (f32[128,1024]{1,0:T(8,128)}, f32[128,1024]{1,0:T(8,128)S(1)}, u32[]{:S(2)}, u32[]{:S(2)}) collective-permute-start(f32[128,1024]{1,0:T(8,128)} %get-tuple-element.832), channel_id=1, source_target_pairs={{0,1},{1,2},{2,3},{3,4},{4,5},{5,6},{6,7},{7,8},{8,9},{9,10},{10,1... | collective-permute-start | bytes 1572872 | tf_op jit(solution)/shard_map/while/body/eval_jaxpr/ppermute | solution.py:11
  496.7 21.0 %collective-permute-start.3 = (f32[128]{0:T(128)S(1)}, f32[128]{0:T(128)S(1)}, u32[]{:S(2)}, u32[]{:S(2)}) collective-permute-start(f32[128]{0:T(128)S(1)} %get-tuple-element.833), channel_id=1, source_target_pairs={{0,1},{1,2},{2,3},{3,4},{4,5},{5,6},{6,7},{7,8},{8,9},{9,10},{10,1... | collective-permute-start | bytes 1544 | tf_op jit(solution)/shard_map/while/body/eval_jaxpr/ppermute | solution.py:11
  518.9 20.0 %collective-permute-start.2 = (f32[128,1024]{1,0:T(8,128)}, f32[128,1024]{1,0:T(8,128)S(1)}, u32[]{:S(2)}, u32[]{:S(2)}) collective-permute-start(f32[128,1024]{1,0:T(8,128)} %get-tuple-element.832), channel_id=1, source_target_pairs={{0,1},{1,2},{2,3},{3,4},{4,5},{5,6},{6,7},{7,8},{8,9},{9,10},{10,1... | collective-permute-start | bytes 1572872 | tf_op jit(solution)/shard_map/while/body/eval_jaxpr/ppermute | solution.py:11
  518.9 20.0 %collective-permute-start.3 = (f32[128]{0:T(128)S(1)}, f32[128]{0:T(128)S(1)}, u32[]{:S(2)}, u32[]{:S(2)}) collective-permute-start(f32[128]{0:T(128)S(1)} %get-tuple-element.833), channel_id=1, source_target_pairs={{0,1},{1,2},{2,3},{3,4},{4,5},{5,6},{6,7},{7,8},{8,9},{9,10},{10,1... | collective-permute-start | bytes 1544 | tf_op jit(solution)/shard_map/while/body/eval_jaxpr/ppermute | solution.py:11
  540.1 19.0 %collective-permute-start.2 = (f32[128,1024]{1,0:T(8,128)}, f32[128,1024]{1,0:T(8,128)S(1)}, u32[]{:S(2)}, u32[]{:S(2)}) collective-permute-start(f32[128,1024]{1,0:T(8,128)} %get-tuple-element.832), channel_id=1, source_target_pairs={{0,1},{1,2},{2,3},{3,4},{4,5},{5,6},{6,7},{7,8},{8,9},{9,10},{10,1... | collective-permute-start | bytes 1572872 | tf_op jit(solution)/shard_map/while/body/eval_jaxpr/ppermute | solution.py:11
  540.1 19.0 %collective-permute-start.3 = (f32[128]{0:T(128)S(1)}, f32[128]{0:T(128)S(1)}, u32[]{:S(2)}, u32[]{:S(2)}) collective-permute-start(f32[128]{0:T(128)S(1)} %get-tuple-element.833), channel_id=1, source_target_pairs={{0,1},{1,2},{2,3},{3,4},{4,5},{5,6},{6,7},{7,8},{8,9},{9,10},{10,1... | collective-permute-start | bytes 1544 | tf_op jit(solution)/shard_map/while/body/eval_jaxpr/ppermute | solution.py:11
  560.3 18.0 %collective-permute-start.2 = (f32[128,1024]{1,0:T(8,128)}, f32[128,1024]{1,0:T(8,128)S(1)}, u32[]{:S(2)}, u32[]{:S(2)}) collective-permute-start(f32[128,1024]{1,0:T(8,128)} %get-tuple-element.832), channel_id=1, source_target_pairs={{0,1},{1,2},{2,3},{3,4},{4,5},{5,6},{6,7},{7,8},{8,9},{9,10},{10,1... | collective-permute-start | bytes 1572872 | tf_op jit(solution)/shard_map/while/body/eval_jaxpr/ppermute | solution.py:11
  560.3 18.0 %collective-permute-start.3 = (f32[128]{0:T(128)S(1)}, f32[128]{0:T(128)S(1)}, u32[]{:S(2)}, u32[]{:S(2)}) collective-permute-start(f32[128]{0:T(128)S(1)} %get-tuple-element.833), channel_id=1, source_target_pairs={{0,1},{1,2},{2,3},{3,4},{4,5},{5,6},{6,7},{7,8},{8,9},{9,10},{10,1... | collective-permute-start | bytes 1544 | tf_op jit(solution)/shard_map/while/body/eval_jaxpr/ppermute | solution.py:11
  579.5 17.0 %collective-permute-start.2 = (f32[128,1024]{1,0:T(8,128)}, f32[128,1024]{1,0:T(8,128)S(1)}, u32[]{:S(2)}, u32[]{:S(2)}) collective-permute-start(f32[128,1024]{1,0:T(8,128)} %get-tuple-element.832), channel_id=1, source_target_pairs={{0,1},{1,2},{2,3},{3,4},{4,5},{5,6},{6,7},{7,8},{8,9},{9,10},{10,1... | collective-permute-start | bytes 1572872 | tf_op jit(solution)/shard_map/while/body/eval_jaxpr/ppermute | solution.py:11
  579.5 17.0 %collective-permute-start.3 = (f32[128]{0:T(128)S(1)}, f32[128]{0:T(128)S(1)}, u32[]{:S(2)}, u32[]{:S(2)}) collective-permute-start(f32[128]{0:T(128)S(1)} %get-tuple-element.833), channel_id=1, source_target_pairs={{0,1},{1,2},{2,3},{3,4},{4,5},{5,6},{6,7},{7,8},{8,9},{9,10},{10,1... | collective-permute-start | bytes 1544 | tf_op jit(solution)/shard_map/while/body/eval_jaxpr/ppermute | solution.py:11
  597.7 17.0 %collective-permute-start.2 = (f32[128,1024]{1,0:T(8,128)}, f32[128,1024]{1,0:T(8,128)S(1)}, u32[]{:S(2)}, u32[]{:S(2)}) collective-permute-start(f32[128,1024]{1,0:T(8,128)} %get-tuple-element.832), channel_id=1, source_target_pairs={{0,1},{1,2},{2,3},{3,4},{4,5},{5,6},{6,7},{7,8},{8,9},{9,10},{10,1... | collective-permute-start | bytes 1572872 | tf_op jit(solution)/shard_map/while/body/eval_jaxpr/ppermute | solution.py:11
  597.7 17.0 %collective-permute-start.3 = (f32[128]{0:T(128)S(1)}, f32[128]{0:T(128)S(1)}, u32[]{:S(2)}, u32[]{:S(2)}) collective-permute-start(f32[128]{0:T(128)S(1)} %get-tuple-element.833), channel_id=1, source_target_pairs={{0,1},{1,2},{2,3},{3,4},{4,5},{5,6},{6,7},{7,8},{8,9},{9,10},{10,1... | collective-permute-start | bytes 1544 | tf_op jit(solution)/shard_map/while/body/eval_jaxpr/ppermute | solution.py:11
  615.8 18.1 %collective-permute-start.2 = (f32[128,1024]{1,0:T(8,128)}, f32[128,1024]{1,0:T(8,128)S(1)}, u32[]{:S(2)}, u32[]{:S(2)}) collective-permute-start(f32[128,1024]{1,0:T(8,128)} %get-tuple-element.832), channel_id=1, source_target_pairs={{0,1},{1,2},{2,3},{3,4},{4,5},{5,6},{6,7},{7,8},{8,9},{9,10},{10,1... | collective-permute-start | bytes 1572872 | tf_op jit(solution)/shard_map/while/body/eval_jaxpr/ppermute | solution.py:11
  615.8 18.1 %collective-permute-start.3 = (f32[128]{0:T(128)S(1)}, f32[128]{0:T(128)S(1)}, u32[]{:S(2)}, u32[]{:S(2)}) collective-permute-start(f32[128]{0:T(128)S(1)} %get-tuple-element.833), channel_id=1, source_target_pairs={{0,1},{1,2},{2,3},{3,4},{4,5},{5,6},{6,7},{7,8},{8,9},{9,10},{10,1... | collective-permute-start | bytes 1544 | tf_op jit(solution)/shard_map/while/body/eval_jaxpr/ppermute | solution.py:11
  635.1 19.2 %collective-permute-start.2 = (f32[128,1024]{1,0:T(8,128)}, f32[128,1024]{1,0:T(8,128)S(1)}, u32[]{:S(2)}, u32[]{:S(2)}) collective-permute-start(f32[128,1024]{1,0:T(8,128)} %get-tuple-element.832), channel_id=1, source_target_pairs={{0,1},{1,2},{2,3},{3,4},{4,5},{5,6},{6,7},{7,8},{8,9},{9,10},{10,1... | collective-permute-start | bytes 1572872 | tf_op jit(solution)/shard_map/while/body/eval_jaxpr/ppermute | solution.py:11
  635.1 19.1 %collective-permute-start.3 = (f32[128]{0:T(128)S(1)}, f32[128]{0:T(128)S(1)}, u32[]{:S(2)}, u32[]{:S(2)}) collective-permute-start(f32[128]{0:T(128)S(1)} %get-tuple-element.833), channel_id=1, source_target_pairs={{0,1},{1,2},{2,3},{3,4},{4,5},{5,6},{6,7},{7,8},{8,9},{9,10},{10,1... | collective-permute-start | bytes 1544 | tf_op jit(solution)/shard_map/while/body/eval_jaxpr/ppermute | solution.py:11
  655.4 20.2 %collective-permute-start.2 = (f32[128,1024]{1,0:T(8,128)}, f32[128,1024]{1,0:T(8,128)S(1)}, u32[]{:S(2)}, u32[]{:S(2)}) collective-permute-start(f32[128,1024]{1,0:T(8,128)} %get-tuple-element.832), channel_id=1, source_target_pairs={{0,1},{1,2},{2,3},{3,4},{4,5},{5,6},{6,7},{7,8},{8,9},{9,10},{10,1... | collective-permute-start | bytes 1572872 | tf_op jit(solution)/shard_map/while/body/eval_jaxpr/ppermute | solution.py:11
  655.4 20.2 %collective-permute-start.3 = (f32[128]{0:T(128)S(1)}, f32[128]{0:T(128)S(1)}, u32[]{:S(2)}, u32[]{:S(2)}) collective-permute-start(f32[128]{0:T(128)S(1)} %get-tuple-element.833), channel_id=1, source_target_pairs={{0,1},{1,2},{2,3},{3,4},{4,5},{5,6},{6,7},{7,8},{8,9},{9,10},{10,1... | collective-permute-start | bytes 1544 | tf_op jit(solution)/shard_map/while/body/eval_jaxpr/ppermute | solution.py:11
  676.8 21.3 %collective-permute-start.2 = (f32[128,1024]{1,0:T(8,128)}, f32[128,1024]{1,0:T(8,128)S(1)}, u32[]{:S(2)}, u32[]{:S(2)}) collective-permute-start(f32[128,1024]{1,0:T(8,128)} %get-tuple-element.832), channel_id=1, source_target_pairs={{0,1},{1,2},{2,3},{3,4},{4,5},{5,6},{6,7},{7,8},{8,9},{9,10},{10,1... | collective-permute-start | bytes 1572872 | tf_op jit(solution)/shard_map/while/body/eval_jaxpr/ppermute | solution.py:11
  676.8 21.3 %collective-permute-start.3 = (f32[128]{0:T(128)S(1)}, f32[128]{0:T(128)S(1)}, u32[]{:S(2)}, u32[]{:S(2)}) collective-permute-start(f32[128]{0:T(128)S(1)} %get-tuple-element.833), channel_id=1, source_target_pairs={{0,1},{1,2},{2,3},{3,4},{4,5},{5,6},{6,7},{7,8},{8,9},{9,10},{10,1... | collective-permute-start | bytes 1544 | tf_op jit(solution)/shard_map/while/body/eval_jaxpr/ppermute | solution.py:11
  699.2 22.4 %collective-permute-start.2 = (f32[128,1024]{1,0:T(8,128)}, f32[128,1024]{1,0:T(8,128)S(1)}, u32[]{:S(2)}, u32[]{:S(2)}) collective-permute-start(f32[128,1024]{1,0:T(8,128)} %get-tuple-element.832), channel_id=1, source_target_pairs={{0,1},{1,2},{2,3},{3,4},{4,5},{5,6},{6,7},{7,8},{8,9},{9,10},{10,1... | collective-permute-start | bytes 1572872 | tf_op jit(solution)/shard_map/while/body/eval_jaxpr/ppermute | solution.py:11
  699.2 22.4 %collective-permute-start.3 = (f32[128]{0:T(128)S(1)}, f32[128]{0:T(128)S(1)}, u32[]{:S(2)}, u32[]{:S(2)}) collective-permute-start(f32[128]{0:T(128)S(1)} %get-tuple-element.833), channel_id=1, source_target_pairs={{0,1},{1,2},{2,3},{3,4},{4,5},{5,6},{6,7},{7,8},{8,9},{9,10},{10,1... | collective-permute-start | bytes 1544 | tf_op jit(solution)/shard_map/while/body/eval_jaxpr/ppermute | solution.py:11
  722.8 23.5 %collective-permute-start.2 = (f32[128,1024]{1,0:T(8,128)}, f32[128,1024]{1,0:T(8,128)S(1)}, u32[]{:S(2)}, u32[]{:S(2)}) collective-permute-start(f32[128,1024]{1,0:T(8,128)} %get-tuple-element.832), channel_id=1, source_target_pairs={{0,1},{1,2},{2,3},{3,4},{4,5},{5,6},{6,7},{7,8},{8,9},{9,10},{10,1... | collective-permute-start | bytes 1572872 | tf_op jit(solution)/shard_map/while/body/eval_jaxpr/ppermute | solution.py:11
  722.8 23.5 %collective-permute-start.3 = (f32[128]{0:T(128)S(1)}, f32[128]{0:T(128)S(1)}, u32[]{:S(2)}, u32[]{:S(2)}) collective-permute-start(f32[128]{0:T(128)S(1)} %get-tuple-element.833), channel_id=1, source_target_pairs={{0,1},{1,2},{2,3},{3,4},{4,5},{5,6},{6,7},{7,8},{8,9},{9,10},{10,1... | collective-permute-start | bytes 1544 | tf_op jit(solution)/shard_map/while/body/eval_jaxpr/ppermute | solution.py:11
  747.5 24.7 %collective-permute-start.2 = (f32[128,1024]{1,0:T(8,128)}, f32[128,1024]{1,0:T(8,128)S(1)}, u32[]{:S(2)}, u32[]{:S(2)}) collective-permute-start(f32[128,1024]{1,0:T(8,128)} %get-tuple-element.832), channel_id=1, source_target_pairs={{0,1},{1,2},{2,3},{3,4},{4,5},{5,6},{6,7},{7,8},{8,9},{9,10},{10,1... | collective-permute-start | bytes 1572872 | tf_op jit(solution)/shard_map/while/body/eval_jaxpr/ppermute | solution.py:11
  747.5 24.7 %collective-permute-start.3 = (f32[128]{0:T(128)S(1)}, f32[128]{0:T(128)S(1)}, u32[]{:S(2)}, u32[]{:S(2)}) collective-permute-start(f32[128]{0:T(128)S(1)} %get-tuple-element.833), channel_id=1, source_target_pairs={{0,1},{1,2},{2,3},{3,4},{4,5},{5,6},{6,7},{7,8},{8,9},{9,10},{10,1... | collective-permute-start | bytes 1544 | tf_op jit(solution)/shard_map/while/body/eval_jaxpr/ppermute | solution.py:11
  773.3 23.8 %collective-permute-start.2 = (f32[128,1024]{1,0:T(8,128)}, f32[128,1024]{1,0:T(8,128)S(1)}, u32[]{:S(2)}, u32[]{:S(2)}) collective-permute-start(f32[128,1024]{1,0:T(8,128)} %get-tuple-element.832), channel_id=1, source_target_pairs={{0,1},{1,2},{2,3},{3,4},{4,5},{5,6},{6,7},{7,8},{8,9},{9,10},{10,1... | collective-permute-start | bytes 1572872 | tf_op jit(solution)/shard_map/while/body/eval_jaxpr/ppermute | solution.py:11
  773.3 23.8 %collective-permute-start.3 = (f32[128]{0:T(128)S(1)}, f32[128]{0:T(128)S(1)}, u32[]{:S(2)}, u32[]{:S(2)}) collective-permute-start(f32[128]{0:T(128)S(1)} %get-tuple-element.833), channel_id=1, source_target_pairs={{0,1},{1,2},{2,3},{3,4},{4,5},{5,6},{6,7},{7,8},{8,9},{9,10},{10,1... | collective-permute-start | bytes 1544 | tf_op jit(solution)/shard_map/while/body/eval_jaxpr/ppermute | solution.py:11
  798.2 22.9 %collective-permute-start.2 = (f32[128,1024]{1,0:T(8,128)}, f32[128,1024]{1,0:T(8,128)S(1)}, u32[]{:S(2)}, u32[]{:S(2)}) collective-permute-start(f32[128,1024]{1,0:T(8,128)} %get-tuple-element.832), channel_id=1, source_target_pairs={{0,1},{1,2},{2,3},{3,4},{4,5},{5,6},{6,7},{7,8},{8,9},{9,10},{10,1... | collective-permute-start | bytes 1572872 | tf_op jit(solution)/shard_map/while/body/eval_jaxpr/ppermute | solution.py:11
  798.2 22.9 %collective-permute-start.3 = (f32[128]{0:T(128)S(1)}, f32[128]{0:T(128)S(1)}, u32[]{:S(2)}, u32[]{:S(2)}) collective-permute-start(f32[128]{0:T(128)S(1)} %get-tuple-element.833), channel_id=1, source_target_pairs={{0,1},{1,2},{2,3},{3,4},{4,5},{5,6},{6,7},{7,8},{8,9},{9,10},{10,1... | collective-permute-start | bytes 1544 | tf_op jit(solution)/shard_map/while/body/eval_jaxpr/ppermute | solution.py:11
  822.3 21.9 %collective-permute-start.2 = (f32[128,1024]{1,0:T(8,128)}, f32[128,1024]{1,0:T(8,128)S(1)}, u32[]{:S(2)}, u32[]{:S(2)}) collective-permute-start(f32[128,1024]{1,0:T(8,128)} %get-tuple-element.832), channel_id=1, source_target_pairs={{0,1},{1,2},{2,3},{3,4},{4,5},{5,6},{6,7},{7,8},{8,9},{9,10},{10,1... | collective-permute-start | bytes 1572872 | tf_op jit(solution)/shard_map/while/body/eval_jaxpr/ppermute | solution.py:11
  822.3 21.9 %collective-permute-start.3 = (f32[128]{0:T(128)S(1)}, f32[128]{0:T(128)S(1)}, u32[]{:S(2)}, u32[]{:S(2)}) collective-permute-start(f32[128]{0:T(128)S(1)} %get-tuple-element.833), channel_id=1, source_target_pairs={{0,1},{1,2},{2,3},{3,4},{4,5},{5,6},{6,7},{7,8},{8,9},{9,10},{10,1... | collective-permute-start | bytes 1544 | tf_op jit(solution)/shard_map/while/body/eval_jaxpr/ppermute | solution.py:11
  845.3 20.9 %collective-permute-start.2 = (f32[128,1024]{1,0:T(8,128)}, f32[128,1024]{1,0:T(8,128)S(1)}, u32[]{:S(2)}, u32[]{:S(2)}) collective-permute-start(f32[128,1024]{1,0:T(8,128)} %get-tuple-element.832), channel_id=1, source_target_pairs={{0,1},{1,2},{2,3},{3,4},{4,5},{5,6},{6,7},{7,8},{8,9},{9,10},{10,1... | collective-permute-start | bytes 1572872 | tf_op jit(solution)/shard_map/while/body/eval_jaxpr/ppermute | solution.py:11
  845.3 20.9 %collective-permute-start.3 = (f32[128]{0:T(128)S(1)}, f32[128]{0:T(128)S(1)}, u32[]{:S(2)}, u32[]{:S(2)}) collective-permute-start(f32[128]{0:T(128)S(1)} %get-tuple-element.833), channel_id=1, source_target_pairs={{0,1},{1,2},{2,3},{3,4},{4,5},{5,6},{6,7},{7,8},{8,9},{9,10},{10,1... | collective-permute-start | bytes 1544 | tf_op jit(solution)/shard_map/while/body/eval_jaxpr/ppermute | solution.py:11
  867.3 19.9 %collective-permute-start.2 = (f32[128,1024]{1,0:T(8,128)}, f32[128,1024]{1,0:T(8,128)S(1)}, u32[]{:S(2)}, u32[]{:S(2)}) collective-permute-start(f32[128,1024]{1,0:T(8,128)} %get-tuple-element.832), channel_id=1, source_target_pairs={{0,1},{1,2},{2,3},{3,4},{4,5},{5,6},{6,7},{7,8},{8,9},{9,10},{10,1... | collective-permute-start | bytes 1572872 | tf_op jit(solution)/shard_map/while/body/eval_jaxpr/ppermute | solution.py:11
  867.3 19.9 %collective-permute-start.3 = (f32[128]{0:T(128)S(1)}, f32[128]{0:T(128)S(1)}, u32[]{:S(2)}, u32[]{:S(2)}) collective-permute-start(f32[128]{0:T(128)S(1)} %get-tuple-element.833), channel_id=1, source_target_pairs={{0,1},{1,2},{2,3},{3,4},{4,5},{5,6},{6,7},{7,8},{8,9},{9,10},{10,1... | collective-permute-start | bytes 1544 | tf_op jit(solution)/shard_map/while/body/eval_jaxpr/ppermute | solution.py:11
  888.4 18.9 %collective-permute-start.2 = (f32[128,1024]{1,0:T(8,128)}, f32[128,1024]{1,0:T(8,128)S(1)}, u32[]{:S(2)}, u32[]{:S(2)}) collective-permute-start(f32[128,1024]{1,0:T(8,128)} %get-tuple-element.832), channel_id=1, source_target_pairs={{0,1},{1,2},{2,3},{3,4},{4,5},{5,6},{6,7},{7,8},{8,9},{9,10},{10,1... | collective-permute-start | bytes 1572872 | tf_op jit(solution)/shard_map/while/body/eval_jaxpr/ppermute | solution.py:11
  888.4 18.9 %collective-permute-start.3 = (f32[128]{0:T(128)S(1)}, f32[128]{0:T(128)S(1)}, u32[]{:S(2)}, u32[]{:S(2)}) collective-permute-start(f32[128]{0:T(128)S(1)} %get-tuple-element.833), channel_id=1, source_target_pairs={{0,1},{1,2},{2,3},{3,4},{4,5},{5,6},{6,7},{7,8},{8,9},{9,10},{10,1... | collective-permute-start | bytes 1544 | tf_op jit(solution)/shard_map/while/body/eval_jaxpr/ppermute | solution.py:11
  908.5 17.9 %collective-permute-start.2 = (f32[128,1024]{1,0:T(8,128)}, f32[128,1024]{1,0:T(8,128)S(1)}, u32[]{:S(2)}, u32[]{:S(2)}) collective-permute-start(f32[128,1024]{1,0:T(8,128)} %get-tuple-element.832), channel_id=1, source_target_pairs={{0,1},{1,2},{2,3},{3,4},{4,5},{5,6},{6,7},{7,8},{8,9},{9,10},{10,1... | collective-permute-start | bytes 1572872 | tf_op jit(solution)/shard_map/while/body/eval_jaxpr/ppermute | solution.py:11
  908.5 17.9 %collective-permute-start.3 = (f32[128]{0:T(128)S(1)}, f32[128]{0:T(128)S(1)}, u32[]{:S(2)}, u32[]{:S(2)}) collective-permute-start(f32[128]{0:T(128)S(1)} %get-tuple-element.833), channel_id=1, source_target_pairs={{0,1},{1,2},{2,3},{3,4},{4,5},{5,6},{6,7},{7,8},{8,9},{9,10},{10,1... | collective-permute-start | bytes 1544 | tf_op jit(solution)/shard_map/while/body/eval_jaxpr/ppermute | solution.py:11
  927.5 16.9 %collective-permute-start.2 = (f32[128,1024]{1,0:T(8,128)}, f32[128,1024]{1,0:T(8,128)S(1)}, u32[]{:S(2)}, u32[]{:S(2)}) collective-permute-start(f32[128,1024]{1,0:T(8,128)} %get-tuple-element.832), channel_id=1, source_target_pairs={{0,1},{1,2},{2,3},{3,4},{4,5},{5,6},{6,7},{7,8},{8,9},{9,10},{10,1... | collective-permute-start | bytes 1572872 | tf_op jit(solution)/shard_map/while/body/eval_jaxpr/ppermute | solution.py:11
  927.6 16.9 %collective-permute-start.3 = (f32[128]{0:T(128)S(1)}, f32[128]{0:T(128)S(1)}, u32[]{:S(2)}, u32[]{:S(2)}) collective-permute-start(f32[128]{0:T(128)S(1)} %get-tuple-element.833), channel_id=1, source_target_pairs={{0,1},{1,2},{2,3},{3,4},{4,5},{5,6},{6,7},{7,8},{8,9},{9,10},{10,1... | collective-permute-start | bytes 1544 | tf_op jit(solution)/shard_map/while/body/eval_jaxpr/ppermute | solution.py:11
  945.6 17.1 %collective-permute-start.2 = (f32[128,1024]{1,0:T(8,128)}, f32[128,1024]{1,0:T(8,128)S(1)}, u32[]{:S(2)}, u32[]{:S(2)}) collective-permute-start(f32[128,1024]{1,0:T(8,128)} %get-tuple-element.832), channel_id=1, source_target_pairs={{0,1},{1,2},{2,3},{3,4},{4,5},{5,6},{6,7},{7,8},{8,9},{9,10},{10,1... | collective-permute-start | bytes 1572872 | tf_op jit(solution)/shard_map/while/body/eval_jaxpr/ppermute | solution.py:11
  945.6 17.1 %collective-permute-start.3 = (f32[128]{0:T(128)S(1)}, f32[128]{0:T(128)S(1)}, u32[]{:S(2)}, u32[]{:S(2)}) collective-permute-start(f32[128]{0:T(128)S(1)} %get-tuple-element.833), channel_id=1, source_target_pairs={{0,1},{1,2},{2,3},{3,4},{4,5},{5,6},{6,7},{7,8},{8,9},{9,10},{10,1... | collective-permute-start | bytes 1544 | tf_op jit(solution)/shard_map/while/body/eval_jaxpr/ppermute | solution.py:11
  963.9 18.2 %collective-permute-start.2 = (f32[128,1024]{1,0:T(8,128)}, f32[128,1024]{1,0:T(8,128)S(1)}, u32[]{:S(2)}, u32[]{:S(2)}) collective-permute-start(f32[128,1024]{1,0:T(8,128)} %get-tuple-element.832), channel_id=1, source_target_pairs={{0,1},{1,2},{2,3},{3,4},{4,5},{5,6},{6,7},{7,8},{8,9},{9,10},{10,1... | collective-permute-start | bytes 1572872 | tf_op jit(solution)/shard_map/while/body/eval_jaxpr/ppermute | solution.py:11
  963.9 18.2 %collective-permute-start.3 = (f32[128]{0:T(128)S(1)}, f32[128]{0:T(128)S(1)}, u32[]{:S(2)}, u32[]{:S(2)}) collective-permute-start(f32[128]{0:T(128)S(1)} %get-tuple-element.833), channel_id=1, source_target_pairs={{0,1},{1,2},{2,3},{3,4},{4,5},{5,6},{6,7},{7,8},{8,9},{9,10},{10,1... | collective-permute-start | bytes 1544 | tf_op jit(solution)/shard_map/while/body/eval_jaxpr/ppermute | solution.py:11
  983.3 19.3 %collective-permute-start.2 = (f32[128,1024]{1,0:T(8,128)}, f32[128,1024]{1,0:T(8,128)S(1)}, u32[]{:S(2)}, u32[]{:S(2)}) collective-permute-start(f32[128,1024]{1,0:T(8,128)} %get-tuple-element.832), channel_id=1, source_target_pairs={{0,1},{1,2},{2,3},{3,4},{4,5},{5,6},{6,7},{7,8},{8,9},{9,10},{10,1... | collective-permute-start | bytes 1572872 | tf_op jit(solution)/shard_map/while/body/eval_jaxpr/ppermute | solution.py:11
  983.3 19.3 %collective-permute-start.3 = (f32[128]{0:T(128)S(1)}, f32[128]{0:T(128)S(1)}, u32[]{:S(2)}, u32[]{:S(2)}) collective-permute-start(f32[128]{0:T(128)S(1)} %get-tuple-element.833), channel_id=1, source_target_pairs={{0,1},{1,2},{2,3},{3,4},{4,5},{5,6},{6,7},{7,8},{8,9},{9,10},{10,1... | collective-permute-start | bytes 1544 | tf_op jit(solution)/shard_map/while/body/eval_jaxpr/ppermute | solution.py:11
  1003.7 20.2 %collective-permute-start.2 = (f32[128,1024]{1,0:T(8,128)}, f32[128,1024]{1,0:T(8,128)S(1)}, u32[]{:S(2)}, u32[]{:S(2)}) collective-permute-start(f32[128,1024]{1,0:T(8,128)} %get-tuple-element.832), channel_id=1, source_target_pairs={{0,1},{1,2},{2,3},{3,4},{4,5},{5,6},{6,7},{7,8},{8,9},{9,10},{10,1... | collective-permute-start | bytes 1572872 | tf_op jit(solution)/shard_map/while/body/eval_jaxpr/ppermute | solution.py:11
  1003.7 20.1 %collective-permute-start.3 = (f32[128]{0:T(128)S(1)}, f32[128]{0:T(128)S(1)}, u32[]{:S(2)}, u32[]{:S(2)}) collective-permute-start(f32[128]{0:T(128)S(1)} %get-tuple-element.833), channel_id=1, source_target_pairs={{0,1},{1,2},{2,3},{3,4},{4,5},{5,6},{6,7},{7,8},{8,9},{9,10},{10,1... | collective-permute-start | bytes 1544 | tf_op jit(solution)/shard_map/while/body/eval_jaxpr/ppermute | solution.py:11
  1025.0 16.3 %collective-permute-start.2 = (f32[128,1024]{1,0:T(8,128)}, f32[128,1024]{1,0:T(8,128)S(1)}, u32[]{:S(2)}, u32[]{:S(2)}) collective-permute-start(f32[128,1024]{1,0:T(8,128)} %get-tuple-element.832), channel_id=1, source_target_pairs={{0,1},{1,2},{2,3},{3,4},{4,5},{5,6},{6,7},{7,8},{8,9},{9,10},{10,1... | collective-permute-start | bytes 1572872 | tf_op jit(solution)/shard_map/while/body/eval_jaxpr/ppermute | solution.py:11
  1025.0 16.3 %collective-permute-start.3 = (f32[128]{0:T(128)S(1)}, f32[128]{0:T(128)S(1)}, u32[]{:S(2)}, u32[]{:S(2)}) collective-permute-start(f32[128]{0:T(128)S(1)} %get-tuple-element.833), channel_id=1, source_target_pairs={{0,1},{1,2},{2,3},{3,4},{4,5},{5,6},{6,7},{7,8},{8,9},{9,10},{10,1... | collective-permute-start | bytes 1544 | tf_op jit(solution)/shard_map/while/body/eval_jaxpr/ppermute | solution.py:11
  1042.5 16.3 %collective-permute-start.2 = (f32[128,1024]{1,0:T(8,128)}, f32[128,1024]{1,0:T(8,128)S(1)}, u32[]{:S(2)}, u32[]{:S(2)}) collective-permute-start(f32[128,1024]{1,0:T(8,128)} %get-tuple-element.832), channel_id=1, source_target_pairs={{0,1},{1,2},{2,3},{3,4},{4,5},{5,6},{6,7},{7,8},{8,9},{9,10},{10,1... | collective-permute-start | bytes 1572872 | tf_op jit(solution)/shard_map/while/body/eval_jaxpr/ppermute | solution.py:11
  1042.5 16.3 %collective-permute-start.3 = (f32[128]{0:T(128)S(1)}, f32[128]{0:T(128)S(1)}, u32[]{:S(2)}, u32[]{:S(2)}) collective-permute-start(f32[128]{0:T(128)S(1)} %get-tuple-element.833), channel_id=1, source_target_pairs={{0,1},{1,2},{2,3},{3,4},{4,5},{5,6},{6,7},{7,8},{8,9},{9,10},{10,1... | collective-permute-start | bytes 1544 | tf_op jit(solution)/shard_map/while/body/eval_jaxpr/ppermute | solution.py:11
  1059.9 16.3 %collective-permute-start.2 = (f32[128,1024]{1,0:T(8,128)}, f32[128,1024]{1,0:T(8,128)S(1)}, u32[]{:S(2)}, u32[]{:S(2)}) collective-permute-start(f32[128,1024]{1,0:T(8,128)} %get-tuple-element.832), channel_id=1, source_target_pairs={{0,1},{1,2},{2,3},{3,4},{4,5},{5,6},{6,7},{7,8},{8,9},{9,10},{10,1... | collective-permute-start | bytes 1572872 | tf_op jit(solution)/shard_map/while/body/eval_jaxpr/ppermute | solution.py:11
  1059.9 16.3 %collective-permute-start.3 = (f32[128]{0:T(128)S(1)}, f32[128]{0:T(128)S(1)}, u32[]{:S(2)}, u32[]{:S(2)}) collective-permute-start(f32[128]{0:T(128)S(1)} %get-tuple-element.833), channel_id=1, source_target_pairs={{0,1},{1,2},{2,3},{3,4},{4,5},{5,6},{6,7},{7,8},{8,9},{9,10},{10,1... | collective-permute-start | bytes 1544 | tf_op jit(solution)/shard_map/while/body/eval_jaxpr/ppermute | solution.py:11
  1077.3 13.7 %collective-permute-start.4 = (f32[128,1024]{1,0:T(8,128)}, f32[128,1024]{1,0:T(8,128)S(1)}, u32[]{:S(2)}, u32[]{:S(2)}) collective-permute-start(f32[128,1024]{1,0:T(8,128)} %get-tuple-element.518), channel_id=1, source_target_pairs={{0,1},{1,2},{2,3},{3,4},{4,5},{5,6},{6,7},{7,8},{8,9},{9,10},{10,1... | collective-permute-start | bytes 1572872 | tf_op jit(solution)/shard_map/ppermute | solution.py:11
  (68 other events, 769.8 us)
where the time goes:
time: 1100 us; the launch traced here: 1090 us
  waiting for transfers between devices  773 us (70%)
  local copies, waits for them, and re-layouts  172 us (16%)
  matrix products  67.4 us (6%)
  other arithmetic  65.1 us (6%)
    ppermute x126, waiting for transfers between devices, passed_along(): lax.ppermute(shard, axis, [(i, (i + by) % peers) for i in range(peers)])  750 us
    gather x63, local copies, waits for them, and re-layouts, pick(): jnp.take(blocks, index, axis=0)  139 us
    dot_general x32, matrix products, weighted(): lax.dot_general(flat, chosen, (((0,), (0,)), ((), ())), preferred_element...  36.9 us
    dot_general x63, matrix products, scores(): jnp.einsum('rd,pd->rp', chosen, panel, preferred_element_type=jnp.float32)  30.5 us
    all_to_all x1, waiting for transfers between devices, shards(): lax.all_to_all(coarse_cluster_means, 'row', split_axis=0, concat_axis=1,...  22.5 us
  transfers between devices with their start and end apart: 127, of which 95 were waited for; matrix products, arithmetic and copies ran while one was open for 21% of the time, Pallas kernels for 0%

commit v1 on v0

v1 whole, which is shorter than its diff:
```python
import math

import jax
import jax.numpy as jnp
from jax import lax
from jax.experimental import pallas as pl
from jax.experimental.pallas import tpu as pltpu
from jax.sharding import Mesh, PartitionSpec as P

PANEL = 128
BLOCK = 128
DIM = 1024
HALF = PANEL // 2
SLICE = 256
BLOCKS = 16
SLOTS = 8
LOW = -1e30
PACK = 4 * HALF + 16
CHUNK = HALF + 16


def moved(value, axis, by):
    size = lax.axis_size(axis)
    return lax.ppermute(value, axis, [(i, (i - by) % size) for i in range(size)])


def swapped(value):
    return lax.ppermute(value, ("c", "yl"), [(0, 0), (1, 2), (2, 1), (3, 3)])


def nt_dot(a, b):
    return lax.dot_general(a, b, (((1,), (1,)), ((), ())), preferred_element_type=jnp.float32)


def point_copies(here_ref, own, oth, x_ref, sem):
    y, c = here_ref[0], here_ref[1]
    copies = []
    for d in range(4):
        src = lax.rem(y + d, 4)
        yh, yl = src // 2, lax.rem(src, 2)
        for i, (refs, core) in enumerate(((own, c), (oth, 1 - c))):
            copies.append(
                pltpu.make_async_copy(
                    refs[d], x_ref.at[2 * yh + core, pl.ds(yl * 8, 8)], sem.at[2 * d + i]
                )
            )
    return copies


def score_kernel(
    here_ref, count_ref, list_ref, scale_ref, *refs
):
    own, oth, a_in, b_in = refs[0:4], refs[4:8], refs[8:12], refs[12:16]
    logit_ref, stat_ref = refs[16:18]
    x_ref, p_ref, l_ref, xsem, psem, lsem = refs[18:]
    xcopies = point_copies(here_ref, own, oth, x_ref, xsem)
    pcopies = []
    for dz in range(4):
        for dx in range(4):
            r = dz * 4 + dx
            pcopies.append(
                pltpu.make_async_copy(a_in[dx].at[dz], p_ref.at[r, pl.ds(0, HALF)], psem.at[2 * r])
            )
            pcopies.append(
                pltpu.make_async_copy(
                    b_in[dz].at[dx], p_ref.at[r, pl.ds(HALF, HALF)], psem.at[2 * r + 1]
                )
            )
    for copy in xcopies + pcopies:
        copy.start()
    scale = scale_ref[0]
    stat_ref[0:BLOCKS, :] = jnp.full((BLOCKS, BLOCK), LOW, jnp.float32)
    stat_ref[BLOCKS : 2 * BLOCKS, :] = jnp.zeros((BLOCKS, BLOCK), jnp.float32)
    for copy in xcopies:
        copy.wait()
    for copy in pcopies:
        copy.wait()

    def out_copy(r, t):
        return pltpu.make_async_copy(l_ref.at[r, t], logit_ref.at[r, t], lsem)

    def panel_step(r, _):
        count = count_ref[r]
        panel32 = p_ref[r].astype(jnp.float32)
        sqnorm = jnp.sum(panel32 * panel32, axis=1, keepdims=True)

        def turn(t, _):
            first, second = list_ref[r, 2 * t], list_ref[r, 2 * t + 1]
            acc = jnp.zeros((PANEL, 2 * BLOCK), jnp.float32)
            for f in range(4):
                rhs = jnp.concatenate([x_ref[f, first], x_ref[f, second]], axis=0)
                acc += nt_dot(p_ref[r, :, f * SLICE : (f + 1) * SLICE], rhs)
            logit = (2.0 * acc - sqnorm) * scale
            both = 2 * t + 1 < count
            lane = lax.broadcasted_iota(jnp.int32, (PANEL, 2 * BLOCK), 1)
            logit = jnp.where((lane < BLOCK) | both, logit, LOW)
            l_ref[r, t] = logit
            out_copy(r, t).start()

            def merge(block, part):
                old = stat_ref[pl.ds(block, 1), :]
                new = jnp.maximum(old, jnp.max(part, axis=0, keepdims=True))
                total = stat_ref[pl.ds(BLOCKS + block, 1), :] * jnp.exp(old - new)
                total += jnp.sum(jnp.exp(part - new), axis=0, keepdims=True)
                stat_ref[pl.ds(block, 1), :] = new
                stat_ref[pl.ds(BLOCKS + block, 1), :] = total

            merge(first, logit[:, :BLOCK])

            @pl.when(both)
            def _():
                merge(second, logit[:, BLOCK:])

            return 0

        return lax.fori_loop(0, (count + 1) // 2, turn, 0)

    lax.fori_loop(0, 16, panel_step, 0)

    def drain(r, _):
        def one(t, _):
            out_copy(r, t).wait()
            return 0

        return lax.fori_loop(0, (count_ref[r] + 1) // 2, one, 0)

    lax.fori_loop(0, 16, drain, 0)


def sum_kernel(here_ref, count_ref, list_ref, logit_ref, mine_ref, other_ref, *refs):
    own, oth = refs[0:4], refs[4:8]
    a_out, b_out = refs[8:12], refs[12:16]
    norm_ref = refs[16]
    x_ref, l_ref, acc_ref, mass_ref, xsem, lsem = refs[17:]
    xcopies = point_copies(here_ref, own, oth, x_ref, xsem)

    def in_copy(r, t):
        return pltpu.make_async_copy(logit_ref.at[r, t], l_ref.at[r, t], lsem.at[r])

    for copy in xcopies:
        copy.start()

    def fetch(r, _):
        def one(t, _):
            in_copy(r, t).start()
            return 0

        return lax.fori_loop(0, (count_ref[r] + 1) // 2, one, 0)

    lax.fori_loop(0, 16, fetch, 0)
    m0, s0 = mine_ref[0:BLOCKS, :], mine_ref[BLOCKS : 2 * BLOCKS, :]
    m1, s1 = other_ref[0:BLOCKS, :], other_ref[BLOCKS : 2 * BLOCKS, :]
    top = jnp.maximum(m0, m1)
    norm_ref[...] = top + jnp.log(s0 * jnp.exp(m0 - top) + s1 * jnp.exp(m1 - top))
    mass_ref[...] = jnp.zeros_like(mass_ref)
    for copy in xcopies:
        copy.wait()
    ones = jnp.ones((8, 2 * BLOCK), jnp.bfloat16)

    for dz in range(4):
        for dx in range(4):
            r = dz * 4 + dx
            turns = (count_ref[r] + 1) // 2

            def landed(t, _, r=r):
                in_copy(r, t).wait()
                return 0

            lax.fori_loop(0, turns, landed, 0)
            acc_ref[...] = jnp.zeros_like(acc_ref)

            def turn(t, mass, r=r):
                first, second = list_ref[r, 2 * t], list_ref[r, 2 * t + 1]
                norm = jnp.concatenate(
                    [norm_ref[pl.ds(first, 1), :], norm_ref[pl.ds(second, 1), :]], axis=1
                )
                weight = jnp.exp(l_ref[r, t] - norm).astype(jnp.bfloat16)
                for f in range(4):
                    rhs = jnp.concatenate([x_ref[f, first], x_ref[f, second]], axis=0)
                    acc_ref[:, f * SLICE : (f + 1) * SLICE] += jnp.dot(
                        weight, rhs, preferred_element_type=jnp.float32
                    )
                return mass + nt_dot(ones, weight)

            mass = lax.fori_loop(0, turns, turn, jnp.zeros((8, PANEL), jnp.float32))[0:1, :]
            a_out[dz][dx * HALF : (dx + 1) * HALF, :] = acc_ref[0:HALF, :].astype(jnp.bfloat16)
            b_out[dx][dz * HALF : (dz + 1) * HALF, :] = acc_ref[HALF:, :].astype(jnp.bfloat16)
            high = mass.astype(jnp.bfloat16).astype(jnp.float32)
            mass_ref[dz, dx : dx + 1, 0:PANEL] = high
            mass_ref[dz, 4 + dx : 5 + dx, 0:PANEL] = mass - high
            mass_ref[4 + dx, dz : dz + 1, 0:PANEL] = high
            mass_ref[4 + dx, 4 + dz : 5 + dz, 0:PANEL] = mass - high
    for i in range(4):
        a_out[i][4 * HALF :, :] = mass_ref[i].astype(jnp.bfloat16)
        b_out[i][4 * HALF :, :] = mass_ref[4 + i].astype(jnp.bfloat16)


def fold_kernel(*refs):
    a_in, b_in = refs[0:4], refs[4:8]
    a_out, b_out = refs[8:12], refs[12:16]
    for ins, outs in ((a_in, a_out), (b_in, b_out)):
        total = sum(ref[4 * HALF :, :].astype(jnp.float32) for ref in ins)
        mass = total[0:4, :] + total[4:8, :]
        high = mass.astype(jnp.bfloat16).astype(jnp.float32)
        for i in range(4):
            rows = slice(i * HALF, (i + 1) * HALF)
            outs[i][0:HALF, :] = sum(ref[rows, :].astype(jnp.float32) for ref in ins).astype(
                jnp.bfloat16
            )
            tail = jnp.concatenate(
                [high[i : i + 1], mass[i : i + 1] - high[i : i + 1], jnp.zeros((14, DIM), jnp.float32)],
                axis=0,
            )
            outs[i][HALF:, :] = tail.astype(jnp.bfloat16)


def finish_kernel(panel_ref, *refs):
    a_in, b_in, out_ref = refs[0:4], refs[4:8], refs[8]
    eye = lax.broadcasted_iota(jnp.int32, (HALF, PANEL), 0)
    lane = lax.broadcasted_iota(jnp.int32, (HALF, PANEL), 1)
    for h, ins in enumerate((a_in, b_in)):
        rows = slice(h * HALF, (h + 1) * HALF)
        sums = sum(ref[0:HALF, :].astype(jnp.float32) for ref in ins)
        tail = sum(ref[HALF:, 0:PANEL].astype(jnp.float32) for ref in ins)
        mass = tail[0:1, :] + tail[1:2, :]
        column = jnp.sum(jnp.where(eye + h * HALF == lane, mass, 0.0), axis=1, keepdims=True)
        panel = panel_ref[rows, :].astype(jnp.float32)
        out_ref[rows, :] = ((sums + panel) / (column + 1.0)).astype(jnp.bfloat16)


def shards(coarse_cluster_means, fine_cluster_means, block_panel_candidates, softmax_heat):
    y = 2 * lax.axis_index("yh") + lax.axis_index("yl")
    c = lax.axis_index("c")
    z, x = lax.axis_index("z"), lax.axis_index("x")
    here = jnp.stack([y, c]).astype(jnp.int32)
    scale = 1.0 / (softmax_heat * math.sqrt(DIM))

    panel = swapped(fine_cluster_means)
    half_a, half_b = panel[:HALF], panel[HALF:]
    stack_a = jnp.stack([half_a] + [moved(half_a, "z", d) for d in (1, 2, 3)])
    stack_b = jnp.stack([half_b] + [moved(half_b, "x", d) for d in (1, 2, 3)])
    all_a = [stack_a] + [moved(stack_a, "x", d) for d in (1, 2, 3)]
    all_b = [stack_b] + [moved(stack_b, "z", d) for d in (1, 2, 3)]

    groups = coarse_cluster_means.reshape(4, 8, BLOCK, SLICE)
    own = []
    for d in range(4):
        part = lax.dynamic_index_in_dim(groups, (y - d) % 4, 0, keepdims=False)
        own.append(part if d == 0 else moved(part, ("yh", "yl"), d))
    oth = [moved(part, "c", 1) for part in own]

    mine = swapped(block_panel_candidates)
    other = moved(mine, "c", 1)
    cands = jnp.where(c == 0, jnp.stack([mine, other]), jnp.stack([other, mine])).reshape(BLOCKS, 8)
    spot = ((cands // 4 % 4 - z) % 4) * 4 + (cands % 4 - x) % 4
    spot = jnp.where(cands // 16 == c, spot, -1)
    hits = jnp.any(spot[None] == jnp.arange(16, dtype=jnp.int32)[:, None, None], axis=2)
    order = jnp.cumsum(hits.astype(jnp.int32), axis=1) - 1
    count = jnp.sum(hits.astype(jnp.int32), axis=1)
    chosen = (order[:, None, :] == jnp.arange(SLOTS, dtype=jnp.int32)[None, :, None]) & hits[:, None, :]
    table = jnp.sum(jnp.where(chosen, jnp.arange(BLOCKS, dtype=jnp.int32)[None, None, :], 0), axis=2)

    smem = pl.BlockSpec(memory_space=pltpu.SMEM)
    vmem = pl.BlockSpec(memory_space=pltpu.VMEM)
    hbm = pl.BlockSpec(memory_space=pl.ANY)
    points_scratch = pltpu.VMEM((4, BLOCKS, BLOCK, SLICE), jnp.bfloat16)
    logit_scratch = pltpu.VMEM((16, SLOTS // 2, PANEL, 2 * BLOCK), jnp.float32)
    logit, stat = pl.pallas_call(
        score_kernel,
        in_specs=[smem] * 4 + [hbm] * 16,
        out_specs=[hbm, vmem],
        out_shape=[
            jax.ShapeDtypeStruct((16, SLOTS // 2, PANEL, 2 * BLOCK), jnp.float32),
            jax.ShapeDtypeStruct((2 * BLOCKS, BLOCK), jnp.float32),
        ],
        scratch_shapes=[
            points_scratch,
            pltpu.VMEM((16, PANEL, DIM), jnp.bfloat16),
            logit_scratch,
            pltpu.SemaphoreType.DMA((8,)),
            pltpu.SemaphoreType.DMA((32,)),
            pltpu.SemaphoreType.DMA,
        ],
        compiler_params=pltpu.CompilerParams(vmem_limit_bytes=40 << 20),
        name="scores",
    )(here, count, table, scale, *own, *oth, *all_a, *all_b)
    stat_other = moved(stat, "c", 1)

    packs = pl.pallas_call(
        sum_kernel,
        in_specs=[smem] * 3 + [hbm, vmem, vmem] + [hbm] * 8,
        out_specs=[vmem] * 9,
        out_shape=[jax.ShapeDtypeStruct((PACK, DIM), jnp.bfloat16)] * 8
        + [jax.ShapeDtypeStruct((BLOCKS, BLOCK), jnp.float32)],
        scratch_shapes=[
            points_scratch,
            logit_scratch,
            pltpu.VMEM((PANEL, DIM), jnp.float32),
            pltpu.VMEM((8, 16, DIM), jnp.float32),
            pltpu.SemaphoreType.DMA((8,)),
            pltpu.SemaphoreType.DMA((16,)),
        ],
        compiler_params=pltpu.CompilerParams(vmem_limit_bytes=48 << 20),
        name="sums",
    )(here, count, table, logit, stat, stat_other, *own, *oth)
    pack_a, pack_b, norm = packs[0:4], packs[4:8], packs[8]

    part_norm = lax.dynamic_slice_in_dim(norm, c * 8, 8, axis=0)
    log_norm = swapped(part_norm).reshape(8 * BLOCK)

    got_a = [pack_a[0]] + [moved(pack_a[d], "z", -d) for d in (1, 2, 3)]
    got_b = [pack_b[0]] + [moved(pack_b[d], "x", -d) for d in (1, 2, 3)]
    folded = pl.pallas_call(
        fold_kernel,
        in_specs=[vmem] * 8,
        out_specs=[vmem] * 8,
        out_shape=[jax.ShapeDtypeStruct((CHUNK, DIM), jnp.bfloat16)] * 8,
        compiler_params=pltpu.CompilerParams(vmem_limit_bytes=32 << 20),
        name="fold",
    )(*got_a, *got_b)
    part_a, part_b = folded[0:4], folded[4:8]
    last_a = [part_a[0]] + [moved(part_a[d], "x", -d) for d in (1, 2, 3)]
    last_b = [part_b[0]] + [moved(part_b[d], "z", -d) for d in (1, 2, 3)]
    revised = pl.pallas_call(
        finish_kernel,
        in_specs=[vmem] * 9,
        out_specs=vmem,
        out_shape=jax.ShapeDtypeStruct((PANEL, DIM), jnp.bfloat16),
        name="finish",
    )(panel, *last_a, *last_b)
    return (swapped(revised), log_norm)


def solution(mesh):
    split = Mesh(mesh.devices.reshape(2, 2, 2, 4, 4), ("yh", "c", "yl", "z", "x"))
    blk, row = ("yl", "z", "x"), ("yh", "c")
    return jax.shard_map(
        shards,
        mesh=split,
        in_specs=(P(blk, row), P(blk + row, None), P(blk + row, None), P()),
        out_specs=(P(blk + row, None), P(blk + row)),
        check_vma=False,
    )
```

time: 1100 us -> 179 us (0.16)
  the two profiles are of different devices: /device:TPU:16 before, /device:TPU:1 now
where the time goes in v1:
time: 179 us
  starting transfers between devices  78.5 us (44%)
  waiting for transfers between devices  55.8 us (31%)
  Pallas kernels  32.8 us (18%)
  local copies, waits for them, and re-layouts  8.04 us (4%)
  other arithmetic  2.51 us (1%)
    ppermute x33, waiting for transfers between devices, moved(): lax.ppermute(value, axis, [(i, (i - by) % size) for i in range(size)])  52.8 us
    ppermute x33, starting transfers between devices, moved(): lax.ppermute(value, axis, [(i, (i - by) % size) for i in range(size)])  52.6 us
    ppermute x4, starting transfers between devices, swapped(): return lax.ppermute(value, ('c', 'yl'), [(0, 0), (1, 2), (2, 1), (3, 3)])  25.8 us
    pallas_call x1, Pallas kernels, shards(): pl.pallas_call(score_kernel, in_specs=[smem] * 4 + [hbm] * 16, out_specs=...  17.5 us
    pallas_call x1, Pallas kernels, shards(): pl.pallas_call(sum_kernel, in_specs=[smem] * 3 + [hbm, vmem, vmem] + [hbm...  12.3 us
    unnamed x26, local copies, waits for them, and re-layouts  6.24 us
  transfers between devices with their start and end apart: 37, of which 16 were waited for; matrix products, arithmetic and copies ran while one was open for 2% of the time, Pallas kernels for 0%

profile of v1, /device:TPU:1, one launch (start us, length us, event | category | flops | bytes accessed | tf_op | source)
XLA Modules:
  0.0 179.2 jit_solution(6289936462398537257)
XLA Ops:
  0.6 4.6 %collective-permute-start = (bf16[128,1024]{1,0:T(8,128)(2,1)}, bf16[128,1024]{1,0:T(8,128)(2,1)S(1)}, u32[]{:S(2)}, u32[]{:S(2)}) collective-permute-start(bf16[128,1024]{1,0:T(8,128)(2,1)} %param.5), channel_id=1, source_target_pairs={{0,0},{16,32},{32,16},{48,48},{1,1},{17,33},{33,17},{49,49},{2,2},... | collective-permute-start | bytes 786440 | tf_op jit(solution)/shard_map/ppermute | solution.py:28
  5.2 1.9 %collective-permute-start.1 = (s32[8,8]{1,0:T(8,128)}, s32[8,8]{1,0:T(8,128)S(1)}, u32[]{:S(2)}, u32[]{:S(2)}) collective-permute-start(s32[8,8]{1,0:T(8,128)} %param.6), channel_id=1, source_target_pairs={{0,0},{16,32},{32,16},{48,48},{1,1},{17,33},{33,17},{49,49},{2,2},... | collective-permute-start | bytes 776 | tf_op jit(solution)/shard_map/ppermute | solution.py:28
  7.2 1.7 dynamic-slice_bitcast_fusion
  9.0 2.9 %collective-permute-start.4 = (bf16[8,128,256]{2,1,0:T(8,128)(2,1)S(1)}, bf16[8,128,256]{2,1,0:T(8,128)(2,1)S(1)}, u32[]{:S(2)}, u32[]{:S(2)}) collective-permute-start(bf16[8,128,256]{2,1,0:T(8,128)(2,1)S(1)} %get-tuple-element.41), channel_id=1, source_target_pairs={{0,64},{16,80},{64,0},{80,16},{1,65},{17,81},{65,1},{81,17},{2,66}... | collective-permute-start | bytes 1572872 | tf_op jit(solution)/shard_map/ppermute | solution.py:24
  11.9 2.0 %collective-permute-start.3 = (bf16[8,128,256]{2,1,0:T(8,128)(2,1)S(1)}, bf16[8,128,256]{2,1,0:T(8,128)(2,1)S(1)}, u32[]{:S(2)}, u32[]{:S(2)}) collective-permute-start(bf16[8,128,256]{2,1,0:T(8,128)(2,1)S(1)} %get-tuple-element.42), channel_id=1, source_target_pairs={{0,80},{16,0},{64,16},{80,64},{1,81},{17,1},{65,17},{81,65},{2,82}... | collective-permute-start | bytes 1572872 | tf_op jit(solution)/shard_map/ppermute | solution.py:24
  13.9 2.8 %collective-permute-start.17 = (bf16[64,1024]{1,0:T(8,128)(2,1)S(1)}, bf16[64,1024]{1,0:T(8,128)(2,1)S(1)}, u32[]{:S(2)}, u32[]{:S(2)}) collective-permute-start(bf16[64,1024]{1,0:T(8,128)(2,1)S(1)} %get-tuple-element.46), channel_id=1, source_target_pairs={{0,2},{1,3},{2,0},{3,1},{4,6},{5,7},{6,4},{7,5},{8,10},{9,11},{10,... | collective-permute-start | bytes 393224 | tf_op jit(solution)/shard_map/ppermute | solution.py:24
  16.7 0.9 collective-permute-start.16
  17.6 2.8 %collective-permute-done.17 = bf16[64,1024]{1,0:T(8,128)(2,1)S(1)} collective-permute-done((bf16[64,1024]{1,0:T(8,128)(2,1)S(1)}, bf16[64,1024]{1,0:T(8,128)(2,1)S(1)}, u32[]{:S(2)}, u32[]{:S(2)}) %collective-permute-start.17) | collective-permute-done | bytes 131104 | tf_op jit(solution)/shard_map/ppermute | solution.py:24
  20.4 1.3 collective-permute-start.18
  21.7 1.6 collective-permute-done.16
  23.3 3.6 %collective-permute-start.11 = (bf16[64,1024]{1,0:T(8,128)(2,1)S(1)}, bf16[64,1024]{1,0:T(8,128)(2,1)S(1)}, u32[]{:S(2)}, u32[]{:S(2)}) collective-permute-start(bf16[64,1024]{1,0:T(8,128)(2,1)S(1)} %get-tuple-element.47), channel_id=1, source_target_pairs={{0,8},{4,12},{8,0},{12,4},{1,9},{5,13},{9,1},{13,5},{2,10},{6,14},... | collective-permute-start | bytes 393224 | tf_op jit(solution)/shard_map/ppermute | solution.py:24
  26.9 2.6 %collective-permute-start.10 = (bf16[64,1024]{1,0:T(8,128)(2,1)S(1)}, bf16[64,1024]{1,0:T(8,128)(2,1)S(1)}, u32[]{:S(2)}, u32[]{:S(2)}) collective-permute-start(bf16[64,1024]{1,0:T(8,128)(2,1)S(1)} %get-tuple-element.47), channel_id=1, source_target_pairs={{0,12},{4,0},{8,4},{12,8},{1,13},{5,1},{9,5},{13,9},{2,14},{6,2},{... | collective-permute-start | bytes 393224 | tf_op jit(solution)/shard_map/ppermute | solution.py:24
  29.5 0.3 collective-permute-done.11
  29.8 0.8 collective-permute-start.12
  30.6 0.9 pad_maximum_fusion.1.refs_12_
  31.4 1.6 collective-permute-done.10
  33.0 1.9 %collective-permute-start.6 = (bf16[8,128,256]{2,1,0:T(8,128)(2,1)S(1)}, bf16[8,128,256]{2,1,0:T(8,128)(2,1)S(1)}, u32[]{:S(2)}, u32[]{:S(2)}) collective-permute-start(bf16[8,128,256]{2,1,0:T(8,128)(2,1)S(1)} %get-tuple-element.43.refs_0_), channel_id=1, source_target_pairs={{0,32},{32,0},{1,33},{33,1},{2,34},{34,2},{3,35},{35,3},{4,36},{36... | collective-permute-start | bytes 1572872 | tf_op jit(solution)/shard_map/ppermute | solution.py:24
  34.9 0.4 collective-permute-done.12
  35.4 3.9 %collective-permute-start.2 = (s32[8,8]{1,0:T(8,128)S(1)}, s32[8,8]{1,0:T(8,128)S(1)}, u32[]{:S(2)}, u32[]{:S(2)}) collective-permute-start(s32[8,8]{1,0:T(8,128)S(1)} %collective-permute-done.1), channel_id=1, source_target_pairs={{0,32},{32,0},{1,33},{33,1},{2,34},{34,2},{3,35},{35,3},{4,36},{36... | collective-permute-start | bytes 776 | tf_op jit(solution)/shard_map/ppermute | solution.py:24
  39.2 0.9 pad_maximum_fusion.refs_8_
  40.1 1.0 collective-permute-start.15
  41.1 2.5 %collective-permute-start.14 = (bf16[4,64,1024]{2,1,0:T(8,128)(2,1)}, bf16[4,64,1024]{2,1,0:T(8,128)(2,1)}, u32[]{:S(2)}, u32[]{:S(2)}) collective-permute-start(bf16[4,64,1024]{2,1,0:T(8,128)(2,1)} %pad_maximum_fusion.refs_8_), channel_id=1, source_target_pairs={{0,2},{1,3},{2,0},{3,1},{4,6},{5,7},{6,4},{7,5},{8,10},{9,11},{10,... | collective-permute-start | bytes 1572872 | tf_op jit(solution)/shard_map/ppermute | solution.py:24
  43.6 0.4 collective-permute-start.13
  44.9 3.0 %collective-permute-start.20 = (bf16[4,64,1024]{2,1,0:T(8,128)(2,1)}, bf16[4,64,1024]{2,1,0:T(8,128)(2,1)}, u32[]{:S(2)}, u32[]{:S(2)}) collective-permute-start(bf16[4,64,1024]{2,1,0:T(8,128)(2,1)} %pad_maximum_fusion.1.refs_12_), channel_id=1, source_target_pairs={{0,8},{4,12},{8,0},{12,4},{1,9},{5,13},{9,1},{13,5},{2,10},{6,14},... | collective-permute-start | bytes 1572872 | tf_op jit(solution)/shard_map/ppermute | solution.py:24
  47.9 7.0 %collective-permute-done.15.refs_11_ = bf16[4,64,1024]{2,1,0:T(8,128)(2,1)S(1)} collective-permute-done((bf16[4,64,1024]{2,1,0:T(8,128)(2,1)}, bf16[4,64,1024]{2,1,0:T(8,128)(2,1)S(1)}, u32[]{:S(2)}, u32[]{:S(2)}) %collective-permute-start.15) | collective-permute-done | bytes 524320 | tf_op jit(solution)/shard_map/ppermute | solution.py:24
  54.9 0.8 copy-done.1
  55.7 1.7 collective-permute-start.19
  57.4 9.5 %collective-permute-done.14.refs_10_ = bf16[4,64,1024]{2,1,0:T(8,128)(2,1)} collective-permute-done((bf16[4,64,1024]{2,1,0:T(8,128)(2,1)}, bf16[4,64,1024]{2,1,0:T(8,128)(2,1)}, u32[]{:S(2)}, u32[]{:S(2)}) %collective-permute-start.14) | collective-permute-done | bytes 524320 | tf_op jit(solution)/shard_map/ppermute | solution.py:24
  66.9 1.1 collective-permute-start.9
  68.0 0.5 collective-permute-start.7
  68.6 0.2 reduce_window_sum.11
  68.8 0.1 convert_reduce_fusion.count_ref
  68.9 0.4 select_reduce_fusion.list_ref
  69.3 1.2 collective-permute-done.19.refs_13_
  70.5 0.7 collective-permute-done.7.refs_5_
  71.2 1.0 copy-done.2
  72.2 17.5 %scores.1 = (f32[16,4,128,256]{3,2,1,0:T(8,128)}, f32[32,128]{1,0:T(8,128)S(1)}) custom-call(s32[2]{0:T(128)S(1)} %pad_add_fusion.here_ref, s32[16]{0:T(128)S(1)} %convert_reduce_fusion.count_ref, s32[16,8]{1,0:T(8,128)S(1)} %select_reduce_fusion.list_ref, f32[1]{0:T(128)S(6)} %div.33.scale_ref, bf16[8,128,256]{2,1,0:T(8,128)(2,1)S(1)} %get-tuple-element.43.refs_0_, ...), custom_call_target="tpu_custom_call" | custom-call | tf_op jit(solution)/shard_map/scores/pallas_call | solution.py:268
  89.8 4.7 %collective-permute-start.22 = (f32[32,128]{1,0:T(8,128)S(1)}, f32[32,128]{1,0:T(8,128)S(1)}, u32[]{:S(2)}, u32[]{:S(2)}) collective-permute-start(f32[32,128]{1,0:T(8,128)S(1)} %get-tuple-element.22.mine_ref), channel_id=1, source_target_pairs={{0,32},{32,0},{1,33},{33,1},{2,34},{34,2},{3,35},{35,3},{4,36},{36... | collective-permute-start | bytes 49160 | tf_op jit(solution)/shard_map/ppermute | solution.py:24
  94.5 0.8 collective-permute-done.22.other_ref
  95.3 12.3 %sums.1 = (bf16[272,1024]{1,0:T(8,128)(2,1)S(1)}, bf16[272,1024]{1,0:T(8,128)(2,1)S(1)}, bf16[272,1024]{1,0:T(8,128)(2,1)S(1)}, bf16[272,1024]{1,0:T(8,128)(2,1)...) custom-call(s32[2]{0:T(128)S(1)} %pad_add_fusion.here_ref, ...), custom_call_target="tpu_custom_call" | custom-call | tf_op jit(solution)/shard_map/sums/pallas_call | solution.py:289
  107.7 3.0 %collective-permute-start.24 = (bf16[272,1024]{1,0:T(8,128)(2,1)S(1)}, bf16[272,1024]{1,0:T(8,128)(2,1)S(1)}, u32[]{:S(2)}, u32[]{:S(2)}) collective-permute-start(bf16[272,1024]{1,0:T(8,128)(2,1)S(1)} %get-tuple-element.25), channel_id=1, source_target_pairs={{0,8},{4,12},{8,0},{12,4},{1,9},{5,13},{9,1},{13,5},{2,10},{6,14},... | collective-permute-start | bytes 1671176 | tf_op jit(solution)/shard_map/ppermute | solution.py:24
  110.7 1.6 collective-permute-start.26
  112.3 0.2 collective-permute-start.27
  112.5 8.2 %collective-permute-done.23.refs_1_ = bf16[272,1024]{1,0:T(8,128)(2,1)S(1)} collective-permute-done((bf16[272,1024]{1,0:T(8,128)(2,1)S(1)}, bf16[272,1024]{1,0:T(8,128)(2,1)S(1)}, u32[]{:S(2)}, u32[]{:S(2)}) %collective-permute-start.23) | collective-permute-done | bytes 557088 | tf_op jit(solution)/shard_map/ppermute | solution.py:24
  120.7 12.2 %collective-permute-done.24.refs_2_ = bf16[272,1024]{1,0:T(8,128)(2,1)S(1)} collective-permute-done((bf16[272,1024]{1,0:T(8,128)(2,1)S(1)}, bf16[272,1024]{1,0:T(8,128)(2,1)S(1)}, u32[]{:S(2)}, u32[]{:S(2)}) %collective-permute-start.24) | collective-permute-done | bytes 557088 | tf_op jit(solution)/shard_map/ppermute | solution.py:24
  132.9 2.2 %collective-permute-done.25.refs_3_ = bf16[272,1024]{1,0:T(8,128)(2,1)S(1)} collective-permute-done((bf16[272,1024]{1,0:T(8,128)(2,1)}, bf16[272,1024]{1,0:T(8,128)(2,1)S(1)}, u32[]{:S(2)}, u32[]{:S(2)}) %collective-permute-start.25) | collective-permute-done | bytes 557088 | tf_op jit(solution)/shard_map/ppermute | solution.py:24
  135.1 0.8 collective-permute-done.28.refs_7_
  135.9 1.1 copy-done
  137.0 0.6 fold.1
  137.6 0.7 copy-done.3
  138.2 0.7 copy-done.4
  138.9 2.1 %collective-permute-start.29 = (bf16[80,1024]{1,0:T(8,128)(2,1)S(1)}, bf16[80,1024]{1,0:T(8,128)(2,1)S(1)}, u32[]{:S(2)}, u32[]{:S(2)}) collective-permute-start(bf16[80,1024]{1,0:T(8,128)(2,1)S(1)} %get-tuple-element.32), channel_id=1, source_target_pairs={{0,1},{1,2},{2,3},{3,0},{4,5},{5,6},{6,7},{7,4},{8,9},{9,10},{10,1... | collective-permute-start | bytes 491528 | tf_op jit(solution)/shard_map/ppermute | solution.py:24
  141.0 2.4 %collective-permute-start.30 = (bf16[80,1024]{1,0:T(8,128)(2,1)S(1)}, bf16[80,1024]{1,0:T(8,128)(2,1)S(1)}, u32[]{:S(2)}, u32[]{:S(2)}) collective-permute-start(bf16[80,1024]{1,0:T(8,128)(2,1)S(1)} %get-tuple-element.33), channel_id=1, source_target_pairs={{0,2},{1,3},{2,0},{3,1},{4,6},{5,7},{6,4},{7,5},{8,10},{9,11},{10,... | collective-permute-start | bytes 491528 | tf_op jit(solution)/shard_map/ppermute | solution.py:24
  143.4 2.3 %collective-permute-start.32 = (bf16[80,1024]{1,0:T(8,128)(2,1)S(1)}, bf16[80,1024]{1,0:T(8,128)(2,1)S(1)}, u32[]{:S(2)}, u32[]{:S(2)}) collective-permute-start(bf16[80,1024]{1,0:T(8,128)(2,1)S(1)} %get-tuple-element.36), channel_id=1, source_target_pairs={{0,4},{4,8},{8,12},{12,0},{1,5},{5,9},{9,13},{13,1},{2,6},{6,10},{... | collective-permute-start | bytes 491528 | tf_op jit(solution)/shard_map/ppermute | solution.py:24
  145.7 0.1 collective-permute-start.33
  145.9 3.3 %collective-permute-start.34 = (bf16[80,1024]{1,0:T(8,128)(2,1)S(1)}, bf16[80,1024]{1,0:T(8,128)(2,1)S(1)}, u32[]{:S(2)}, u32[]{:S(2)}) collective-permute-start(bf16[80,1024]{1,0:T(8,128)(2,1)S(1)} %get-tuple-element.38), channel_id=1, source_target_pairs={{0,12},{4,0},{8,4},{12,8},{1,13},{5,1},{9,5},{13,9},{2,14},{6,2},{... | collective-permute-start | bytes 491528 | tf_op jit(solution)/shard_map/ppermute | solution.py:24
  149.2 3.2 %collective-permute-done.33.refs_6_ = bf16[80,1024]{1,0:T(8,128)(2,1)S(1)} collective-permute-done((bf16[80,1024]{1,0:T(8,128)(2,1)S(1)}, bf16[80,1024]{1,0:T(8,128)(2,1)S(1)}, u32[]{:S(2)}, u32[]{:S(2)}) %collective-permute-start.33) | collective-permute-done | bytes 163872 | tf_op jit(solution)/shard_map/ppermute | solution.py:24
  152.5 0.6 copy-done.10
  153.2 2.4 %finish.1 = bf16[128,1024]{1,0:T(8,128)(2,1)} custom-call(bf16[128,1024]{1,0:T(8,128)(2,1)} %copy-done.5, bf16[80,1024]{1,0:T(8,128)(2,1)} %copy-done.3, bf16[80,1024]{1,0:T(8,128)(2,1)} %copy-done.6, bf16[80,1024]{1,0:T(8,128)(2,1)} %copy-done.7, bf16[80,1024]{1,0:T(8,128)(2,1)} %copy-done.8, bf16[80,1024]{1,0:T(8,128)(2,1)} %copy-done.4, ...), custom_call_target="tpu_custom_call" | custom-call | tf_op jit(solution)/shard_map/finish/pallas_call | solution.py:324
  155.6 17.4 %collective-permute-start.35 = (bf16[128,1024]{1,0:T(8,128)(2,1)}, bf16[128,1024]{1,0:T(8,128)(2,1)S(1)}, u32[]{:S(2)}, u32[]{:S(2)}) collective-permute-start(bf16[128,1024]{1,0:T(8,128)(2,1)} %finish.1), channel_id=1, source_target_pairs={{0,0},{16,32},{32,16},{48,48},{1,1},{17,33},{33,17},{49,49},{2,2},... | collective-permute-start | bytes 786440 | tf_op jit(solution)/shard_map/ppermute | solution.py:28
  173.0 1.9 %collective-permute-start.36 = (f32[8,128]{1,0:T(8,128)S(1)}, f32[8,128]{1,0:T(8,128)S(1)}, u32[]{:S(2)}, u32[]{:S(2)}) collective-permute-start(f32[8,128]{1,0:T(8,128)S(1)} %constant_dynamic-slice_fusion), channel_id=1, source_target_pairs={{0,0},{16,32},{32,16},{48,48},{1,1},{17,33},{33,17},{49,49},{2,2},... | collective-permute-start | bytes 12296 | tf_op jit(solution)/shard_map/ppermute | solution.py:28
  174.9 3.0 %collective-permute-done.36 = f32[8,128]{1,0:T(8,128)S(1)} collective-permute-done((f32[8,128]{1,0:T(8,128)S(1)}, f32[8,128]{1,0:T(8,128)S(1)}, u32[]{:S(2)}, u32[]{:S(2)}) %collective-permute-start.36) | collective-permute-done | bytes 4128 | tf_op jit(solution)/shard_map/ppermute | solution.py:28
  177.9 0.7 copy.13
  178.6 0.6 copy.14
  (55 shorter events, 0.7 us)
Async XLA Ops:
  0.6 13.2 %collective-permute-start = (bf16[128,1024]{1,0:T(8,128)(2,1)}, bf16[128,1024]{1,0:T(8,128)(2,1)S(1)}, u32[]{:S(2)}, u32[]{:S(2)}) collective-permute-start(bf16[128,1024]{1,0:T(8,128)(2,1)} %param.5), channel_id=1, source_target_pairs={{0,0},{16,32},{32,16},{48,48},{1,1},{17,33},{33,17},{49,49},{2,2},... | collective-permute-start | bytes 786440 | tf_op jit(solution)/shard_map/ppermute | solution.py:28
  5.2 11.5 %collective-permute-start.1 = (s32[8,8]{1,0:T(8,128)}, s32[8,8]{1,0:T(8,128)S(1)}, u32[]{:S(2)}, u32[]{:S(2)}) collective-permute-start(s32[8,8]{1,0:T(8,128)} %param.6), channel_id=1, source_target_pairs={{0,0},{16,32},{32,16},{48,48},{1,1},{17,33},{33,17},{49,49},{2,2},... | collective-permute-start | bytes 776 | tf_op jit(solution)/shard_map/ppermute | solution.py:28
  8.9 32.2 %collective-permute-start.5 = (bf16[8,128,256]{2,1,0:T(8,128)(2,1)S(1)}, bf16[8,128,256]{2,1,0:T(8,128)(2,1)S(1)}, u32[]{:S(2)}, u32[]{:S(2)}) collective-permute-start(bf16[8,128,256]{2,1,0:T(8,128)(2,1)S(1)} %get-tuple-element.40), channel_id=1, source_target_pairs={{0,16},{16,64},{64,80},{80,0},{1,17},{17,65},{65,81},{81,1},{2,18}... | collective-permute-start | bytes 1572872 | tf_op jit(solution)/shard_map/ppermute | solution.py:24
  9.0 34.6 %collective-permute-start.4 = (bf16[8,128,256]{2,1,0:T(8,128)(2,1)S(1)}, bf16[8,128,256]{2,1,0:T(8,128)(2,1)S(1)}, u32[]{:S(2)}, u32[]{:S(2)}) collective-permute-start(bf16[8,128,256]{2,1,0:T(8,128)(2,1)S(1)} %get-tuple-element.41), channel_id=1, source_target_pairs={{0,64},{16,80},{64,0},{80,16},{1,65},{17,81},{65,1},{81,17},{2,66}... | collective-permute-start | bytes 1572872 | tf_op jit(solution)/shard_map/ppermute | solution.py:24
  11.9 32.1 %collective-permute-start.3 = (bf16[8,128,256]{2,1,0:T(8,128)(2,1)S(1)}, bf16[8,128,256]{2,1,0:T(8,128)(2,1)S(1)}, u32[]{:S(2)}, u32[]{:S(2)}) collective-permute-start(bf16[8,128,256]{2,1,0:T(8,128)(2,1)S(1)} %get-tuple-element.42), channel_id=1, source_target_pairs={{0,80},{16,0},{64,16},{80,64},{1,81},{17,1},{65,17},{81,65},{2,82}... | collective-permute-start | bytes 1572872 | tf_op jit(solution)/shard_map/ppermute | solution.py:24
  13.9 75.9 %copy-start.5 = (bf16[128,1024]{1,0:T(8,128)(2,1)}, bf16[128,1024]{1,0:T(8,128)(2,1)S(1)}, u32[]{:S(2)}) copy-start(bf16[128,1024]{1,0:T(8,128)(2,1)S(1)} %collective-permute-done.panel_ref) | copy-start | bytes 786436
  13.9 6.5 %collective-permute-start.17 = (bf16[64,1024]{1,0:T(8,128)(2,1)S(1)}, bf16[64,1024]{1,0:T(8,128)(2,1)S(1)}, u32[]{:S(2)}, u32[]{:S(2)}) collective-permute-start(bf16[64,1024]{1,0:T(8,128)(2,1)S(1)} %get-tuple-element.46), channel_id=1, source_target_pairs={{0,2},{1,3},{2,0},{3,1},{4,6},{5,7},{6,4},{7,5},{8,10},{9,11},{10,... | collective-permute-start | bytes 393224 | tf_op jit(solution)/shard_map/ppermute | solution.py:24
  16.7 6.6 %collective-permute-start.16 = (bf16[64,1024]{1,0:T(8,128)(2,1)S(1)}, bf16[64,1024]{1,0:T(8,128)(2,1)S(1)}, u32[]{:S(2)}, u32[]{:S(2)}) collective-permute-start(bf16[64,1024]{1,0:T(8,128)(2,1)S(1)} %get-tuple-element.46), channel_id=1, source_target_pairs={{0,3},{1,0},{2,1},{3,2},{4,7},{5,4},{6,5},{7,6},{8,11},{9,8},{10,9... | collective-permute-start | bytes 393224 | tf_op jit(solution)/shard_map/ppermute | solution.py:24
  20.4 6.5 %collective-permute-start.18 = (bf16[64,1024]{1,0:T(8,128)(2,1)S(1)}, bf16[64,1024]{1,0:T(8,128)(2,1)S(1)}, u32[]{:S(2)}, u32[]{:S(2)}) collective-permute-start(bf16[64,1024]{1,0:T(8,128)(2,1)S(1)} %get-tuple-element.46), channel_id=1, source_target_pairs={{0,1},{1,2},{2,3},{3,0},{4,5},{5,6},{6,7},{7,4},{8,9},{9,10},{10,1... | collective-permute-start | bytes 393224 | tf_op jit(solution)/shard_map/ppermute | solution.py:24
  23.3 6.5 %collective-permute-start.11 = (bf16[64,1024]{1,0:T(8,128)(2,1)S(1)}, bf16[64,1024]{1,0:T(8,128)(2,1)S(1)}, u32[]{:S(2)}, u32[]{:S(2)}) collective-permute-start(bf16[64,1024]{1,0:T(8,128)(2,1)S(1)} %get-tuple-element.47), channel_id=1, source_target_pairs={{0,8},{4,12},{8,0},{12,4},{1,9},{5,13},{9,1},{13,5},{2,10},{6,14},... | collective-permute-start | bytes 393224 | tf_op jit(solution)/shard_map/ppermute | solution.py:24
  26.9 6.1 %collective-permute-start.10 = (bf16[64,1024]{1,0:T(8,128)(2,1)S(1)}, bf16[64,1024]{1,0:T(8,128)(2,1)S(1)}, u32[]{:S(2)}, u32[]{:S(2)}) collective-permute-start(bf16[64,1024]{1,0:T(8,128)(2,1)S(1)} %get-tuple-element.47), channel_id=1, source_target_pairs={{0,12},{4,0},{8,4},{12,8},{1,13},{5,1},{9,5},{13,9},{2,14},{6,2},{... | collective-permute-start | bytes 393224 | tf_op jit(solution)/shard_map/ppermute | solution.py:24
  29.8 5.6 %collective-permute-start.12 = (bf16[64,1024]{1,0:T(8,128)(2,1)S(1)}, bf16[64,1024]{1,0:T(8,128)(2,1)S(1)}, u32[]{:S(2)}, u32[]{:S(2)}) collective-permute-start(bf16[64,1024]{1,0:T(8,128)(2,1)S(1)} %get-tuple-element.47), channel_id=1, source_target_pairs={{0,4},{4,8},{8,12},{12,0},{1,5},{5,9},{9,13},{13,1},{2,6},{6,10},{... | collective-permute-start | bytes 393224 | tf_op jit(solution)/shard_map/ppermute | solution.py:24
  33.0 11.8 %collective-permute-start.6 = (bf16[8,128,256]{2,1,0:T(8,128)(2,1)S(1)}, bf16[8,128,256]{2,1,0:T(8,128)(2,1)S(1)}, u32[]{:S(2)}, u32[]{:S(2)}) collective-permute-start(bf16[8,128,256]{2,1,0:T(8,128)(2,1)S(1)} %get-tuple-element.43.refs_0_), channel_id=1, source_target_pairs={{0,32},{32,0},{1,33},{33,1},{2,34},{34,2},{3,35},{35,3},{4,36},{36... | collective-permute-start | bytes 1572872 | tf_op jit(solution)/shard_map/ppermute | solution.py:24
  35.4 4.8 %collective-permute-start.2 = (s32[8,8]{1,0:T(8,128)S(1)}, s32[8,8]{1,0:T(8,128)S(1)}, u32[]{:S(2)}, u32[]{:S(2)}) collective-permute-start(s32[8,8]{1,0:T(8,128)S(1)} %collective-permute-done.1), channel_id=1, source_target_pairs={{0,32},{32,0},{1,33},{33,1},{2,34},{34,2},{3,35},{35,3},{4,36},{36... | collective-permute-start | bytes 776 | tf_op jit(solution)/shard_map/ppermute | solution.py:24
  40.1 14.8 %collective-permute-start.15 = (bf16[4,64,1024]{2,1,0:T(8,128)(2,1)}, bf16[4,64,1024]{2,1,0:T(8,128)(2,1)S(1)}, u32[]{:S(2)}, u32[]{:S(2)}) collective-permute-start(bf16[4,64,1024]{2,1,0:T(8,128)(2,1)} %pad_maximum_fusion.refs_8_), channel_id=1, source_target_pairs={{0,1},{1,2},{2,3},{3,0},{4,5},{5,6},{6,7},{7,4},{8,9},{9,10},{10,1... | collective-permute-start | bytes 1572872 | tf_op jit(solution)/shard_map/ppermute | solution.py:24
  41.1 25.8 %collective-permute-start.14 = (bf16[4,64,1024]{2,1,0:T(8,128)(2,1)}, bf16[4,64,1024]{2,1,0:T(8,128)(2,1)}, u32[]{:S(2)}, u32[]{:S(2)}) collective-permute-start(bf16[4,64,1024]{2,1,0:T(8,128)(2,1)} %pad_maximum_fusion.refs_8_), channel_id=1, source_target_pairs={{0,2},{1,3},{2,0},{3,1},{4,6},{5,7},{6,4},{7,5},{8,10},{9,11},{10,... | collective-permute-start | bytes 1572872 | tf_op jit(solution)/shard_map/ppermute | solution.py:24
  43.6 24.4 %collective-permute-start.13 = (bf16[4,64,1024]{2,1,0:T(8,128)(2,1)}, bf16[4,64,1024]{2,1,0:T(8,128)(2,1)}, u32[]{:S(2)}, u32[]{:S(2)}) collective-permute-start(bf16[4,64,1024]{2,1,0:T(8,128)(2,1)} %pad_maximum_fusion.refs_8_), channel_id=1, source_target_pairs={{0,3},{1,0},{2,1},{3,2},{4,7},{5,4},{6,5},{7,6},{8,11},{9,8},{10,9... | collective-permute-start | bytes 1572872 | tf_op jit(solution)/shard_map/ppermute | solution.py:24
  44.0 24.1 %collective-permute-start.21 = (bf16[4,64,1024]{2,1,0:T(8,128)(2,1)}, bf16[4,64,1024]{2,1,0:T(8,128)(2,1)}, u32[]{:S(2)}, u32[]{:S(2)}) collective-permute-start(bf16[4,64,1024]{2,1,0:T(8,128)(2,1)} %pad_maximum_fusion.1.refs_12_), channel_id=1, source_target_pairs={{0,4},{4,8},{8,12},{12,0},{1,5},{5,9},{9,13},{13,1},{2,6},{6,10},{... | collective-permute-start | bytes 1572872 | tf_op jit(solution)/shard_map/ppermute | solution.py:24
  44.9 24.4 %collective-permute-start.20 = (bf16[4,64,1024]{2,1,0:T(8,128)(2,1)}, bf16[4,64,1024]{2,1,0:T(8,128)(2,1)}, u32[]{:S(2)}, u32[]{:S(2)}) collective-permute-start(bf16[4,64,1024]{2,1,0:T(8,128)(2,1)} %pad_maximum_fusion.1.refs_12_), channel_id=1, source_target_pairs={{0,8},{4,12},{8,0},{12,4},{1,9},{5,13},{9,1},{13,5},{2,10},{6,14},... | collective-permute-start | bytes 1572872 | tf_op jit(solution)/shard_map/ppermute | solution.py:24
  54.9 0.8 copy-start.1
  55.7 14.8 %collective-permute-start.19 = (bf16[4,64,1024]{2,1,0:T(8,128)(2,1)}, bf16[4,64,1024]{2,1,0:T(8,128)(2,1)}, u32[]{:S(2)}, u32[]{:S(2)}) collective-permute-start(bf16[4,64,1024]{2,1,0:T(8,128)(2,1)} %pad_maximum_fusion.1.refs_12_), channel_id=1, source_target_pairs={{0,12},{4,0},{8,4},{12,8},{1,13},{5,1},{9,5},{13,9},{2,14},{6,2},{... | collective-permute-start | bytes 1572872 | tf_op jit(solution)/shard_map/ppermute | solution.py:24
  66.9 3.6 %collective-permute-start.9 = (bf16[8,128,256]{2,1,0:T(8,128)(2,1)S(1)}, bf16[8,128,256]{2,1,0:T(8,128)(2,1)S(1)}, u32[]{:S(2)}, u32[]{:S(2)}) collective-permute-start(bf16[8,128,256]{2,1,0:T(8,128)(2,1)S(1)} %collective-permute-done.5.refs_3_), channel_id=1, source_target_pairs={{0,32},{32,0},{1,33},{33,1},{2,34},{34,2},{3,35},{35,3},{4,36},{36... | collective-permute-start | bytes 1572872 | tf_op jit(solution)/shard_map/ppermute | solution.py:24
  68.0 2.5 %collective-permute-start.8 = (bf16[8,128,256]{2,1,0:T(8,128)(2,1)S(1)}, bf16[8,128,256]{2,1,0:T(8,128)(2,1)}, u32[]{:S(2)}, u32[]{:S(2)}) collective-permute-start(bf16[8,128,256]{2,1,0:T(8,128)(2,1)S(1)} %collective-permute-done.4.refs_2_), channel_id=1, source_target_pairs={{0,32},{32,0},{1,33},{33,1},{2,34},{34,2},{3,35},{35,3},{4,36},{36... | collective-permute-start | bytes 1572872 | tf_op jit(solution)/shard_map/ppermute | solution.py:24
  68.0 3.2 %collective-permute-start.7 = (bf16[8,128,256]{2,1,0:T(8,128)(2,1)S(1)}, bf16[8,128,256]{2,1,0:T(8,128)(2,1)}, u32[]{:S(2)}, u32[]{:S(2)}) collective-permute-start(bf16[8,128,256]{2,1,0:T(8,128)(2,1)S(1)} %collective-permute-done.3.refs_1_), channel_id=1, source_target_pairs={{0,32},{32,0},{1,33},{33,1},{2,34},{34,2},{3,35},{35,3},{4,36},{36... | collective-permute-start | bytes 1572872 | tf_op jit(solution)/shard_map/ppermute | solution.py:24
  71.2 1.0 copy-start.2
  89.8 5.5 %collective-permute-start.22 = (f32[32,128]{1,0:T(8,128)S(1)}, f32[32,128]{1,0:T(8,128)S(1)}, u32[]{:S(2)}, u32[]{:S(2)}) collective-permute-start(f32[32,128]{1,0:T(8,128)S(1)} %get-tuple-element.22.mine_ref), channel_id=1, source_target_pairs={{0,32},{32,0},{1,33},{33,1},{2,34},{34,2},{3,35},{35,3},{4,36},{36... | collective-permute-start | bytes 49160 | tf_op jit(solution)/shard_map/ppermute | solution.py:24
  107.7 13.1 %collective-permute-start.23 = (bf16[272,1024]{1,0:T(8,128)(2,1)S(1)}, bf16[272,1024]{1,0:T(8,128)(2,1)S(1)}, u32[]{:S(2)}, u32[]{:S(2)}) collective-permute-start(bf16[272,1024]{1,0:T(8,128)(2,1)S(1)} %get-tuple-element.24), channel_id=1, source_target_pairs={{0,4},{4,8},{8,12},{12,0},{1,5},{5,9},{9,13},{13,1},{2,6},{6,10},{... | collective-permute-start | bytes 1671176 | tf_op jit(solution)/shard_map/ppermute | solution.py:24
  107.7 25.2 %collective-permute-start.24 = (bf16[272,1024]{1,0:T(8,128)(2,1)S(1)}, bf16[272,1024]{1,0:T(8,128)(2,1)S(1)}, u32[]{:S(2)}, u32[]{:S(2)}) collective-permute-start(bf16[272,1024]{1,0:T(8,128)(2,1)S(1)} %get-tuple-element.25), channel_id=1, source_target_pairs={{0,8},{4,12},{8,0},{12,4},{1,9},{5,13},{9,1},{13,5},{2,10},{6,14},... | collective-permute-start | bytes 1671176 | tf_op jit(solution)/shard_map/ppermute | solution.py:24
  110.7 24.4 %collective-permute-start.25 = (bf16[272,1024]{1,0:T(8,128)(2,1)}, bf16[272,1024]{1,0:T(8,128)(2,1)S(1)}, u32[]{:S(2)}, u32[]{:S(2)}) collective-permute-start(bf16[272,1024]{1,0:T(8,128)(2,1)} %get-tuple-element.26), channel_id=1, source_target_pairs={{0,12},{4,0},{8,4},{12,8},{1,13},{5,1},{9,5},{13,9},{2,14},{6,2},{... | collective-permute-start | bytes 1671176 | tf_op jit(solution)/shard_map/ppermute | solution.py:24
  110.7 24.4 %collective-permute-start.26 = (bf16[272,1024]{1,0:T(8,128)(2,1)}, bf16[272,1024]{1,0:T(8,128)(2,1)S(1)}, u32[]{:S(2)}, u32[]{:S(2)}) collective-permute-start(bf16[272,1024]{1,0:T(8,128)(2,1)} %get-tuple-element.28), channel_id=1, source_target_pairs={{0,1},{1,2},{2,3},{3,0},{4,5},{5,6},{6,7},{7,4},{8,9},{9,10},{10,1... | collective-permute-start | bytes 1671176 | tf_op jit(solution)/shard_map/ppermute | solution.py:24
  112.3 22.8 %collective-permute-start.27 = (bf16[272,1024]{1,0:T(8,128)(2,1)}, bf16[272,1024]{1,0:T(8,128)(2,1)S(1)}, u32[]{:S(2)}, u32[]{:S(2)}) collective-permute-start(bf16[272,1024]{1,0:T(8,128)(2,1)} %get-tuple-element.29), channel_id=1, source_target_pairs={{0,2},{1,3},{2,0},{3,1},{4,6},{5,7},{6,4},{7,5},{8,10},{9,11},{10,... | collective-permute-start | bytes 1671176 | tf_op jit(solution)/shard_map/ppermute | solution.py:24
  120.7 15.2 %collective-permute-start.28 = (bf16[272,1024]{1,0:T(8,128)(2,1)}, bf16[272,1024]{1,0:T(8,128)(2,1)S(1)}, u32[]{:S(2)}, u32[]{:S(2)}) collective-permute-start(bf16[272,1024]{1,0:T(8,128)(2,1)} %get-tuple-element.30), channel_id=1, source_target_pairs={{0,3},{1,0},{2,1},{3,2},{4,7},{5,4},{6,5},{7,6},{8,11},{9,8},{10,9... | collective-permute-start | bytes 1671176 | tf_op jit(solution)/shard_map/ppermute | solution.py:24
  135.9 1.1 copy-start
  137.6 0.7 copy-start.3
  138.2 0.7 copy-start.4
  138.9 7.0 %collective-permute-start.29 = (bf16[80,1024]{1,0:T(8,128)(2,1)S(1)}, bf16[80,1024]{1,0:T(8,128)(2,1)S(1)}, u32[]{:S(2)}, u32[]{:S(2)}) collective-permute-start(bf16[80,1024]{1,0:T(8,128)(2,1)S(1)} %get-tuple-element.32), channel_id=1, source_target_pairs={{0,1},{1,2},{2,3},{3,0},{4,5},{5,6},{6,7},{7,4},{8,9},{9,10},{10,1... | collective-permute-start | bytes 491528 | tf_op jit(solution)/shard_map/ppermute | solution.py:24
  141.0 8.2 %collective-permute-start.30 = (bf16[80,1024]{1,0:T(8,128)(2,1)S(1)}, bf16[80,1024]{1,0:T(8,128)(2,1)S(1)}, u32[]{:S(2)}, u32[]{:S(2)}) collective-permute-start(bf16[80,1024]{1,0:T(8,128)(2,1)S(1)} %get-tuple-element.33), channel_id=1, source_target_pairs={{0,2},{1,3},{2,0},{3,1},{4,6},{5,7},{6,4},{7,5},{8,10},{9,11},{10,... | collective-permute-start | bytes 491528 | tf_op jit(solution)/shard_map/ppermute | solution.py:24
  143.4 5.8 %collective-permute-start.31 = (bf16[80,1024]{1,0:T(8,128)(2,1)S(1)}, bf16[80,1024]{1,0:T(8,128)(2,1)S(1)}, u32[]{:S(2)}, u32[]{:S(2)}) collective-permute-start(bf16[80,1024]{1,0:T(8,128)(2,1)S(1)} %get-tuple-element.34), channel_id=1, source_target_pairs={{0,3},{1,0},{2,1},{3,2},{4,7},{5,4},{6,5},{7,6},{8,11},{9,8},{10,9... | collective-permute-start | bytes 491528 | tf_op jit(solution)/shard_map/ppermute | solution.py:24
  143.4 5.8 %collective-permute-start.32 = (bf16[80,1024]{1,0:T(8,128)(2,1)S(1)}, bf16[80,1024]{1,0:T(8,128)(2,1)S(1)}, u32[]{:S(2)}, u32[]{:S(2)}) collective-permute-start(bf16[80,1024]{1,0:T(8,128)(2,1)S(1)} %get-tuple-element.36), channel_id=1, source_target_pairs={{0,4},{4,8},{8,12},{12,0},{1,5},{5,9},{9,13},{13,1},{2,6},{6,10},{... | collective-permute-start | bytes 491528 | tf_op jit(solution)/shard_map/ppermute | solution.py:24
  145.7 6.7 %collective-permute-start.33 = (bf16[80,1024]{1,0:T(8,128)(2,1)S(1)}, bf16[80,1024]{1,0:T(8,128)(2,1)S(1)}, u32[]{:S(2)}, u32[]{:S(2)}) collective-permute-start(bf16[80,1024]{1,0:T(8,128)(2,1)S(1)} %get-tuple-element.37), channel_id=1, source_target_pairs={{0,8},{4,12},{8,0},{12,4},{1,9},{5,13},{9,1},{13,5},{2,10},{6,14},... | collective-permute-start | bytes 491528 | tf_op jit(solution)/shard_map/ppermute | solution.py:24
  145.9 6.6 %copy-start.6 = (bf16[80,1024]{1,0:T(8,128)(2,1)}, bf16[80,1024]{1,0:T(8,128)(2,1)S(1)}, u32[]{:S(2)}) copy-start(bf16[80,1024]{1,0:T(8,128)(2,1)S(1)} %collective-permute-done.29.refs_1_) | copy-start | bytes 491524
  145.9 6.6 %collective-permute-start.34 = (bf16[80,1024]{1,0:T(8,128)(2,1)S(1)}, bf16[80,1024]{1,0:T(8,128)(2,1)S(1)}, u32[]{:S(2)}, u32[]{:S(2)}) collective-permute-start(bf16[80,1024]{1,0:T(8,128)(2,1)S(1)} %get-tuple-element.38), channel_id=1, source_target_pairs={{0,12},{4,0},{8,4},{12,8},{1,13},{5,1},{9,5},{13,9},{2,14},{6,2},{... | collective-permute-start | bytes 491528 | tf_op jit(solution)/shard_map/ppermute | solution.py:24
  149.2 3.3 %copy-start.7 = (bf16[80,1024]{1,0:T(8,128)(2,1)}, bf16[80,1024]{1,0:T(8,128)(2,1)S(1)}, u32[]{:S(2)}) copy-start(bf16[80,1024]{1,0:T(8,128)(2,1)S(1)} %collective-permute-done.30.refs_2_) | copy-start | bytes 491524
  149.2 3.3 %copy-start.8 = (bf16[80,1024]{1,0:T(8,128)(2,1)}, bf16[80,1024]{1,0:T(8,128)(2,1)S(1)}, u32[]{:S(2)}) copy-start(bf16[80,1024]{1,0:T(8,128)(2,1)S(1)} %collective-permute-done.31.refs_3_) | copy-start | bytes 491524
  149.2 3.3 %copy-start.9 = (bf16[80,1024]{1,0:T(8,128)(2,1)}, bf16[80,1024]{1,0:T(8,128)(2,1)S(1)}, u32[]{:S(2)}) copy-start(bf16[80,1024]{1,0:T(8,128)(2,1)S(1)} %collective-permute-done.32.refs_5_) | copy-start | bytes 491524
  152.5 0.7 copy-start.10
  152.5 0.7 copy-start.11
  155.6 22.3 %collective-permute-start.35 = (bf16[128,1024]{1,0:T(8,128)(2,1)}, bf16[128,1024]{1,0:T(8,128)(2,1)S(1)}, u32[]{:S(2)}, u32[]{:S(2)}) collective-permute-start(bf16[128,1024]{1,0:T(8,128)(2,1)} %finish.1), channel_id=1, source_target_pairs={{0,0},{16,32},{32,16},{48,48},{1,1},{17,33},{33,17},{49,49},{2,2},... | collective-permute-start | bytes 786440 | tf_op jit(solution)/shard_map/ppermute | solution.py:28
  173.0 4.9 %collective-permute-start.36 = (f32[8,128]{1,0:T(8,128)S(1)}, f32[8,128]{1,0:T(8,128)S(1)}, u32[]{:S(2)}, u32[]{:S(2)}) collective-permute-start(f32[8,128]{1,0:T(8,128)S(1)} %constant_dynamic-slice_fusion), channel_id=1, source_target_pairs={{0,0},{16,32},{32,16},{48,48},{1,1},{17,33},{33,17},{49,49},{2,2},... | collective-permute-start | bytes 12296 | tf_op jit(solution)/shard_map/ppermute | solution.py:28

commit v2 on v0

v2 whole, which is shorter than its diff:
```python
import math

import jax
import jax.numpy as jnp
from jax import lax
from jax.experimental import pallas as pl
from jax.experimental.pallas import tpu as pltpu
from jax.sharding import Mesh, PartitionSpec as P

PANEL = 128
BLOCK = 128
DIM = 1024
HALF = PANEL // 2
SLICE = 256
BLOCKS = 16
SLOTS = 8
Y = ("yh", "yl")
LOW = -1e30
HIGH = 1e30
LN2 = math.log(2.0)
PACK = 4 * HALF + 8
CHUNK = HALF + 8
STATS = 24


def moved(value, axis, by):
    size = lax.axis_size(axis)
    return lax.ppermute(value, axis, [(i, (i - by) % size) for i in range(size)])


def swapped(value):
    return lax.ppermute(value, ("c", "yl"), [(0, 0), (1, 2), (2, 1), (3, 3)])


def nt_dot(a, b):
    return lax.dot_general(a, b, (((1,), (1,)), ((), ())), preferred_element_type=jnp.float32)


def points_of(own, oth, c):
    parts = []
    for ref, core in ((own, c), (oth, 1 - c)):
        for yh in range(2):
            parts.append((ref, 16 * yh, pl.multiple_of((2 * yh + core) * SLICE, SLICE)))
    return parts


def rows_of(parts, places, features):
    return jnp.concatenate(
        [
            jnp.concatenate([ref[(place + shift) % 32] for ref, shift, _ in parts], axis=features)
            for place in places
        ],
        axis=1 - features,
    )


def by_turns(turns, run):
    for t in range(1, SLOTS // 2 + 1):
        pl.when(turns == t)(lambda t=t: run(t))


def split_kernel(*refs):
    for i in range(4):
        refs[4 + i][...] = refs[i][2 * (i % 2) : 2 * (i % 2) + 2]


def turn_kernel(ref, out):
    def one(i, _):
        out[i] = ref[i].T
        return 0

    lax.fori_loop(0, 32, one, 0, unroll=4)


def score_kernel(here_ref, count_ref, list_ref, place_ref, scale_ref, own, oth, *refs):
    a_in, b_in = refs[0:5], refs[5:10]
    l_ref, top_ref, stat_ref = refs[10:13]
    b_ref, bsem = refs[13:]

    def b_copy(dz, dx):
        src = b_in[dz].at[dx] if dz < 2 else b_in[4].at[dx] if dz == 3 else b_in[2 + dx // 2].at[dx % 2]
        return pltpu.make_async_copy(src, b_ref.at[dx, dz], bsem.at[dx, dz])

    for dx in (0, 1, 3, 2):
        for dz in range(4):
            b_copy(dz, dx).start()
    twice, once = scale_ref[0], scale_ref[1]
    parts = points_of(own, oth, here_ref[1])
    stat_ref[0:STATS, :] = jnp.full((STATS, BLOCK), LOW, jnp.float32)
    stat_ref[STATS : 2 * STATS, :] = jnp.zeros((STATS, BLOCK), jnp.float32)

    def panel_step(i, dx, a_ref, base):
        dz = base + i
        r = 4 * dx + dz
        pltpu.make_async_copy(b_in[0].at[0], b_ref.at[dx, dz], bsem.at[dx, dz]).wait()
        panel32 = jnp.concatenate([a_ref[i], b_ref[dx, dz]], axis=0).astype(jnp.float32)
        sqnorm = jnp.sum(panel32 * panel32, axis=1, keepdims=True) * once

        def run(turns):
            blocks = [list_ref[r, n] for n in range(2 * turns)]
            places = [place_ref[r, n] for n in range(2 * turns)]
            lhs = jnp.concatenate(
                [
                    jnp.concatenate(
                        [a_ref[i, :, pl.ds(at, SLICE)], b_ref[dx, dz, :, pl.ds(at, SLICE)]], axis=0
                    )
                    for _, _, at in parts
                ],
                axis=1,
            )
            old = jnp.concatenate([stat_ref[pl.ds(block, 1), :] for block in blocks], axis=1)
            total = jnp.concatenate(
                [stat_ref[pl.ds(STATS + block, 1), :] for block in blocks], axis=1
            )
            tops, adds = [], []
            for t in range(turns):
                lanes = slice(2 * t * BLOCK, 2 * (t + 1) * BLOCK)
                rhs = rows_of(parts, places[2 * t : 2 * t + 2], 0)
                logit = jnp.dot(lhs, rhs, preferred_element_type=jnp.float32) * twice - sqnorm
                top = jnp.maximum(old[:, lanes], jnp.max(logit, axis=0, keepdims=True))
                power = jnp.exp2(logit - top)
                l_ref[r, :, lanes] = power
                tops.append(top)
                adds.append(jnp.sum(power, axis=0, keepdims=True))
            new = jnp.concatenate(tops, axis=1)
            total = total * jnp.exp2(old - new) + jnp.concatenate(adds, axis=1)
            top_ref[r, :, 0 : 2 * turns * BLOCK] = jnp.broadcast_to(new, (8, 2 * turns * BLOCK))
            for j, block in enumerate(blocks):
                lanes = slice(j * BLOCK, (j + 1) * BLOCK)
                stat_ref[pl.ds(block, 1), :] = new[:, lanes]
                stat_ref[pl.ds(STATS + block, 1), :] = total[:, lanes]

        by_turns((count_ref[r] + 1) // 2, run)
        return 0

    stacks = ((0, 0, 4, 0), (1, 1, 4, 0), (3, 4, 4, 0), (2, 2, 2, 0), (2, 3, 2, 2))
    for dx, k, size, base in stacks:

        def step(i, _, dx=dx, k=k, base=base):
            return panel_step(i, dx, a_in[k], base)

        lax.fori_loop(0, size, step, 0)


def sum_kernel(
    here_ref, count_ref, list_ref, place_ref, own, oth, l_ref, top_ref, mine_ref, other_ref, *refs
):
    a_out, b_out, norm_ref = refs[0:4], refs[4:8], refs[8]
    b_ref, full_ref, mass_ref = refs[9:]
    parts = points_of(own, oth, here_ref[1])
    m0, s0 = mine_ref[0:STATS, :], mine_ref[STATS : 2 * STATS, :]
    m1, s1 = other_ref[0:STATS, :], other_ref[STATS : 2 * STATS, :]
    top = jnp.maximum(m0, m1)
    norm = top + jnp.log(s0 * jnp.exp2(m0 - top) + s1 * jnp.exp2(m1 - top)) * (1.0 / LN2)
    norm_ref[...] = norm[0:BLOCKS, :] * LN2
    row = lax.broadcasted_iota(jnp.int32, (STATS, BLOCK), 0)
    full_ref[...] = jnp.where(row < BLOCKS, norm, HIGH)
    mass_ref[...] = jnp.zeros_like(mass_ref)
    for ref in a_out:
        ref[4 * HALF :, :] = jnp.zeros((8, DIM), jnp.bfloat16)

    def panel_step(dx, _, dz):
        r = 4 * dx + dz
        arow = pl.multiple_of(dx * HALF, HALF)
        brows = slice(dz * HALF, (dz + 1) * HALF)
        turns = (count_ref[r] + 1) // 2

        @pl.when(turns == 0)
        def _():
            zeros = jnp.zeros((HALF, DIM), jnp.bfloat16)
            a_out[dz][pl.ds(arow, HALF), :] = zeros
            b_ref[dx, brows, :] = zeros

        def run(turns):
            blocks = [list_ref[r, n] for n in range(2 * turns)]
            places = [place_ref[r, n] for n in range(2 * turns)]
            norm = jnp.concatenate([full_ref[pl.ds(block, 1), :] for block in blocks], axis=1)
            lanes = slice(0, 2 * turns * BLOCK)
            factor = jnp.exp2(top_ref[r, 0:1, lanes] - norm)
            weight = (l_ref[r, :, lanes] * factor).astype(jnp.bfloat16)
            sums = jnp.dot(weight, rows_of(parts, places, 1), preferred_element_type=jnp.float32)
            sums = sums.astype(jnp.bfloat16)
            for i, (_, _, offset) in enumerate(parts):
                part = sums[:, i * SLICE : (i + 1) * SLICE]
                a_out[dz][pl.ds(arow, HALF), pl.ds(offset, SLICE)] = part[:HALF]
                b_ref[dx, brows, pl.ds(offset, SLICE)] = part[HALF:]
            mass = nt_dot(jnp.ones((8, 2 * turns * BLOCK), jnp.bfloat16), weight)[0:1, :]
            high = mass.astype(jnp.bfloat16).astype(jnp.float32)
            mass_ref[pl.ds(8 * dz + dx, 1), :] = high
            mass_ref[pl.ds(8 * dz + 4 + dx, 1), :] = mass - high

        by_turns(turns, run)
        return 0

    for i in range(4):
        lax.fori_loop(0, 4, lambda dx, _, i=i: panel_step(dx, _, i), 0)
        a_out[i][4 * HALF :, 0:PANEL] = mass_ref[8 * i : 8 * i + 8, :].astype(jnp.bfloat16)
    for i in range(4):
        b_out[i][...] = b_ref[i]


def fold_kernel(*refs):
    a_in, b_in, a_out, b_out = refs[0:4], refs[4:8], refs[8:12], refs[12:16]
    total = sum(ref[4 * HALF :, :].astype(jnp.float32) for ref in a_in)
    mass = total[0:4, :] + total[4:8, :]
    high = mass.astype(jnp.bfloat16).astype(jnp.float32)
    for i in range(4):
        rows = slice(i * HALF, (i + 1) * HALF)
        for ins, outs in ((a_in, a_out), (b_in, b_out)):
            added = sum(ref[rows, :].astype(jnp.float32) for ref in ins)
            outs[i][0:HALF, :] = added.astype(jnp.bfloat16)
        tail = jnp.concatenate(
            [high[i : i + 1], mass[i : i + 1] - high[i : i + 1], jnp.zeros((6, DIM), jnp.float32)],
            axis=0,
        )
        a_out[i][HALF:, :] = tail.astype(jnp.bfloat16)


def finish_kernel(panel_ref, *refs):
    a_in, b_in, out_ref = refs[0:4], refs[4:8], refs[8]
    row = lax.broadcasted_iota(jnp.int32, (PANEL, PANEL), 0)
    lane = lax.broadcasted_iota(jnp.int32, (PANEL, PANEL), 1)
    tail = sum(ref[HALF:, 0:PANEL].astype(jnp.float32) for ref in a_in)
    mass = tail[0:1, :] + tail[1:2, :]
    column = jnp.sum(jnp.where(row == lane, mass, 0.0), axis=1, keepdims=True)
    top = sum(ref[0:HALF, :].astype(jnp.float32) for ref in a_in)
    low = sum(ref[...].astype(jnp.float32) for ref in b_in)
    for h, sums in enumerate((top, low)):
        rows = slice(h * HALF, (h + 1) * HALF)
        panel = panel_ref[rows, :].astype(jnp.float32)
        out_ref[rows, :] = ((sums + panel) / (column[rows] + 1.0)).astype(jnp.bfloat16)


def shards(coarse_cluster_means, fine_cluster_means, block_panel_candidates, softmax_heat):
    y = 2 * lax.axis_index("yh") + lax.axis_index("yl")
    c = lax.axis_index("c")
    z, x = lax.axis_index("z"), lax.axis_index("x")
    here = jnp.stack([y, c, z, x]).astype(jnp.int32)
    once = 1.0 / (softmax_heat * (math.sqrt(DIM) * LN2))
    scale = jnp.concatenate([2.0 * once, once])

    smem = pl.BlockSpec(memory_space=pltpu.SMEM)
    vmem = pl.BlockSpec(memory_space=pltpu.VMEM)

    panel = swapped(fine_cluster_means)
    half_a, half_b = panel[:HALF], panel[HALF:]
    groups = coarse_cluster_means.reshape(4, 8, BLOCK, SLICE)
    own = [lax.dynamic_index_in_dim(groups, (y - d) % 4, 0, keepdims=False) for d in range(4)]
    own[1], own[3] = moved(own[1], Y, 1), moved(own[3], Y, 3)
    stack_a = jnp.stack([half_a] + [moved(half_a, "z", d) for d in (1, 2, 3)])
    stack_b = jnp.stack([half_b] + [moved(half_b, "x", d) for d in (1, 2, 3)])
    mine = swapped(block_panel_candidates)
    stack_a, stack_b, own, mine = lax.optimization_barrier((stack_a, stack_b, own, mine))
    other = moved(mine, "c", 1)
    next_a, last_a = moved(stack_a, "x", 1), moved(stack_a, "x", 3)
    next_b, last_b = moved(stack_b, "z", 1), moved(stack_b, "z", 3)
    own[2] = moved(own[2], Y, 2)
    own, next_a, last_a, next_b, last_b, other = lax.optimization_barrier(
        (own, next_a, last_a, next_b, last_b, other)
    )
    own = jnp.concatenate(own)
    oth = moved(own, "c", 1)
    passed = pl.pallas_call(
        split_kernel,
        in_specs=[vmem] * 4,
        out_specs=[vmem] * 4,
        out_shape=[jax.ShapeDtypeStruct((2, HALF, DIM), jnp.bfloat16)] * 4,
        name="split",
    )(next_a, last_a, next_b, last_b)
    far_a = [moved(passed[0], "x", 1), moved(passed[1], "x", 3)]
    far_b = [moved(passed[2], "z", 1), moved(passed[3], "z", 3)]
    all_a = [stack_a, next_a, *far_a, last_a]
    all_b = [stack_b, next_b, *far_b, last_b]

    cands = jnp.where(c == 0, jnp.stack([mine, other]), jnp.stack([other, mine])).reshape(BLOCKS, 8)
    spot = ((cands % 4 - x) % 4) * 4 + (cands // 4 % 4 - z) % 4
    spot = jnp.where(cands // 16 == c, spot, -1)
    hits = jnp.any(spot[None] == jnp.arange(16, dtype=jnp.int32)[:, None, None], axis=2)
    order = jnp.cumsum(hits.astype(jnp.int32), axis=1) - 1
    count = jnp.sum(hits.astype(jnp.int32), axis=1)
    chosen = (order[:, None, :] == jnp.arange(SLOTS, dtype=jnp.int32)[None, :, None]) & hits[:, None, :]
    table = BLOCKS + jnp.sum(
        jnp.where(chosen, jnp.arange(BLOCKS, dtype=jnp.int32)[None, None, :] - BLOCKS, 0), axis=2
    )
    place = (table // 8 - y) % 4 * 8 + table % 8

    turned = jax.ShapeDtypeStruct((32, SLICE, BLOCK), jnp.bfloat16)
    turn = pl.pallas_call(
        turn_kernel,
        in_specs=[vmem],
        out_specs=vmem,
        out_shape=turned,
        compiler_params=pltpu.CompilerParams(vmem_limit_bytes=16 << 20),
        name="turn",
    )
    power, top, stat = pl.pallas_call(
        score_kernel,
        in_specs=[smem] * 5 + [vmem] * 12,
        out_specs=[vmem] * 3,
        out_shape=[
            jax.ShapeDtypeStruct((16, PANEL, SLOTS * BLOCK), jnp.float32),
            jax.ShapeDtypeStruct((16, 8, SLOTS * BLOCK), jnp.float32),
            jax.ShapeDtypeStruct((2 * STATS, BLOCK), jnp.float32),
        ],
        scratch_shapes=[
            pltpu.VMEM((4, 4, HALF, DIM), jnp.bfloat16),
            pltpu.SemaphoreType.DMA((4, 4)),
        ],
        compiler_params=pltpu.CompilerParams(vmem_limit_bytes=24 << 20),
        name="scores",
    )(here, count, table, place, scale, turn(own), turn(oth), *all_a, *all_b)
    stat_other = moved(stat, "c", 1)

    packs = pl.pallas_call(
        sum_kernel,
        in_specs=[smem] * 4 + [vmem] * 6,
        out_specs=[vmem] * 9,
        out_shape=[jax.ShapeDtypeStruct((PACK, DIM), jnp.bfloat16)] * 4
        + [jax.ShapeDtypeStruct((4 * HALF, DIM), jnp.bfloat16)] * 4
        + [jax.ShapeDtypeStruct((BLOCKS, BLOCK), jnp.float32)],
        scratch_shapes=[
            pltpu.VMEM((4, 4 * HALF, DIM), jnp.bfloat16),
            pltpu.VMEM((STATS, BLOCK), jnp.float32),
            pltpu.VMEM((32, PANEL), jnp.float32),
        ],
        compiler_params=pltpu.CompilerParams(vmem_limit_bytes=24 << 20),
        name="sums",
    )(here, count, table, place, own, oth, power, top, stat, stat_other)
    pack_a, pack_b, norm = packs[0:4], packs[4:8], packs[8]

    got_a, got_b = [pack_a[0]] * 4, [pack_b[0]] * 4
    for d in (1, 3, 2):
        got_a[d] = moved(pack_a[d], "z", -d)
        got_b[d] = moved(pack_b[d], "x", -d)
    parts = pl.pallas_call(
        fold_kernel,
        in_specs=[vmem] * 8,
        out_specs=[vmem] * 8,
        out_shape=[jax.ShapeDtypeStruct((CHUNK, DIM), jnp.bfloat16)] * 4
        + [jax.ShapeDtypeStruct((HALF, DIM), jnp.bfloat16)] * 4,
        compiler_params=pltpu.CompilerParams(vmem_limit_bytes=16 << 20),
        name="fold",
    )(*got_a, *got_b)
    part_a, part_b = parts[0:4], parts[4:8]
    last_a, last_b = [part_a[0]] * 4, [part_b[0]] * 4
    for d in (1, 3, 2):
        last_a[d] = moved(part_a[d], "x", -d)
        last_b[d] = moved(part_b[d], "z", -d)
    revised = pl.pallas_call(
        finish_kernel,
        in_specs=[vmem] * 9,
        out_specs=vmem,
        out_shape=jax.ShapeDtypeStruct((PANEL, DIM), jnp.bfloat16),
        name="finish",
    )(panel, *last_a, *last_b)
    norm, revised = lax.optimization_barrier((norm, revised))
    part_norm = lax.dynamic_slice_in_dim(norm, c * 8, 8, axis=0)
    return (swapped(revised), swapped(part_norm).reshape(8 * BLOCK))


def solution(mesh):
    split = Mesh(mesh.devices.reshape(2, 2, 2, 4, 4), ("yh", "c", "yl", "z", "x"))
    blk, row = ("yl", "z", "x"), ("yh", "c")
    return jax.shard_map(
        shards,
        mesh=split,
        in_specs=(P(blk, row), P(blk + row, None), P(blk + row, None), P()),
        out_specs=(P(blk + row, None), P(blk + row)),
        check_vma=False,
    )
```

time: 1100 us -> 148 us (0.13)
  the two profiles are of different devices: /device:TPU:16 before, /device:TPU:1 now
where the time goes in v2:
time: 148 us; the launch traced here: 147 us
  starting transfers between devices  61.6 us (42%)
  waiting for transfers between devices  47.3 us (32%)
  Pallas kernels  28.8 us (19%)
  local copies, waits for them, and re-layouts  6.81 us (5%)
  between operations  1.76 us (1%)
    ppermute x32, starting transfers between devices, moved(): lax.ppermute(value, axis, [(i, (i - by) % size) for i in range(size)])  45.6 us
    ppermute x32, waiting for transfers between devices, moved(): lax.ppermute(value, axis, [(i, (i - by) % size) for i in range(size)])  44.3 us
    ppermute x4, starting transfers between devices, swapped(): return lax.ppermute(value, ('c', 'yl'), [(0, 0), (1, 2), (2, 1), (3, 3)])  16 us
    pallas_call x1, Pallas kernels, shards(): pl.pallas_call(score_kernel, in_specs=[smem] * 5 + [vmem] * 12, out_specs...  12.1 us
    pallas_call x1, Pallas kernels, shards(): pl.pallas_call(sum_kernel, in_specs=[smem] * 4 + [vmem] * 6, out_specs=[v...  7.68 us
    unnamed x37, local copies, waits for them, and re-layouts  4.99 us
    ppermute x4, waiting for transfers between devices, swapped(): return lax.ppermute(value, ('c', 'yl'), [(0, 0), (1, 2), (2, 1), (3, 3)])  3.01 us
  transfers between devices with their start and end apart: 36, of which 15 were waited for; matrix products, arithmetic and copies ran while one was open for 2% of the time, Pallas kernels for 4%

profile of v2, /device:TPU:1, one launch (start us, length us, event | category | flops | bytes accessed | tf_op | source)
XLA Modules:
  0.0 147.4 jit_solution(10940722313771097448)
XLA Ops:
  0.6 4.6 %collective-permute-start = (bf16[128,1024]{1,0:T(8,128)(2,1)}, bf16[128,1024]{1,0:T(8,128)(2,1)S(1)}, u32[]{:S(2)}, u32[]{:S(2)}) collective-permute-start(bf16[128,1024]{1,0:T(8,128)(2,1)} %param.5), channel_id=1, source_target_pairs={{0,0},{16,32},{32,16},{48,48},{1,1},{17,33},{33,17},{49,49},{2,2},... | collective-permute-start | bytes 786440 | tf_op jit(solution)/shard_map/ppermute | solution.py:32
  5.3 1.7 %dynamic-slice_bitcast_fusion = (bf16[8,128,256]{2,1,0:T(8,128)(2,1)S(1)}, bf16[8,128,256]{2,1,0:T(8,128)(2,1)S(1)}, bf16[8,128,256]{2,1,0:T(8,128)(2,1)S(1)}, bf16[8,128,256]{2,1,0:T(8,128)(2,1)S(1)}) fusion(bf16[4,8,128,256]{3,2,1,0:T(8,128)(2,1)} %bitcast.30, s32[]{:T(128)S(6)} %select_n.132, s32[]{:T(128)S(6)} %select_n.130, s32[]{:T(128)S(6)} %select_n.128, ...), kind=kLoop, calls=%fused_computation.2 | loop fusion | bytes 4194320 | tf_op jit(solution)/shard_map/jit(dynamic_index_in_dim)/squeeze | solution.py:248
  7.1 2.7 %collective-permute-start.7 = (bf16[8,128,256]{2,1,0:T(8,128)(2,1)S(1)}, bf16[8,128,256]{2,1,0:T(8,128)(2,1)S(1)}, u32[]{:S(2)}, u32[]{:S(2)}) collective-permute-start(bf16[8,128,256]{2,1,0:T(8,128)(2,1)S(1)} %get-tuple-element.88), channel_id=1, source_target_pairs={{0,80},{16,0},{64,16},{80,64},{1,81},{17,1},{65,17},{81,65},{2,82}... | collective-permute-start | bytes 1572872 | tf_op jit(solution)/shard_map/ppermute | solution.py:28
  9.8 2.8 %collective-permute-start.5 = (bf16[64,1024]{1,0:T(8,128)(2,1)S(1)}, bf16[64,1024]{1,0:T(8,128)(2,1)S(1)}, u32[]{:S(2)}, u32[]{:S(2)}) collective-permute-start(bf16[64,1024]{1,0:T(8,128)(2,1)S(1)} %get-tuple-element.92), channel_id=1, source_target_pairs={{0,2},{1,3},{2,0},{3,1},{4,6},{5,7},{6,4},{7,5},{8,10},{9,11},{10,... | collective-permute-start | bytes 393224 | tf_op jit(solution)/shard_map/ppermute | solution.py:28
  12.6 0.9 collective-permute-start.4
  13.5 0.6 collective-permute-start.6
  14.1 2.6 %collective-permute-done.5 = bf16[64,1024]{1,0:T(8,128)(2,1)S(1)} collective-permute-done((bf16[64,1024]{1,0:T(8,128)(2,1)S(1)}, bf16[64,1024]{1,0:T(8,128)(2,1)S(1)}, u32[]{:S(2)}, u32[]{:S(2)}) %collective-permute-start.5) | collective-permute-done | bytes 131104 | tf_op jit(solution)/shard_map/ppermute | solution.py:28
  16.7 3.6 %collective-permute-start.2 = (bf16[64,1024]{1,0:T(8,128)(2,1)S(1)}, bf16[64,1024]{1,0:T(8,128)(2,1)S(1)}, u32[]{:S(2)}, u32[]{:S(2)}) collective-permute-start(bf16[64,1024]{1,0:T(8,128)(2,1)S(1)} %get-tuple-element.93), channel_id=1, source_target_pairs={{0,8},{4,12},{8,0},{12,4},{1,9},{5,13},{9,1},{13,5},{2,10},{6,14},... | collective-permute-start | bytes 393224 | tf_op jit(solution)/shard_map/ppermute | solution.py:28
  20.3 3.2 %collective-permute-start.1 = (bf16[64,1024]{1,0:T(8,128)(2,1)S(1)}, bf16[64,1024]{1,0:T(8,128)(2,1)S(1)}, u32[]{:S(2)}, u32[]{:S(2)}) collective-permute-start(bf16[64,1024]{1,0:T(8,128)(2,1)S(1)} %get-tuple-element.93), channel_id=1, source_target_pairs={{0,12},{4,0},{8,4},{12,8},{1,13},{5,1},{9,5},{13,9},{2,14},{6,2},{... | collective-permute-start | bytes 393224 | tf_op jit(solution)/shard_map/ppermute | solution.py:28
  23.5 0.3 collective-permute-done.2
  23.8 3.8 %collective-permute-start.9 = (s32[8,8]{1,0:T(8,128)S(1)}, s32[8,8]{1,0:T(8,128)S(1)}, u32[]{:S(2)}, u32[]{:S(2)}) collective-permute-start(s32[8,8]{1,0:T(8,128)S(1)} %copy-done.15), channel_id=1, source_target_pairs={{0,0},{16,32},{32,16},{48,48},{1,1},{17,33},{33,17},{49,49},{2,2},... | collective-permute-start | bytes 776 | tf_op jit(solution)/shard_map/ppermute | solution.py:32
  27.6 1.5 %collective-permute-done.3 = bf16[64,1024]{1,0:T(8,128)(2,1)S(1)} collective-permute-done((bf16[64,1024]{1,0:T(8,128)(2,1)S(1)}, bf16[64,1024]{1,0:T(8,128)(2,1)S(1)}, u32[]{:S(2)}, u32[]{:S(2)}) %collective-permute-start.3) | collective-permute-done | bytes 131104 | tf_op jit(solution)/shard_map/ppermute | solution.py:28
  29.3 1.5 %collective-permute-start.15 = (s32[8,8]{1,0:T(8,128)S(1)}, s32[8,8]{1,0:T(8,128)S(1)}, u32[]{:S(2)}, u32[]{:S(2)}) collective-permute-start(s32[8,8]{1,0:T(8,128)S(1)} %collective-permute-done.9), channel_id=1, source_target_pairs={{0,32},{32,0},{1,33},{33,1},{2,34},{34,2},{3,35},{35,3},{4,36},{36... | collective-permute-start | bytes 776 | tf_op jit(solution)/shard_map/ppermute | solution.py:28
  30.8 1.1 collective-permute-start.12
  31.9 1.6 %collective-permute-start.11 = (bf16[4,64,1024]{2,1,0:T(8,128)(2,1)S(1)}, bf16[4,64,1024]{2,1,0:T(8,128)(2,1)S(1)}, u32[]{:S(2)}, u32[]{:S(2)}) collective-permute-start(bf16[4,64,1024]{2,1,0:T(8,128)(2,1)S(1)} %pad_maximum_fusion.refs_0_), channel_id=1, source_target_pairs={{0,3},{1,0},{2,1},{3,2},{4,7},{5,4},{6,5},{7,6},{8,11},{9,8},{10,9... | collective-permute-start | bytes 1572872 | tf_op jit(solution)/shard_map/ppermute | solution.py:28
  33.5 0.7 collective-permute-start.10
  34.1 0.8 collective-permute-start.14
  35.0 2.2 %collective-permute-start.13 = (bf16[4,64,1024]{2,1,0:T(8,128)(2,1)S(1)}, bf16[4,64,1024]{2,1,0:T(8,128)(2,1)}, u32[]{:S(2)}, u32[]{:S(2)}) collective-permute-start(bf16[4,64,1024]{2,1,0:T(8,128)(2,1)S(1)} %pad_maximum_fusion.1.refs_5_), channel_id=1, source_target_pairs={{0,12},{4,0},{8,4},{12,8},{1,13},{5,1},{9,5},{13,9},{2,14},{6,2},{... | collective-permute-start | bytes 1572872 | tf_op jit(solution)/shard_map/ppermute | solution.py:28
  37.2 10.6 %collective-permute-done.10 = bf16[8,128,256]{2,1,0:T(8,128)(2,1)S(1)} collective-permute-done((bf16[8,128,256]{2,1,0:T(8,128)(2,1)S(1)}, bf16[8,128,256]{2,1,0:T(8,128)(2,1)S(1)}, u32[]{:S(2)}, u32[]{:S(2)}) %collective-permute-start.10) | collective-permute-done | bytes 524320 | tf_op jit(solution)/shard_map/ppermute | solution.py:28
  47.8 0.3 collective-permute-done.14.refs_3_.refs_9_
  48.1 0.5 copy-done
  48.6 0.2 copy-done.2
  48.8 0.8 copy-done.4
  49.8 1.6 %collective-permute-start.16 = (bf16[32,128,256]{2,1,0:T(8,128)(2,1)S(1)}, bf16[32,128,256]{2,1,0:T(8,128)(2,1)}, u32[]{:S(2)}, u32[]{:S(2)}) collective-permute-start(bf16[32,128,256]{2,1,0:T(8,128)(2,1)S(1)} %constant_dynamic-update-slice_fusion.ref.own), channel_id=1, source_target_pairs={{0,32},{32,0},{1,33},{33,1},{2,34},{34,2},{3,35},{35,3},{4,36},{36... | collective-permute-start | bytes 6291464 | tf_op jit(solution)/shard_map/ppermute | solution.py:28
  52.6 2.6 %split.1 = (bf16[2,64,1024]{2,1,0:T(8,128)(2,1)}, bf16[2,64,1024]{2,1,0:T(8,128)(2,1)}, bf16[2,64,1024]{2,1,0:T(8,128)(2,1)}, bf16[2,64,1024]{2,1,0:T(8,128)(2,1)}) custom-call(bf16[4,64,1024]{2,1,0:T(8,128)(2,1)} %copy-done.2, bf16[4,64,1024]{2,1,0:T(8,128)(2,1)} %copy-done, bf16[4,64,1024]{2,1,0:T(8,128)(2,1)} %collective-permute-done.13.refs_2_.refs_6_, ...), custom_call_target="tpu_custom_call" | custom-call | tf_op jit(solution)/shard_map/split/pallas_call | solution.py:263
  55.1 1.1 collective-permute-start.17
  56.3 0.3 collective-permute-start.18
  56.6 1.7 %collective-permute-start.19 = (bf16[2,64,1024]{2,1,0:T(8,128)(2,1)}, bf16[2,64,1024]{2,1,0:T(8,128)(2,1)S(1)}, u32[]{:S(2)}, u32[]{:S(2)}) collective-permute-start(bf16[2,64,1024]{2,1,0:T(8,128)(2,1)} %get-tuple-element.62), channel_id=1, source_target_pairs={{0,12},{4,0},{8,4},{12,8},{1,13},{5,1},{9,5},{13,9},{2,14},{6,2},{... | collective-permute-start | bytes 786440 | tf_op jit(solution)/shard_map/ppermute | solution.py:28
  58.3 0.4 select_reduce_fusion
  58.8 1.0 turn.2.own
  59.8 2.7 %turn.3.oth = bf16[32,256,128]{2,1,0:T(8,128)(2,1)S(1)} custom-call(bf16[32,128,256]{2,1,0:T(8,128)(2,1)} %collective-permute-done.16.ref.oth), custom_call_target="tpu_custom_call" | custom-call | tf_op jit(solution)/shard_map/turn/pallas_call | solution.py:311
  62.5 0.7 collective-permute-done.17.refs_2_
  63.3 2.0 %collective-permute-done.18.refs_3_ = bf16[2,64,1024]{2,1,0:T(8,128)(2,1)S(1)} collective-permute-done((bf16[2,64,1024]{2,1,0:T(8,128)(2,1)}, bf16[2,64,1024]{2,1,0:T(8,128)(2,1)S(1)}, u32[]{:S(2)}, u32[]{:S(2)}) %collective-permute-start.18) | collective-permute-done | bytes 262176 | tf_op jit(solution)/shard_map/ppermute | solution.py:28
  65.3 1.4 collective-permute-done.20.refs_8_
  66.7 12.1 %scores.1 = (f32[16,128,1024]{2,1,0:T(8,128)S(1)}, f32[16,8,1024]{2,1,0:T(8,128)S(1)}, f32[48,128]{1,0:T(8,128)S(1)}) custom-call(s32[4]{0:T(128)S(1)} %pad_add_fusion.here_ref, s32[16]{0:T(128)S(1)} %convert_reduce_fusion.count_ref, s32[16,8]{1,0:T(8,128)S(1)} %get-tuple-element.95.list_ref, s32[16,8]{1,0:T(8,128)S(1)} %get-tuple-element.94.place_ref, ...), custom_call_target="tpu_custom_call" | custom-call | tf_op jit(solution)/shard_map/scores/pallas_call | solution.py:296
  78.8 2.1 %collective-permute-start.21 = (f32[48,128]{1,0:T(8,128)S(1)}, f32[48,128]{1,0:T(8,128)S(1)}, u32[]{:S(2)}, u32[]{:S(2)}) collective-permute-start(f32[48,128]{1,0:T(8,128)S(1)} %get-tuple-element.66.mine_ref), channel_id=1, source_target_pairs={{0,32},{32,0},{1,33},{33,1},{2,34},{34,2},{3,35},{35,3},{4,36},{36... | collective-permute-start | bytes 73736 | tf_op jit(solution)/shard_map/ppermute | solution.py:28
  80.9 0.8 collective-permute-done.21.other_ref
  81.7 7.7 %sums.1 = (bf16[264,1024]{1,0:T(8,128)(2,1)S(1)}, bf16[264,1024]{1,0:T(8,128)(2,1)S(1)}, bf16[264,1024]{1,0:T(8,128)(2,1)S(1)}, bf16[264,1024]{1,0:T(8,128)(2,1)...) custom-call(s32[4]{0:T(128)S(1)} %pad_add_fusion.here_ref, ...), custom_call_target="tpu_custom_call" | custom-call | tf_op jit(solution)/shard_map/sums/pallas_call | solution.py:314
  89.4 0.3 collective-permute-start.25
  89.7 1.2 collective-permute-start.23
  90.9 1.5 collective-permute-start.24
  92.4 3.6 %collective-permute-start.26 = (bf16[256,1024]{1,0:T(8,128)(2,1)S(1)}, bf16[256,1024]{1,0:T(8,128)(2,1)S(1)}, u32[]{:S(2)}, u32[]{:S(2)}) collective-permute-start(bf16[256,1024]{1,0:T(8,128)(2,1)S(1)} %get-tuple-element.74), channel_id=1, source_target_pairs={{0,2},{1,3},{2,0},{3,1},{4,6},{5,7},{6,4},{7,5},{8,10},{9,11},{10,... | collective-permute-start | bytes 1572872 | tf_op jit(solution)/shard_map/ppermute | solution.py:28
  96.0 7.8 %collective-permute-done.25.refs_5_ = bf16[256,1024]{1,0:T(8,128)(2,1)S(1)} collective-permute-done((bf16[256,1024]{1,0:T(8,128)(2,1)S(1)}, bf16[256,1024]{1,0:T(8,128)(2,1)S(1)}, u32[]{:S(2)}, u32[]{:S(2)}) %collective-permute-start.25) | collective-permute-done | bytes 524320 | tf_op jit(solution)/shard_map/ppermute | solution.py:28
  103.8 1.2 collective-permute-start.27
  105.1 11.0 %collective-permute-done.26.refs_6_ = bf16[256,1024]{1,0:T(8,128)(2,1)S(1)} collective-permute-done((bf16[256,1024]{1,0:T(8,128)(2,1)S(1)}, bf16[256,1024]{1,0:T(8,128)(2,1)S(1)}, u32[]{:S(2)}, u32[]{:S(2)}) %collective-permute-start.26) | collective-permute-done | bytes 524320 | tf_op jit(solution)/shard_map/ppermute | solution.py:28
  116.0 1.8 %collective-permute-done.27.refs_7_ = bf16[256,1024]{1,0:T(8,128)(2,1)S(1)} collective-permute-done((bf16[256,1024]{1,0:T(8,128)(2,1)S(1)}, bf16[256,1024]{1,0:T(8,128)(2,1)S(1)}, u32[]{:S(2)}, u32[]{:S(2)}) %collective-permute-start.27) | collective-permute-done | bytes 524320 | tf_op jit(solution)/shard_map/ppermute | solution.py:28
  117.8 0.5 fold.1
  118.4 0.7 copy-done.6
  119.1 0.6 copy-done.7
  119.7 0.2 collective-permute-start.31
  120.0 2.5 %collective-permute-start.28 = (bf16[72,1024]{1,0:T(8,128)(2,1)S(1)}, bf16[72,1024]{1,0:T(8,128)(2,1)S(1)}, u32[]{:S(2)}, u32[]{:S(2)}) collective-permute-start(bf16[72,1024]{1,0:T(8,128)(2,1)S(1)} %get-tuple-element.77), channel_id=1, source_target_pairs={{0,1},{1,2},{2,3},{3,0},{4,5},{5,6},{6,7},{7,4},{8,9},{9,10},{10,1... | collective-permute-start | bytes 442376 | tf_op jit(solution)/shard_map/ppermute | solution.py:28
  122.5 2.1 %collective-permute-start.29 = (bf16[72,1024]{1,0:T(8,128)(2,1)S(1)}, bf16[72,1024]{1,0:T(8,128)(2,1)S(1)}, u32[]{:S(2)}, u32[]{:S(2)}) collective-permute-start(bf16[72,1024]{1,0:T(8,128)(2,1)S(1)} %get-tuple-element.78), channel_id=1, source_target_pairs={{0,2},{1,3},{2,0},{3,1},{4,6},{5,7},{6,4},{7,5},{8,10},{9,11},{10,... | collective-permute-start | bytes 442376 | tf_op jit(solution)/shard_map/ppermute | solution.py:28
  124.5 0.3 collective-permute-start.30
  124.9 2.9 %collective-permute-start.32 = (bf16[64,1024]{1,0:T(8,128)(2,1)S(1)}, bf16[64,1024]{1,0:T(8,128)(2,1)S(1)}, u32[]{:S(2)}, u32[]{:S(2)}) collective-permute-start(bf16[64,1024]{1,0:T(8,128)(2,1)S(1)} %get-tuple-element.82), channel_id=1, source_target_pairs={{0,8},{4,12},{8,0},{12,4},{1,9},{5,13},{9,1},{13,5},{2,10},{6,14},... | collective-permute-start | bytes 393224 | tf_op jit(solution)/shard_map/ppermute | solution.py:28
  127.7 1.2 collective-permute-start.33
  129.0 1.2 collective-permute-done.32.refs_6_
  130.2 2.1 %collective-permute-done.33.refs_7_ = bf16[64,1024]{1,0:T(8,128)(2,1)S(1)} collective-permute-done((bf16[64,1024]{1,0:T(8,128)(2,1)S(1)}, bf16[64,1024]{1,0:T(8,128)(2,1)S(1)}, u32[]{:S(2)}, u32[]{:S(2)}) %collective-permute-start.33) | collective-permute-done | bytes 131104 | tf_op jit(solution)/shard_map/ppermute | solution.py:28
  132.4 0.6 copy-done.14
  133.1 2.3 %finish.1 = bf16[128,1024]{1,0:T(8,128)(2,1)} custom-call(bf16[128,1024]{1,0:T(8,128)(2,1)} %copy-done.8, bf16[72,1024]{1,0:T(8,128)(2,1)} %copy-done.6, bf16[72,1024]{1,0:T(8,128)(2,1)} %copy-done.9, bf16[72,1024]{1,0:T(8,128)(2,1)} %copy-done.10, bf16[72,1024]{1,0:T(8,128)(2,1)} %copy-done.11, bf16[64,1024]{1,0:T(8,128)(2,1)} %copy-done.7, ...), custom_call_target="tpu_custom_call" | custom-call | tf_op jit(solution)/shard_map/finish/pallas_call | solution.py:349
  135.4 5.7 %collective-permute-start.34 = (bf16[128,1024]{1,0:T(8,128)(2,1)}, bf16[128,1024]{1,0:T(8,128)(2,1)S(1)}, u32[]{:S(2)}, u32[]{:S(2)}) collective-permute-start(bf16[128,1024]{1,0:T(8,128)(2,1)} %finish.1), channel_id=1, source_target_pairs={{0,0},{16,32},{32,16},{48,48},{1,1},{17,33},{33,17},{49,49},{2,2},... | collective-permute-start | bytes 786440 | tf_op jit(solution)/shard_map/ppermute | solution.py:32
  141.1 1.9 %collective-permute-start.35 = (f32[8,128]{1,0:T(8,128)S(1)}, f32[8,128]{1,0:T(8,128)S(1)}, u32[]{:S(2)}, u32[]{:S(2)}) collective-permute-start(f32[8,128]{1,0:T(8,128)S(1)} %constant_dynamic-slice_fusion), channel_id=1, source_target_pairs={{0,0},{16,32},{32,16},{48,48},{1,1},{17,33},{33,17},{49,49},{2,2},... | collective-permute-start | bytes 12296 | tf_op jit(solution)/shard_map/ppermute | solution.py:32
  143.1 3.0 %collective-permute-done.35 = f32[8,128]{1,0:T(8,128)S(1)} collective-permute-done((f32[8,128]{1,0:T(8,128)S(1)}, f32[8,128]{1,0:T(8,128)S(1)}, u32[]{:S(2)}, u32[]{:S(2)}) %collective-permute-start.35) | collective-permute-done | bytes 4128 | tf_op jit(solution)/shard_map/ppermute | solution.py:32
  146.1 0.7 copy.24
  146.8 0.6 copy.25
  (70 shorter events, 1.3 us)
Async XLA Ops:
  0.6 9.1 %collective-permute-start = (bf16[128,1024]{1,0:T(8,128)(2,1)}, bf16[128,1024]{1,0:T(8,128)(2,1)S(1)}, u32[]{:S(2)}, u32[]{:S(2)}) collective-permute-start(bf16[128,1024]{1,0:T(8,128)(2,1)} %param.5), channel_id=1, source_target_pairs={{0,0},{16,32},{32,16},{48,48},{1,1},{17,33},{33,17},{49,49},{2,2},... | collective-permute-start | bytes 786440 | tf_op jit(solution)/shard_map/ppermute | solution.py:32
  5.3 18.5 %copy-start.15 = (s32[8,8]{1,0:T(8,128)S(1)}, s32[8,8]{1,0:T(8,128)}, u32[]{:S(2)}) copy-start(s32[8,8]{1,0:T(8,128)} %param.6) | copy-start | bytes 772
  7.0 22.3 %collective-permute-start.8 = (bf16[8,128,256]{2,1,0:T(8,128)(2,1)S(1)}, bf16[8,128,256]{2,1,0:T(8,128)(2,1)S(1)}, u32[]{:S(2)}, u32[]{:S(2)}) collective-permute-start(bf16[8,128,256]{2,1,0:T(8,128)(2,1)S(1)} %get-tuple-element.86), channel_id=1, source_target_pairs={{0,16},{16,64},{64,80},{80,0},{1,17},{17,65},{65,81},{81,1},{2,18}... | collective-permute-start | bytes 1572872 | tf_op jit(solution)/shard_map/ppermute | solution.py:28
  7.1 22.2 %collective-permute-start.7 = (bf16[8,128,256]{2,1,0:T(8,128)(2,1)S(1)}, bf16[8,128,256]{2,1,0:T(8,128)(2,1)S(1)}, u32[]{:S(2)}, u32[]{:S(2)}) collective-permute-start(bf16[8,128,256]{2,1,0:T(8,128)(2,1)S(1)} %get-tuple-element.88), channel_id=1, source_target_pairs={{0,80},{16,0},{64,16},{80,64},{1,81},{17,1},{65,17},{81,65},{2,82}... | collective-permute-start | bytes 1572872 | tf_op jit(solution)/shard_map/ppermute | solution.py:28
  9.7 40.0 %copy-start.8 = (bf16[128,1024]{1,0:T(8,128)(2,1)}, bf16[128,1024]{1,0:T(8,128)(2,1)S(1)}, u32[]{:S(2)}) copy-start(bf16[128,1024]{1,0:T(8,128)(2,1)S(1)} %collective-permute-done.panel_ref) | copy-start | bytes 786436
  9.8 6.9 %collective-permute-start.5 = (bf16[64,1024]{1,0:T(8,128)(2,1)S(1)}, bf16[64,1024]{1,0:T(8,128)(2,1)S(1)}, u32[]{:S(2)}, u32[]{:S(2)}) collective-permute-start(bf16[64,1024]{1,0:T(8,128)(2,1)S(1)} %get-tuple-element.92), channel_id=1, source_target_pairs={{0,2},{1,3},{2,0},{3,1},{4,6},{5,7},{6,4},{7,5},{8,10},{9,11},{10,... | collective-permute-start | bytes 393224 | tf_op jit(solution)/shard_map/ppermute | solution.py:28
  12.6 7.6 %collective-permute-start.4 = (bf16[64,1024]{1,0:T(8,128)(2,1)S(1)}, bf16[64,1024]{1,0:T(8,128)(2,1)S(1)}, u32[]{:S(2)}, u32[]{:S(2)}) collective-permute-start(bf16[64,1024]{1,0:T(8,128)(2,1)S(1)} %get-tuple-element.92), channel_id=1, source_target_pairs={{0,3},{1,0},{2,1},{3,2},{4,7},{5,4},{6,5},{7,6},{8,11},{9,8},{10,9... | collective-permute-start | bytes 393224 | tf_op jit(solution)/shard_map/ppermute | solution.py:28
  13.5 10.0 %collective-permute-start.6 = (bf16[64,1024]{1,0:T(8,128)(2,1)S(1)}, bf16[64,1024]{1,0:T(8,128)(2,1)S(1)}, u32[]{:S(2)}, u32[]{:S(2)}) collective-permute-start(bf16[64,1024]{1,0:T(8,128)(2,1)S(1)} %get-tuple-element.92), channel_id=1, source_target_pairs={{0,1},{1,2},{2,3},{3,0},{4,5},{5,6},{6,7},{7,4},{8,9},{9,10},{10,1... | collective-permute-start | bytes 393224 | tf_op jit(solution)/shard_map/ppermute | solution.py:28
  16.7 7.1 %collective-permute-start.2 = (bf16[64,1024]{1,0:T(8,128)(2,1)S(1)}, bf16[64,1024]{1,0:T(8,128)(2,1)S(1)}, u32[]{:S(2)}, u32[]{:S(2)}) collective-permute-start(bf16[64,1024]{1,0:T(8,128)(2,1)S(1)} %get-tuple-element.93), channel_id=1, source_target_pairs={{0,8},{4,12},{8,0},{12,4},{1,9},{5,13},{9,1},{13,5},{2,10},{6,14},... | collective-permute-start | bytes 393224 | tf_op jit(solution)/shard_map/ppermute | solution.py:28
  20.3 7.4 %collective-permute-start.1 = (bf16[64,1024]{1,0:T(8,128)(2,1)S(1)}, bf16[64,1024]{1,0:T(8,128)(2,1)S(1)}, u32[]{:S(2)}, u32[]{:S(2)}) collective-permute-start(bf16[64,1024]{1,0:T(8,128)(2,1)S(1)} %get-tuple-element.93), channel_id=1, source_target_pairs={{0,12},{4,0},{8,4},{12,8},{1,13},{5,1},{9,5},{13,9},{2,14},{6,2},{... | collective-permute-start | bytes 393224 | tf_op jit(solution)/shard_map/ppermute | solution.py:28
  23.5 5.7 %collective-permute-start.3 = (bf16[64,1024]{1,0:T(8,128)(2,1)S(1)}, bf16[64,1024]{1,0:T(8,128)(2,1)S(1)}, u32[]{:S(2)}, u32[]{:S(2)}) collective-permute-start(bf16[64,1024]{1,0:T(8,128)(2,1)S(1)} %get-tuple-element.93), channel_id=1, source_target_pairs={{0,4},{4,8},{8,12},{12,0},{1,5},{5,9},{9,13},{13,1},{2,6},{6,10},{... | collective-permute-start | bytes 393224 | tf_op jit(solution)/shard_map/ppermute | solution.py:28
  23.8 5.5 %collective-permute-start.9 = (s32[8,8]{1,0:T(8,128)S(1)}, s32[8,8]{1,0:T(8,128)S(1)}, u32[]{:S(2)}, u32[]{:S(2)}) collective-permute-start(s32[8,8]{1,0:T(8,128)S(1)} %copy-done.15), channel_id=1, source_target_pairs={{0,0},{16,32},{32,16},{48,48},{1,1},{17,33},{33,17},{49,49},{2,2},... | collective-permute-start | bytes 776 | tf_op jit(solution)/shard_map/ppermute | solution.py:32
  29.3 5.7 %collective-permute-start.15 = (s32[8,8]{1,0:T(8,128)S(1)}, s32[8,8]{1,0:T(8,128)S(1)}, u32[]{:S(2)}, u32[]{:S(2)}) collective-permute-start(s32[8,8]{1,0:T(8,128)S(1)} %collective-permute-done.9), channel_id=1, source_target_pairs={{0,32},{32,0},{1,33},{33,1},{2,34},{34,2},{3,35},{35,3},{4,36},{36... | collective-permute-start | bytes 776 | tf_op jit(solution)/shard_map/ppermute | solution.py:28
  30.8 17.0 %collective-permute-start.12 = (bf16[4,64,1024]{2,1,0:T(8,128)(2,1)S(1)}, bf16[4,64,1024]{2,1,0:T(8,128)(2,1)S(1)}, u32[]{:S(2)}, u32[]{:S(2)}) collective-permute-start(bf16[4,64,1024]{2,1,0:T(8,128)(2,1)S(1)} %pad_maximum_fusion.refs_0_), channel_id=1, source_target_pairs={{0,1},{1,2},{2,3},{3,0},{4,5},{5,6},{6,7},{7,4},{8,9},{9,10},{10,1... | collective-permute-start | bytes 1572872 | tf_op jit(solution)/shard_map/ppermute | solution.py:28
  31.9 15.9 %collective-permute-start.11 = (bf16[4,64,1024]{2,1,0:T(8,128)(2,1)S(1)}, bf16[4,64,1024]{2,1,0:T(8,128)(2,1)S(1)}, u32[]{:S(2)}, u32[]{:S(2)}) collective-permute-start(bf16[4,64,1024]{2,1,0:T(8,128)(2,1)S(1)} %pad_maximum_fusion.refs_0_), channel_id=1, source_target_pairs={{0,3},{1,0},{2,1},{3,2},{4,7},{5,4},{6,5},{7,6},{8,11},{9,8},{10,9... | collective-permute-start | bytes 1572872 | tf_op jit(solution)/shard_map/ppermute | solution.py:28
  33.5 14.3 %collective-permute-start.10 = (bf16[8,128,256]{2,1,0:T(8,128)(2,1)S(1)}, bf16[8,128,256]{2,1,0:T(8,128)(2,1)S(1)}, u32[]{:S(2)}, u32[]{:S(2)}) collective-permute-start(bf16[8,128,256]{2,1,0:T(8,128)(2,1)S(1)} %get-tuple-element.47), channel_id=1, source_target_pairs={{0,64},{16,80},{64,0},{80,16},{1,65},{17,81},{65,1},{81,17},{2,66}... | collective-permute-start | bytes 1572872 | tf_op jit(solution)/shard_map/ppermute | solution.py:28
  34.1 14.0 %collective-permute-start.14 = (bf16[4,64,1024]{2,1,0:T(8,128)(2,1)S(1)}, bf16[4,64,1024]{2,1,0:T(8,128)(2,1)S(1)}, u32[]{:S(2)}, u32[]{:S(2)}) collective-permute-start(bf16[4,64,1024]{2,1,0:T(8,128)(2,1)S(1)} %pad_maximum_fusion.1.refs_5_), channel_id=1, source_target_pairs={{0,4},{4,8},{8,12},{12,0},{1,5},{5,9},{9,13},{13,1},{2,6},{6,10},{... | collective-permute-start | bytes 1572872 | tf_op jit(solution)/shard_map/ppermute | solution.py:28
  35.0 14.7 %collective-permute-start.13 = (bf16[4,64,1024]{2,1,0:T(8,128)(2,1)S(1)}, bf16[4,64,1024]{2,1,0:T(8,128)(2,1)}, u32[]{:S(2)}, u32[]{:S(2)}) collective-permute-start(bf16[4,64,1024]{2,1,0:T(8,128)(2,1)S(1)} %pad_maximum_fusion.1.refs_5_), channel_id=1, source_target_pairs={{0,12},{4,0},{8,4},{12,8},{1,13},{5,1},{9,5},{13,9},{2,14},{6,2},{... | collective-permute-start | bytes 1572872 | tf_op jit(solution)/shard_map/ppermute | solution.py:28
  47.8 0.8 copy-start
  47.8 1.0 copy-start.2
  48.8 0.8 copy-start.4
  49.8 10.0 %collective-permute-start.16 = (bf16[32,128,256]{2,1,0:T(8,128)(2,1)S(1)}, bf16[32,128,256]{2,1,0:T(8,128)(2,1)}, u32[]{:S(2)}, u32[]{:S(2)}) collective-permute-start(bf16[32,128,256]{2,1,0:T(8,128)(2,1)S(1)} %constant_dynamic-update-slice_fusion.ref.own), channel_id=1, source_target_pairs={{0,32},{32,0},{1,33},{33,1},{2,34},{34,2},{3,35},{35,3},{4,36},{36... | collective-permute-start | bytes 6291464 | tf_op jit(solution)/shard_map/ppermute | solution.py:28
  55.1 8.1 %collective-permute-start.17 = (bf16[2,64,1024]{2,1,0:T(8,128)(2,1)}, bf16[2,64,1024]{2,1,0:T(8,128)(2,1)S(1)}, u32[]{:S(2)}, u32[]{:S(2)}) collective-permute-start(bf16[2,64,1024]{2,1,0:T(8,128)(2,1)} %get-tuple-element.60), channel_id=1, source_target_pairs={{0,3},{1,0},{2,1},{3,2},{4,7},{5,4},{6,5},{7,6},{8,11},{9,8},{10,9... | collective-permute-start | bytes 786440 | tf_op jit(solution)/shard_map/ppermute | solution.py:28
  56.3 9.0 %collective-permute-start.18 = (bf16[2,64,1024]{2,1,0:T(8,128)(2,1)}, bf16[2,64,1024]{2,1,0:T(8,128)(2,1)S(1)}, u32[]{:S(2)}, u32[]{:S(2)}) collective-permute-start(bf16[2,64,1024]{2,1,0:T(8,128)(2,1)} %get-tuple-element.61), channel_id=1, source_target_pairs={{0,1},{1,2},{2,3},{3,0},{4,5},{5,6},{6,7},{7,4},{8,9},{9,10},{10,1... | collective-permute-start | bytes 786440 | tf_op jit(solution)/shard_map/ppermute | solution.py:28
  56.6 8.7 %collective-permute-start.19 = (bf16[2,64,1024]{2,1,0:T(8,128)(2,1)}, bf16[2,64,1024]{2,1,0:T(8,128)(2,1)S(1)}, u32[]{:S(2)}, u32[]{:S(2)}) collective-permute-start(bf16[2,64,1024]{2,1,0:T(8,128)(2,1)} %get-tuple-element.62), channel_id=1, source_target_pairs={{0,12},{4,0},{8,4},{12,8},{1,13},{5,1},{9,5},{13,9},{2,14},{6,2},{... | collective-permute-start | bytes 786440 | tf_op jit(solution)/shard_map/ppermute | solution.py:28
  58.3 8.4 %collective-permute-start.20 = (bf16[2,64,1024]{2,1,0:T(8,128)(2,1)}, bf16[2,64,1024]{2,1,0:T(8,128)(2,1)S(1)}, u32[]{:S(2)}, u32[]{:S(2)}) collective-permute-start(bf16[2,64,1024]{2,1,0:T(8,128)(2,1)} %get-tuple-element.63), channel_id=1, source_target_pairs={{0,4},{4,8},{8,12},{12,0},{1,5},{5,9},{9,13},{13,1},{2,6},{6,10},{... | collective-permute-start | bytes 786440 | tf_op jit(solution)/shard_map/ppermute | solution.py:28
  59.8 6.9 %copy-start.1 = (bf16[4,64,1024]{2,1,0:T(8,128)(2,1)S(1)}, bf16[4,64,1024]{2,1,0:T(8,128)(2,1)}, u32[]{:S(2)}) copy-start(bf16[4,64,1024]{2,1,0:T(8,128)(2,1)} %copy-done) | copy-start | bytes 1572868
  59.8 6.9 %copy-start.3 = (bf16[4,64,1024]{2,1,0:T(8,128)(2,1)S(1)}, bf16[4,64,1024]{2,1,0:T(8,128)(2,1)}, u32[]{:S(2)}) copy-start(bf16[4,64,1024]{2,1,0:T(8,128)(2,1)} %copy-done.2) | copy-start | bytes 1572868
  59.8 6.9 %copy-start.5 = (bf16[4,64,1024]{2,1,0:T(8,128)(2,1)S(1)}, bf16[4,64,1024]{2,1,0:T(8,128)(2,1)}, u32[]{:S(2)}) copy-start(bf16[4,64,1024]{2,1,0:T(8,128)(2,1)} %copy-done.4) | copy-start | bytes 1572868
  78.8 2.9 %collective-permute-start.21 = (f32[48,128]{1,0:T(8,128)S(1)}, f32[48,128]{1,0:T(8,128)S(1)}, u32[]{:S(2)}, u32[]{:S(2)}) collective-permute-start(f32[48,128]{1,0:T(8,128)S(1)} %get-tuple-element.66.mine_ref), channel_id=1, source_target_pairs={{0,32},{32,0},{1,33},{33,1},{2,34},{34,2},{3,35},{35,3},{4,36},{36... | collective-permute-start | bytes 73736 | tf_op jit(solution)/shard_map/ppermute | solution.py:28
  89.4 14.4 %collective-permute-start.25 = (bf16[256,1024]{1,0:T(8,128)(2,1)S(1)}, bf16[256,1024]{1,0:T(8,128)(2,1)S(1)}, u32[]{:S(2)}, u32[]{:S(2)}) collective-permute-start(bf16[256,1024]{1,0:T(8,128)(2,1)S(1)} %get-tuple-element.73), channel_id=1, source_target_pairs={{0,1},{1,2},{2,3},{3,0},{4,5},{5,6},{6,7},{7,4},{8,9},{9,10},{10,1... | collective-permute-start | bytes 1572872 | tf_op jit(solution)/shard_map/ppermute | solution.py:28
  89.7 28.1 %collective-permute-start.22 = (bf16[264,1024]{1,0:T(8,128)(2,1)S(1)}, bf16[264,1024]{1,0:T(8,128)(2,1)S(1)}, u32[]{:S(2)}, u32[]{:S(2)}) collective-permute-start(bf16[264,1024]{1,0:T(8,128)(2,1)S(1)} %get-tuple-element.69), channel_id=1, source_target_pairs={{0,4},{4,8},{8,12},{12,0},{1,5},{5,9},{9,13},{13,1},{2,6},{6,10},{... | collective-permute-start | bytes 1622024 | tf_op jit(solution)/shard_map/ppermute | solution.py:28
  89.7 28.1 %collective-permute-start.23 = (bf16[264,1024]{1,0:T(8,128)(2,1)S(1)}, bf16[264,1024]{1,0:T(8,128)(2,1)S(1)}, u32[]{:S(2)}, u32[]{:S(2)}) collective-permute-start(bf16[264,1024]{1,0:T(8,128)(2,1)S(1)} %get-tuple-element.70), channel_id=1, source_target_pairs={{0,8},{4,12},{8,0},{12,4},{1,9},{5,13},{9,1},{13,5},{2,10},{6,14},... | collective-permute-start | bytes 1622024 | tf_op jit(solution)/shard_map/ppermute | solution.py:28
  90.9 26.9 %collective-permute-start.24 = (bf16[264,1024]{1,0:T(8,128)(2,1)S(1)}, bf16[264,1024]{1,0:T(8,128)(2,1)S(1)}, u32[]{:S(2)}, u32[]{:S(2)}) collective-permute-start(bf16[264,1024]{1,0:T(8,128)(2,1)S(1)} %get-tuple-element.71), channel_id=1, source_target_pairs={{0,12},{4,0},{8,4},{12,8},{1,13},{5,1},{9,5},{13,9},{2,14},{6,2},{... | collective-permute-start | bytes 1622024 | tf_op jit(solution)/shard_map/ppermute | solution.py:28
  92.4 23.6 %collective-permute-start.26 = (bf16[256,1024]{1,0:T(8,128)(2,1)S(1)}, bf16[256,1024]{1,0:T(8,128)(2,1)S(1)}, u32[]{:S(2)}, u32[]{:S(2)}) collective-permute-start(bf16[256,1024]{1,0:T(8,128)(2,1)S(1)} %get-tuple-element.74), channel_id=1, source_target_pairs={{0,2},{1,3},{2,0},{3,1},{4,6},{5,7},{6,4},{7,5},{8,10},{9,11},{10,... | collective-permute-start | bytes 1572872 | tf_op jit(solution)/shard_map/ppermute | solution.py:28
  103.8 14.0 %collective-permute-start.27 = (bf16[256,1024]{1,0:T(8,128)(2,1)S(1)}, bf16[256,1024]{1,0:T(8,128)(2,1)S(1)}, u32[]{:S(2)}, u32[]{:S(2)}) collective-permute-start(bf16[256,1024]{1,0:T(8,128)(2,1)S(1)} %get-tuple-element.75), channel_id=1, source_target_pairs={{0,3},{1,0},{2,1},{3,2},{4,7},{5,4},{6,5},{7,6},{8,11},{9,8},{10,9... | collective-permute-start | bytes 1572872 | tf_op jit(solution)/shard_map/ppermute | solution.py:28
  118.4 0.7 copy-start.6
  119.1 0.6 copy-start.7
  119.7 8.0 %collective-permute-start.31 = (bf16[64,1024]{1,0:T(8,128)(2,1)S(1)}, bf16[64,1024]{1,0:T(8,128)(2,1)S(1)}, u32[]{:S(2)}, u32[]{:S(2)}) collective-permute-start(bf16[64,1024]{1,0:T(8,128)(2,1)S(1)} %get-tuple-element.81), channel_id=1, source_target_pairs={{0,4},{4,8},{8,12},{12,0},{1,5},{5,9},{9,13},{13,1},{2,6},{6,10},{... | collective-permute-start | bytes 393224 | tf_op jit(solution)/shard_map/ppermute | solution.py:28
  120.0 12.3 %collective-permute-start.28 = (bf16[72,1024]{1,0:T(8,128)(2,1)S(1)}, bf16[72,1024]{1,0:T(8,128)(2,1)S(1)}, u32[]{:S(2)}, u32[]{:S(2)}) collective-permute-start(bf16[72,1024]{1,0:T(8,128)(2,1)S(1)} %get-tuple-element.77), channel_id=1, source_target_pairs={{0,1},{1,2},{2,3},{3,0},{4,5},{5,6},{6,7},{7,4},{8,9},{9,10},{10,1... | collective-permute-start | bytes 442376 | tf_op jit(solution)/shard_map/ppermute | solution.py:28
  122.5 9.8 %collective-permute-start.29 = (bf16[72,1024]{1,0:T(8,128)(2,1)S(1)}, bf16[72,1024]{1,0:T(8,128)(2,1)S(1)}, u32[]{:S(2)}, u32[]{:S(2)}) collective-permute-start(bf16[72,1024]{1,0:T(8,128)(2,1)S(1)} %get-tuple-element.78), channel_id=1, source_target_pairs={{0,2},{1,3},{2,0},{3,1},{4,6},{5,7},{6,4},{7,5},{8,10},{9,11},{10,... | collective-permute-start | bytes 442376 | tf_op jit(solution)/shard_map/ppermute | solution.py:28
  124.5 7.8 %collective-permute-start.30 = (bf16[72,1024]{1,0:T(8,128)(2,1)S(1)}, bf16[72,1024]{1,0:T(8,128)(2,1)S(1)}, u32[]{:S(2)}, u32[]{:S(2)}) collective-permute-start(bf16[72,1024]{1,0:T(8,128)(2,1)S(1)} %get-tuple-element.79), channel_id=1, source_target_pairs={{0,3},{1,0},{2,1},{3,2},{4,7},{5,4},{6,5},{7,6},{8,11},{9,8},{10,9... | collective-permute-start | bytes 442376 | tf_op jit(solution)/shard_map/ppermute | solution.py:28
  124.9 5.3 %collective-permute-start.32 = (bf16[64,1024]{1,0:T(8,128)(2,1)S(1)}, bf16[64,1024]{1,0:T(8,128)(2,1)S(1)}, u32[]{:S(2)}, u32[]{:S(2)}) collective-permute-start(bf16[64,1024]{1,0:T(8,128)(2,1)S(1)} %get-tuple-element.82), channel_id=1, source_target_pairs={{0,8},{4,12},{8,0},{12,4},{1,9},{5,13},{9,1},{13,5},{2,10},{6,14},... | collective-permute-start | bytes 393224 | tf_op jit(solution)/shard_map/ppermute | solution.py:28
  127.7 4.6 %copy-start.12 = (bf16[64,1024]{1,0:T(8,128)(2,1)}, bf16[64,1024]{1,0:T(8,128)(2,1)S(1)}, u32[]{:S(2)}) copy-start(bf16[64,1024]{1,0:T(8,128)(2,1)S(1)} %collective-permute-done.31.refs_5_) | copy-start | bytes 393220
  127.7 4.6 %collective-permute-start.33 = (bf16[64,1024]{1,0:T(8,128)(2,1)S(1)}, bf16[64,1024]{1,0:T(8,128)(2,1)S(1)}, u32[]{:S(2)}, u32[]{:S(2)}) collective-permute-start(bf16[64,1024]{1,0:T(8,128)(2,1)S(1)} %get-tuple-element.83), channel_id=1, source_target_pairs={{0,12},{4,0},{8,4},{12,8},{1,13},{5,1},{9,5},{13,9},{2,14},{6,2},{... | collective-permute-start | bytes 393224 | tf_op jit(solution)/shard_map/ppermute | solution.py:28
  130.2 2.2 %copy-start.13 = (bf16[64,1024]{1,0:T(8,128)(2,1)}, bf16[64,1024]{1,0:T(8,128)(2,1)S(1)}, u32[]{:S(2)}) copy-start(bf16[64,1024]{1,0:T(8,128)(2,1)S(1)} %collective-permute-done.32.refs_6_) | copy-start | bytes 393220
  132.3 0.7 copy-start.14
  132.3 0.7 copy-start.9
  132.3 0.8 copy-start.10
  132.3 0.8 copy-start.11
  135.4 10.6 %collective-permute-start.34 = (bf16[128,1024]{1,0:T(8,128)(2,1)}, bf16[128,1024]{1,0:T(8,128)(2,1)S(1)}, u32[]{:S(2)}, u32[]{:S(2)}) collective-permute-start(bf16[128,1024]{1,0:T(8,128)(2,1)} %finish.1), channel_id=1, source_target_pairs={{0,0},{16,32},{32,16},{48,48},{1,1},{17,33},{33,17},{49,49},{2,2},... | collective-permute-start | bytes 786440 | tf_op jit(solution)/shard_map/ppermute | solution.py:32
  141.1 4.9 %collective-permute-start.35 = (f32[8,128]{1,0:T(8,128)S(1)}, f32[8,128]{1,0:T(8,128)S(1)}, u32[]{:S(2)}, u32[]{:S(2)}) collective-permute-start(f32[8,128]{1,0:T(8,128)S(1)} %constant_dynamic-slice_fusion), channel_id=1, source_target_pairs={{0,0},{16,32},{32,16},{48,48},{1,1},{17,33},{33,17},{49,49},{2,2},... | collective-permute-start | bytes 12296 | tf_op jit(solution)/shard_map/ppermute | solution.py:32

commit v3 on v2

v3 whole, which is shorter than its diff:
```python
import math

import jax
import jax.numpy as jnp
from jax import lax
from jax.experimental import pallas as pl
from jax.experimental.pallas import tpu as pltpu
from jax.sharding import Mesh, PartitionSpec as P

PANEL = 128
BLOCK = 128
DIM = 1024
SLICE = 256
BLOCKS = 16
PANELS = 16
SLOTS = 8
Y = ("yh", "yl")
LOW = -1e30
HIGH = 1e30
LN2 = math.log(2.0)
PACK = 4 * PANEL + 8
CHUNK = PANEL + 8
STATS = 24


def moved(value, axis, by):
    size = lax.axis_size(axis)
    return lax.ppermute(value, axis, [(i, (i - by) % size) for i in range(size)])


def swapped(value):
    return lax.ppermute(value, ("c", "yl"), [(0, 0), (1, 2), (2, 1), (3, 3)])


def nt_dot(a, b):
    return lax.dot_general(a, b, (((1,), (1,)), ((), ())), preferred_element_type=jnp.float32)


def points_of(own, oth, c):
    parts = []
    for ref, core in ((own, c), (oth, 1 - c)):
        for yh in range(2):
            parts.append((ref, 16 * yh, pl.multiple_of((2 * yh + core) * SLICE, SLICE)))
    return parts


def rows_of(parts, places, features):
    return jnp.concatenate(
        [
            jnp.concatenate([ref[(place + shift) % 32] for ref, shift, _ in parts], axis=features)
            for place in places
        ],
        axis=1 - features,
    )


def by_turns(turns, run):
    for t in range(1, SLOTS // 2 + 1):
        pl.when(turns == t)(lambda t=t: run(t))


def shifted(value, first, by):
    pairs = []
    for c in range(2):
        for z in range(4):
            for x in range(4):
                along_z = (c == 0) == first
                far = ((z + by) % 4, x) if along_z else (z, (x + by) % 4)
                pairs.append((16 * c + 4 * far[0] + far[1], 16 * c + 4 * z + x))
    return lax.ppermute(value, ("c", "z", "x"), pairs)


def turn_kernel(ref, out):
    def one(i, _):
        out[i] = ref[i].T
        return 0

    lax.fori_loop(0, 32, one, 0, unroll=4)


def score_kernel(here_ref, count_ref, list_ref, place_ref, scale_ref, own, oth, *refs):
    p_in = refs[0:4]
    l_ref, top_ref, stat_ref = refs[4:7]
    twice, once = scale_ref[0], scale_ref[1]
    parts = points_of(own, oth, here_ref[1])
    stat_ref[0:STATS, :] = jnp.full((STATS, BLOCK), LOW, jnp.float32)
    stat_ref[STATS : 2 * STATS, :] = jnp.zeros((STATS, BLOCK), jnp.float32)

    def panel_step(i, p_ref, base):
        r = base + i
        panel32 = p_ref[i].astype(jnp.float32)
        sqnorm = jnp.sum(panel32 * panel32, axis=1, keepdims=True) * once

        def run(turns):
            blocks = [list_ref[r, n] for n in range(2 * turns)]
            places = [place_ref[r, n] for n in range(2 * turns)]
            lhs = jnp.concatenate([p_ref[i, :, pl.ds(at, SLICE)] for _, _, at in parts], axis=1)
            old = jnp.concatenate([stat_ref[pl.ds(block, 1), :] for block in blocks], axis=1)
            total = jnp.concatenate(
                [stat_ref[pl.ds(STATS + block, 1), :] for block in blocks], axis=1
            )
            tops, adds = [], []
            for t in range(turns):
                lanes = slice(2 * t * BLOCK, 2 * (t + 1) * BLOCK)
                rhs = rows_of(parts, places[2 * t : 2 * t + 2], 0)
                logit = jnp.dot(lhs, rhs, preferred_element_type=jnp.float32) * twice - sqnorm
                top = jnp.maximum(old[:, lanes], jnp.max(logit, axis=0, keepdims=True))
                power = jnp.exp2(logit - top)
                l_ref[r, :, lanes] = power
                tops.append(top)
                adds.append(jnp.sum(power, axis=0, keepdims=True))
            new = jnp.concatenate(tops, axis=1)
            total = total * jnp.exp2(old - new) + jnp.concatenate(adds, axis=1)
            top_ref[r, :, 0 : 2 * turns * BLOCK] = jnp.broadcast_to(new, (8, 2 * turns * BLOCK))
            for j, block in enumerate(blocks):
                lanes = slice(j * BLOCK, (j + 1) * BLOCK)
                stat_ref[pl.ds(block, 1), :] = new[:, lanes]
                stat_ref[pl.ds(STATS + block, 1), :] = total[:, lanes]

        by_turns((count_ref[r] + 1) // 2, run)

    for k in range(4):

        def step(i, _, k=k):
            panel_step(i, p_in[k], 4 * k)
            return 0

        lax.fori_loop(0, 4, step, 0)


def sum_kernel(
    here_ref, count_ref, list_ref, place_ref, own, oth, l_ref, top_ref, mine_ref, other_ref, *refs
):
    outs, norm_ref, full_ref, mass_ref = refs[0:4], refs[4], refs[5], refs[6]
    parts = points_of(own, oth, here_ref[1])
    m0, s0 = mine_ref[0:STATS, :], mine_ref[STATS : 2 * STATS, :]
    m1, s1 = other_ref[0:STATS, :], other_ref[STATS : 2 * STATS, :]
    top = jnp.maximum(m0, m1)
    norm = top + jnp.log(s0 * jnp.exp2(m0 - top) + s1 * jnp.exp2(m1 - top)) * (1.0 / LN2)
    norm_ref[...] = norm[0:BLOCKS, :] * LN2
    row = lax.broadcasted_iota(jnp.int32, (STATS, BLOCK), 0)
    full_ref[...] = jnp.where(row < BLOCKS, norm, HIGH)
    mass_ref[...] = jnp.zeros_like(mass_ref)

    def panel_step(k, _, d):
        r = 4 * k + d
        rows = pl.multiple_of(k * PANEL, PANEL)
        turns = (count_ref[r] + 1) // 2

        @pl.when(turns == 0)
        def _():
            outs[d][pl.ds(rows, PANEL), :] = jnp.zeros((PANEL, DIM), jnp.bfloat16)

        def run(turns):
            blocks = [list_ref[r, n] for n in range(2 * turns)]
            places = [place_ref[r, n] for n in range(2 * turns)]
            norm = jnp.concatenate([full_ref[pl.ds(block, 1), :] for block in blocks], axis=1)
            lanes = slice(0, 2 * turns * BLOCK)
            factor = jnp.exp2(top_ref[r, 0:1, lanes] - norm)
            weight = (l_ref[r, :, lanes] * factor).astype(jnp.bfloat16)
            sums = jnp.dot(weight, rows_of(parts, places, 1), preferred_element_type=jnp.float32)
            sums = sums.astype(jnp.bfloat16)
            for i, (_, _, offset) in enumerate(parts):
                outs[d][pl.ds(rows, PANEL), pl.ds(offset, SLICE)] = sums[:, i * SLICE : (i + 1) * SLICE]
            mass = nt_dot(jnp.ones((8, 2 * turns * BLOCK), jnp.bfloat16), weight)[0:1, :]
            high = mass.astype(jnp.bfloat16).astype(jnp.float32)
            mass_ref[pl.ds(8 * d + k, 1), :] = high
            mass_ref[pl.ds(8 * d + 4 + k, 1), :] = mass - high

        by_turns(turns, run)
        return 0

    for d in range(4):
        lax.fori_loop(0, 4, lambda k, _, d=d: panel_step(k, _, d), 0)
        outs[d][4 * PANEL :, :] = jnp.zeros((8, DIM), jnp.bfloat16)
        outs[d][4 * PANEL :, 0:PANEL] = mass_ref[8 * d : 8 * d + 8, :].astype(jnp.bfloat16)


def fold_kernel(*refs):
    ins, outs = refs[0:4], refs[4:8]
    total = sum(ref[4 * PANEL :, 0:PANEL].astype(jnp.float32) for ref in ins)
    mass = total[0:4, :] + total[4:8, :]
    high = mass.astype(jnp.bfloat16).astype(jnp.float32)
    for i in range(4):
        rows = slice(i * PANEL, (i + 1) * PANEL)
        added = sum(ref[rows, :].astype(jnp.float32) for ref in ins)
        outs[i][0:PANEL, :] = added.astype(jnp.bfloat16)
        outs[i][PANEL:, :] = jnp.zeros((8, DIM), jnp.bfloat16)
        pieces = [high[i : i + 1], mass[i : i + 1] - high[i : i + 1]]
        pieces.append(jnp.zeros((6, PANEL), jnp.float32))
        outs[i][PANEL:, 0:PANEL] = jnp.concatenate(pieces, axis=0).astype(jnp.bfloat16)


def finish_kernel(panel_ref, *refs):
    ins, out_ref = refs[0:4], refs[4]
    row = lax.broadcasted_iota(jnp.int32, (PANEL, PANEL), 0)
    lane = lax.broadcasted_iota(jnp.int32, (PANEL, PANEL), 1)
    tail = sum(ref[PANEL:, 0:PANEL].astype(jnp.float32) for ref in ins)
    mass = tail[0:1, :] + tail[1:2, :]
    column = jnp.sum(jnp.where(row == lane, mass, 0.0), axis=1, keepdims=True)
    sums = sum(ref[0:PANEL, :].astype(jnp.float32) for ref in ins)
    panel = panel_ref[...].astype(jnp.float32)
    out_ref[...] = ((sums + panel) / (column + 1.0)).astype(jnp.bfloat16)


def shards(coarse_cluster_means, fine_cluster_means, block_panel_candidates, softmax_heat):
    yl, c = lax.axis_index("yl"), lax.axis_index("c")
    y = 2 * lax.axis_index("yh") + yl
    z, x = lax.axis_index("z"), lax.axis_index("x")
    here = jnp.stack([y, c]).astype(jnp.int32)
    once = 1.0 / (softmax_heat * (math.sqrt(DIM) * LN2))
    scale = jnp.concatenate([2.0 * once, once])
    smem = pl.BlockSpec(memory_space=pltpu.SMEM)
    vmem = pl.BlockSpec(memory_space=pltpu.VMEM)

    panel = swapped(fine_cluster_means)
    groups = coarse_cluster_means.reshape(4, 8, BLOCK, SLICE)
    own = [lax.dynamic_index_in_dim(groups, (y - d) % 4, 0, keepdims=False) for d in range(4)]
    own[1], own[3] = moved(own[1], Y, 1), moved(own[3], Y, 3)
    stack = jnp.stack([panel] + [shifted(panel, True, d) for d in (1, 2, 3)])
    mine = swapped(block_panel_candidates)
    stack, own, mine = lax.optimization_barrier((stack, own, mine))
    own[2] = moved(own[2], Y, 2)
    other = moved(mine, "c", 1)
    stacks = [stack] + [shifted(stack, False, d) for d in (1, 2, 3)]
    own = jnp.concatenate(lax.optimization_barrier((own, stacks[1], stacks[3]))[0])
    oth = moved(own, "c", 1)

    cands = jnp.where(c == 0, jnp.stack([mine, other]), jnp.stack([other, mine])).reshape(BLOCKS, 8)
    dz, dx = (cands // 4 % 4 - z) % 4, (cands % 4 - x) % 4
    spot = jnp.where(c == 0, 4 * dx + dz, 4 * dz + dx)
    spot = jnp.where(cands // 16 == c, spot, -1)
    hits = jnp.any(spot[None] == jnp.arange(PANELS, dtype=jnp.int32)[:, None, None], axis=2)
    order = jnp.cumsum(hits.astype(jnp.int32), axis=1) - 1
    count = jnp.sum(hits.astype(jnp.int32), axis=1)
    chosen = (order[:, None, :] == jnp.arange(SLOTS, dtype=jnp.int32)[None, :, None]) & hits[:, None, :]
    table = BLOCKS + jnp.sum(
        jnp.where(chosen, jnp.arange(BLOCKS, dtype=jnp.int32)[None, None, :] - BLOCKS, 0), axis=2
    )
    place = (table // 8 - y) % 4 * 8 + table % 8

    turn = pl.pallas_call(
        turn_kernel,
        in_specs=[vmem],
        out_specs=vmem,
        out_shape=jax.ShapeDtypeStruct((32, SLICE, BLOCK), jnp.bfloat16),
        compiler_params=pltpu.CompilerParams(vmem_limit_bytes=16 << 20),
        name="turn",
    )
    power, top, stat = pl.pallas_call(
        score_kernel,
        in_specs=[smem] * 5 + [vmem] * 6,
        out_specs=[vmem] * 3,
        out_shape=[
            jax.ShapeDtypeStruct((PANELS, PANEL, SLOTS * BLOCK), jnp.float32),
            jax.ShapeDtypeStruct((PANELS, 8, SLOTS * BLOCK), jnp.float32),
            jax.ShapeDtypeStruct((2 * STATS, BLOCK), jnp.float32),
        ],
        compiler_params=pltpu.CompilerParams(vmem_limit_bytes=24 << 20),
        name="scores",
    )(here, count, table, place, scale, turn(own), turn(oth), *stacks)
    stat_other = moved(stat, "c", 1)

    sums = pl.pallas_call(
        sum_kernel,
        in_specs=[smem] * 4 + [vmem] * 6,
        out_specs=[vmem] * 5,
        out_shape=[jax.ShapeDtypeStruct((PACK, DIM), jnp.bfloat16)] * 4
        + [jax.ShapeDtypeStruct((BLOCKS, BLOCK), jnp.float32)],
        scratch_shapes=[
            pltpu.VMEM((STATS, BLOCK), jnp.float32),
            pltpu.VMEM((32, PANEL), jnp.float32),
        ],
        compiler_params=pltpu.CompilerParams(vmem_limit_bytes=24 << 20),
        name="sums",
    )(here, count, table, place, own, oth, power, top, stat, stat_other)
    packs, norm = sums[0:4], sums[4]
    got = [packs[0]] + [shifted(packs[d], True, -d) for d in (1, 2, 3)]
    chunks = pl.pallas_call(
        fold_kernel,
        in_specs=[vmem] * 4,
        out_specs=[vmem] * 4,
        out_shape=[jax.ShapeDtypeStruct((CHUNK, DIM), jnp.bfloat16)] * 4,
        compiler_params=pltpu.CompilerParams(vmem_limit_bytes=16 << 20),
        name="fold",
    )(*got)
    last = [chunks[0]] + [shifted(chunks[d], False, -d) for d in (1, 2, 3)]
    revised = pl.pallas_call(
        finish_kernel,
        in_specs=[vmem] * 5,
        out_specs=vmem,
        out_shape=jax.ShapeDtypeStruct((PANEL, DIM), jnp.bfloat16),
        name="finish",
    )(panel, *last)
    norm, revised = lax.optimization_barrier((norm, revised))
    part_norm = lax.dynamic_slice_in_dim(norm, c * 8, 8, axis=0)
    return (swapped(revised), swapped(part_norm).reshape(8 * BLOCK))


def solution(mesh):
    split = Mesh(mesh.devices.reshape(2, 2, 2, 4, 4), ("yh", "c", "yl", "z", "x"))
    blk, row = ("yl", "z", "x"), ("yh", "c")
    return jax.shard_map(
        shards,
        mesh=split,
        in_specs=(P(blk, row), P(blk + row, None), P(blk + row, None), P()),
        out_specs=(P(blk + row, None), P(blk + row)),
        check_vma=False,
    )
```

time: 148 us -> 133 us (0.90)
  starting transfers between devices: 61.6 us -> 41 us
  waiting for transfers between devices: 47.3 us -> 60.1 us
  Pallas kernels: 28.8 us -> 23.2 us
    ppermute x0 -> x12, waiting for transfers between devices: none -> 41.1 us  [shifted(): return lax.ppermute(value, ('c', 'z', 'x'), pairs)]
    ppermute x32 -> x6, starting transfers between devices: 45.6 us -> 7.95 us  [moved(): lax.ppermute(value, axis, [(i, (i - by) % size) for i in range(size)])]
    ppermute x32 -> x6, waiting for transfers between devices: 44.3 us -> 14.9 us  [moved(): lax.ppermute(value, axis, [(i, (i - by) % size) for i in range(size)])]
    ppermute x0 -> x12, starting transfers between devices: none -> 15.4 us  [shifted(): return lax.ppermute(value, ('c', 'z', 'x'), pairs)]
    pallas_call x4 -> x3, Pallas kernels: 17.5 us -> 12.2 us  [the longest x1 9.55 us: shards(): pl.pallas_call(score_kernel, in_specs=[smem] * 5 + [vmem] * 6, out_specs=...]
    ppermute x4, starting transfers between devices: 16 us -> 17.7 us  [swapped(): return lax.ppermute(value, ('c', 'yl'), [(0, 0), (1, 2), (2, 1), (3, 3)])]
    unnamed x37 -> x25, local copies, waits for them, and re-layouts: 4.99 us -> 4.79 us
  transfers between devices with their start and end apart: 36 -> 22, of which waited for: 15 -> 11; matrix products, arithmetic and copies ran while one was open for 2% -> 2% of each run, Pallas kernels for 4% -> 3%
where the time goes in v3:
time: 133 us; the launch traced here: 134 us
  waiting for transfers between devices  60.1 us (45%)
  starting transfers between devices  41 us (31%)
  Pallas kernels  23.2 us (17%)
  local copies, waits for them, and re-layouts  6.57 us (5%)
  between operations  1.65 us (1%)
    ppermute x12, waiting for transfers between devices, shifted(): return lax.ppermute(value, ('c', 'z', 'x'), pairs)  41.1 us
    ppermute x4, starting transfers between devices, swapped(): return lax.ppermute(value, ('c', 'yl'), [(0, 0), (1, 2), (2, 1), (3, 3)])  17.7 us
    ppermute x12, starting transfers between devices, shifted(): return lax.ppermute(value, ('c', 'z', 'x'), pairs)  15.4 us
    ppermute x6, waiting for transfers between devices, moved(): lax.ppermute(value, axis, [(i, (i - by) % size) for i in range(size)])  14.9 us
    pallas_call x1, Pallas kernels, shards(): pl.pallas_call(score_kernel, in_specs=[smem] * 5 + [vmem] * 6, out_specs=...  9.55 us
    ppermute x6, starting transfers between devices, moved(): lax.ppermute(value, axis, [(i, (i - by) % size) for i in range(size)])  7.95 us
    pallas_call x1, Pallas kernels, shards(): pl.pallas_call(sum_kernel, in_specs=[smem] * 4 + [vmem] * 6, out_specs=[v...  7.31 us
    unnamed x25, local copies, waits for them, and re-layouts  4.79 us
  transfers between devices with their start and end apart: 22, of which 11 were waited for; matrix products, arithmetic and copies ran while one was open for 2% of the time, Pallas kernels for 3%

profile of v3, /device:TPU:1, one launch (start us, length us, event | category | flops | bytes accessed | tf_op | source)
XLA Modules:
  0.0 133.6 jit_solution(6698894723635322286)
XLA Ops:
  0.6 4.6 %collective-permute-start = (bf16[128,1024]{1,0:T(8,128)(2,1)}, bf16[128,1024]{1,0:T(8,128)(2,1)S(1)}, u32[]{:S(2)}, u32[]{:S(2)}) collective-permute-start(bf16[128,1024]{1,0:T(8,128)(2,1)} %param.5), channel_id=1, source_target_pairs={{0,0},{16,32},{32,16},{48,48},{1,1},{17,33},{33,17},{49,49},{2,2},... | collective-permute-start | bytes 786440 | tf_op jit(solution)/shard_map/ppermute | solution.py:32
  5.3 1.7 %dynamic-slice_bitcast_fusion = (bf16[8,128,256]{2,1,0:T(8,128)(2,1)S(1)}, bf16[8,128,256]{2,1,0:T(8,128)(2,1)S(1)}, bf16[8,128,256]{2,1,0:T(8,128)(2,1)S(1)}, bf16[8,128,256]{2,1,0:T(8,128)(2,1)S(1)}) fusion(bf16[4,8,128,256]{3,2,1,0:T(8,128)(2,1)} %bitcast.22, s32[]{:T(128)S(6)} %select_n.144, s32[]{:T(128)S(6)} %select_n.142, s32[]{:T(128)S(6)} %select_n.140, ...), kind=kLoop, calls=%fused_computation.1 | loop fusion | bytes 4194320 | tf_op jit(solution)/shard_map/jit(dynamic_index_in_dim)/squeeze | solution.py:218
  7.0 0.1 collective-permute-start.5
  7.1 2.7 %collective-permute-start.4 = (bf16[8,128,256]{2,1,0:T(8,128)(2,1)S(1)}, bf16[8,128,256]{2,1,0:T(8,128)(2,1)S(1)}, u32[]{:S(2)}, u32[]{:S(2)}) collective-permute-start(bf16[8,128,256]{2,1,0:T(8,128)(2,1)S(1)} %get-tuple-element.52), channel_id=1, source_target_pairs={{0,80},{16,0},{64,16},{80,64},{1,81},{17,1},{65,17},{81,65},{2,82}... | collective-permute-start | bytes 1572872 | tf_op jit(solution)/shard_map/ppermute | solution.py:28
  9.7 0.0 collective-permute-done.panel_ref
  9.7 1.2 collective-permute-start.3
  11.0 2.5 %collective-permute-start.2 = (bf16[128,1024]{1,0:T(8,128)(2,1)S(1)}, bf16[128,1024]{1,0:T(8,128)(2,1)S(1)}, u32[]{:S(2)}, u32[]{:S(2)}) collective-permute-start(bf16[128,1024]{1,0:T(8,128)(2,1)S(1)} %collective-permute-done.panel_ref), channel_id=1, source_target_pairs={{8,0},{9,1},{10,2},{11,3},{12,4},{13,5},{14,6},{15,7},{0,8},{1,9},... | collective-permute-start | bytes 786440 | tf_op jit(solution)/shard_map/ppermute | solution.py:70
  13.4 1.2 collective-permute-start.1
  14.6 1.9 %collective-permute-done.3 = bf16[128,1024]{1,0:T(8,128)(2,1)S(1)} collective-permute-done((bf16[128,1024]{1,0:T(8,128)(2,1)S(1)}, bf16[128,1024]{1,0:T(8,128)(2,1)S(1)}, u32[]{:S(2)}, u32[]{:S(2)}) %collective-permute-start.3) | collective-permute-done | bytes 262176 | tf_op jit(solution)/shard_map/ppermute | solution.py:70
  16.5 5.5 %collective-permute-start.6 = (s32[8,8]{1,0:T(8,128)S(1)}, s32[8,8]{1,0:T(8,128)S(1)}, u32[]{:S(2)}, u32[]{:S(2)}) collective-permute-start(s32[8,8]{1,0:T(8,128)S(1)} %copy-done.9), channel_id=1, source_target_pairs={{0,0},{16,32},{32,16},{48,48},{1,1},{17,33},{33,17},{49,49},{2,2},... | collective-permute-start | bytes 776 | tf_op jit(solution)/shard_map/ppermute | solution.py:32
  22.0 0.0 collective-permute-done.2
  22.0 0.0 collective-permute-done.1
  22.1 0.1 pad_maximum_fusion.refs_0_
  22.2 1.1 collective-permute-done.6
  23.3 0.0 collective-permute-done.5
  23.3 0.0 collective-permute-done.4
  23.3 0.2 collective-permute-start.10
  23.5 2.5 %collective-permute-start.9 = (bf16[4,128,1024]{2,1,0:T(8,128)(2,1)S(1)}, bf16[4,128,1024]{2,1,0:T(8,128)(2,1)S(1)}, u32[]{:S(2)}, u32[]{:S(2)}) collective-permute-start(bf16[4,128,1024]{2,1,0:T(8,128)(2,1)S(1)} %pad_maximum_fusion.refs_0_), channel_id=1, source_target_pairs={{1,0},{2,1},{3,2},{0,3},{5,4},{6,5},{7,6},{4,7},{9,8},{10,9},{11,1... | collective-permute-start | bytes 3145736 | tf_op jit(solution)/shard_map/ppermute | solution.py:70
  26.0 2.5 %collective-permute-start.8 = (bf16[8,128,256]{2,1,0:T(8,128)(2,1)S(1)}, bf16[8,128,256]{2,1,0:T(8,128)(2,1)S(1)}, u32[]{:S(2)}, u32[]{:S(2)}) collective-permute-start(bf16[8,128,256]{2,1,0:T(8,128)(2,1)S(1)} %get-tuple-element.29), channel_id=1, source_target_pairs={{0,64},{16,80},{64,0},{80,16},{1,65},{17,81},{65,1},{81,17},{2,66}... | collective-permute-start | bytes 1572872 | tf_op jit(solution)/shard_map/ppermute | solution.py:28
  28.4 12.9 %collective-permute-done.8 = bf16[8,128,256]{2,1,0:T(8,128)(2,1)S(1)} collective-permute-done((bf16[8,128,256]{2,1,0:T(8,128)(2,1)S(1)}, bf16[8,128,256]{2,1,0:T(8,128)(2,1)S(1)}, u32[]{:S(2)}, u32[]{:S(2)}) %collective-permute-start.8) | collective-permute-done | bytes 524320 | tf_op jit(solution)/shard_map/ppermute | solution.py:28
  41.3 0.0 collective-permute-done.10.refs_3_
  41.3 1.0 copy-done
  42.3 1.0 copy-done.2
  43.5 0.5 collective-permute-start.11
  44.6 1.1 collective-permute-start.12
  45.8 0.1 pad_maximum_fusion.1.scale_ref
  45.8 0.1 pad_add_fusion.here_ref
  45.9 0.7 collective-permute-start.7
  46.6 1.2 collective-permute-done.7
  47.8 0.1 copy.16
  47.9 0.2 reduce_window_sum.11
  48.1 0.1 convert_reduce_fusion.count_ref
  48.2 0.4 select_reduce_fusion
  48.6 1.0 turn.2.own
  49.6 0.0 collective-permute-done.11.ref.oth
  49.6 2.7 %turn.3.oth = bf16[32,256,128]{2,1,0:T(8,128)(2,1)S(1)} custom-call(bf16[32,128,256]{2,1,0:T(8,128)(2,1)} %collective-permute-done.11.ref.oth), custom_call_target="tpu_custom_call" | custom-call | tf_op jit(solution)/shard_map/turn/pallas_call | solution.py:261
  52.3 8.0 %collective-permute-done.12.refs_2_ = bf16[4,128,1024]{2,1,0:T(8,128)(2,1)} collective-permute-done((bf16[4,128,1024]{2,1,0:T(8,128)(2,1)S(1)}, bf16[4,128,1024]{2,1,0:T(8,128)(2,1)}, u32[]{:S(2)}, u32[]{:S(2)}) %collective-permute-start.12) | collective-permute-done | bytes 1048608 | tf_op jit(solution)/shard_map/ppermute | solution.py:70
  60.3 9.6 %scores.1 = (f32[16,128,1024]{2,1,0:T(8,128)S(1)}, f32[16,8,1024]{2,1,0:T(8,128)S(1)}, f32[48,128]{1,0:T(8,128)S(1)}) custom-call(s32[2]{0:T(128)S(1)} %pad_add_fusion.here_ref, s32[16]{0:T(128)S(1)} %convert_reduce_fusion.count_ref, s32[16,8]{1,0:T(8,128)S(1)} %get-tuple-element.55.list_ref, s32[16,8]{1,0:T(8,128)S(1)} %get-tuple-element.54.place_ref, ...), custom_call_target="tpu_custom_call" | custom-call | tf_op jit(solution)/shard_map/scores/pallas_call | solution.py:250
  69.8 1.6 %collective-permute-start.13 = (f32[48,128]{1,0:T(8,128)S(1)}, f32[48,128]{1,0:T(8,128)S(1)}, u32[]{:S(2)}, u32[]{:S(2)}) collective-permute-start(f32[48,128]{1,0:T(8,128)S(1)} %get-tuple-element.38.mine_ref), channel_id=1, source_target_pairs={{0,32},{32,0},{1,33},{33,1},{2,34},{34,2},{3,35},{35,3},{4,36},{36... | collective-permute-start | bytes 73736 | tf_op jit(solution)/shard_map/ppermute | solution.py:28
  71.5 0.8 collective-permute-done.13.other_ref
  72.3 7.3 %sums.1 = (bf16[520,1024]{1,0:T(8,128)(2,1)S(1)}, bf16[520,1024]{1,0:T(8,128)(2,1)S(1)}, bf16[520,1024]{1,0:T(8,128)(2,1)S(1)}, bf16[520,1024]{1,0:T(8,128)(2,1)S(1)}, f32[16,128]{1,0:T(8,128)S(1)}) custom-call(s32[2]{0:T(128)S(1)} %pad_add_fusion.here_ref, s32[16]{0:T(128)S(1)} %convert_reduce_fusion.count_ref, s32[16,8]{1,0:T(8,128)S(1)} %get-tuple-element.55.list_ref, ...), custom_call_target="tpu_custom_call" | custom-call | tf_op jit(solution)/shard_map/sums/pallas_call | solution.py:264
  79.6 0.1 collective-permute-start.14
  79.7 2.2 %collective-permute-start.15 = (bf16[520,1024]{1,0:T(8,128)(2,1)S(1)}, bf16[520,1024]{1,0:T(8,128)(2,1)S(1)}, u32[]{:S(2)}, u32[]{:S(2)}) collective-permute-start(bf16[520,1024]{1,0:T(8,128)(2,1)S(1)} %get-tuple-element.42), channel_id=1, source_target_pairs={{8,0},{9,1},{10,2},{11,3},{12,4},{13,5},{14,6},{15,7},{0,8},{1,9},... | collective-permute-start | bytes 3194888 | tf_op jit(solution)/shard_map/ppermute | solution.py:70
  81.9 1.2 collective-permute-start.16
  83.2 23.3 %collective-permute-done.14.refs_1_ = bf16[520,1024]{1,0:T(8,128)(2,1)S(1)} collective-permute-done((bf16[520,1024]{1,0:T(8,128)(2,1)S(1)}, bf16[520,1024]{1,0:T(8,128)(2,1)S(1)}, u32[]{:S(2)}, u32[]{:S(2)}) %collective-permute-start.14) | collective-permute-done | bytes 1064992 | tf_op jit(solution)/shard_map/ppermute | solution.py:70
  106.4 0.0 collective-permute-done.15.refs_2_
  106.5 0.6 collective-permute-done.16.refs_3_
  107.1 0.5 fold.1
  107.6 0.7 copy-done.4
  108.3 2.4 %collective-permute-start.18 = (bf16[136,1024]{1,0:T(8,128)(2,1)S(1)}, bf16[136,1024]{1,0:T(8,128)(2,1)S(1)}, u32[]{:S(2)}, u32[]{:S(2)}) collective-permute-start(bf16[136,1024]{1,0:T(8,128)(2,1)S(1)} %get-tuple-element.46), channel_id=1, source_target_pairs={{2,0},{3,1},{0,2},{1,3},{6,4},{7,5},{4,6},{5,7},{10,8},{11,9},{8,1... | collective-permute-start | bytes 835592 | tf_op jit(solution)/shard_map/ppermute | solution.py:70
  110.7 0.8 collective-permute-start.19
  111.5 6.6 %collective-permute-done.17.refs_1_ = bf16[136,1024]{1,0:T(8,128)(2,1)S(1)} collective-permute-done((bf16[136,1024]{1,0:T(8,128)(2,1)S(1)}, bf16[136,1024]{1,0:T(8,128)(2,1)S(1)}, u32[]{:S(2)}, u32[]{:S(2)}) %collective-permute-start.17) | collective-permute-done | bytes 278560 | tf_op jit(solution)/shard_map/ppermute | solution.py:70
  118.2 0.0 collective-permute-done.18.refs_2_
  118.2 0.6 collective-permute-done.19.refs_3_
  118.8 0.1 copy-done.6
  118.9 0.1 copy-done.7
  119.0 0.5 copy-done.8
  119.5 2.2 %finish.1 = bf16[128,1024]{1,0:T(8,128)(2,1)} custom-call(bf16[128,1024]{1,0:T(8,128)(2,1)} %copy-done.5, bf16[136,1024]{1,0:T(8,128)(2,1)} %copy-done.4, bf16[136,1024]{1,0:T(8,128)(2,1)} %copy-done.6, bf16[136,1024]{1,0:T(8,128)(2,1)} %copy-done.7, bf16[136,1024]{1,0:T(8,128)(2,1)} %copy-done.8), custom_call_target="tpu_custom_call" | custom-call | tf_op jit(solution)/shard_map/finish/pallas_call | solution.py:288
  121.7 5.6 %collective-permute-start.20 = (bf16[128,1024]{1,0:T(8,128)(2,1)}, bf16[128,1024]{1,0:T(8,128)(2,1)S(1)}, u32[]{:S(2)}, u32[]{:S(2)}) collective-permute-start(bf16[128,1024]{1,0:T(8,128)(2,1)} %finish.1), channel_id=1, source_target_pairs={{0,0},{16,32},{32,16},{48,48},{1,1},{17,33},{33,17},{49,49},{2,2},... | collective-permute-start | bytes 786440 | tf_op jit(solution)/shard_map/ppermute | solution.py:32
  127.3 1.9 %collective-permute-start.21 = (f32[8,128]{1,0:T(8,128)S(1)}, f32[8,128]{1,0:T(8,128)S(1)}, u32[]{:S(2)}, u32[]{:S(2)}) collective-permute-start(f32[8,128]{1,0:T(8,128)S(1)} %constant_dynamic-slice_fusion), channel_id=1, source_target_pairs={{0,0},{16,32},{32,16},{48,48},{1,1},{17,33},{33,17},{49,49},{2,2},... | collective-permute-start | bytes 12296 | tf_op jit(solution)/shard_map/ppermute | solution.py:32
  129.3 3.0 %collective-permute-done.21 = f32[8,128]{1,0:T(8,128)S(1)} collective-permute-done((f32[8,128]{1,0:T(8,128)S(1)}, f32[8,128]{1,0:T(8,128)S(1)}, u32[]{:S(2)}, u32[]{:S(2)}) %collective-permute-start.21) | collective-permute-done | bytes 4128 | tf_op jit(solution)/shard_map/ppermute | solution.py:32
  132.3 0.0 collective-permute-done.20
  132.3 0.7 copy.24
  133.0 0.6 copy.25
  (27 shorter events, 0.3 us)
Async XLA Ops:
  0.6 9.1 %collective-permute-start = (bf16[128,1024]{1,0:T(8,128)(2,1)}, bf16[128,1024]{1,0:T(8,128)(2,1)S(1)}, u32[]{:S(2)}, u32[]{:S(2)}) collective-permute-start(bf16[128,1024]{1,0:T(8,128)(2,1)} %param.5), channel_id=1, source_target_pairs={{0,0},{16,32},{32,16},{48,48},{1,1},{17,33},{33,17},{49,49},{2,2},... | collective-permute-start | bytes 786440 | tf_op jit(solution)/shard_map/ppermute | solution.py:32
  5.3 11.2 %copy-start.9 = (s32[8,8]{1,0:T(8,128)S(1)}, s32[8,8]{1,0:T(8,128)}, u32[]{:S(2)}) copy-start(s32[8,8]{1,0:T(8,128)} %param.6) | copy-start | bytes 772
  7.0 16.3 %collective-permute-start.5 = (bf16[8,128,256]{2,1,0:T(8,128)(2,1)S(1)}, bf16[8,128,256]{2,1,0:T(8,128)(2,1)S(1)}, u32[]{:S(2)}, u32[]{:S(2)}) collective-permute-start(bf16[8,128,256]{2,1,0:T(8,128)(2,1)S(1)} %get-tuple-element.50), channel_id=1, source_target_pairs={{0,16},{16,64},{64,80},{80,0},{1,17},{17,65},{65,81},{81,1},{2,18}... | collective-permute-start | bytes 1572872 | tf_op jit(solution)/shard_map/ppermute | solution.py:28
  7.1 16.2 %collective-permute-start.4 = (bf16[8,128,256]{2,1,0:T(8,128)(2,1)S(1)}, bf16[8,128,256]{2,1,0:T(8,128)(2,1)S(1)}, u32[]{:S(2)}, u32[]{:S(2)}) collective-permute-start(bf16[8,128,256]{2,1,0:T(8,128)(2,1)S(1)} %get-tuple-element.52), channel_id=1, source_target_pairs={{0,80},{16,0},{64,16},{80,64},{1,81},{17,1},{65,17},{81,65},{2,82}... | collective-permute-start | bytes 1572872 | tf_op jit(solution)/shard_map/ppermute | solution.py:28
  9.7 33.6 %copy-start.5 = (bf16[128,1024]{1,0:T(8,128)(2,1)}, bf16[128,1024]{1,0:T(8,128)(2,1)S(1)}, u32[]{:S(2)}) copy-start(bf16[128,1024]{1,0:T(8,128)(2,1)S(1)} %collective-permute-done.panel_ref) | copy-start | bytes 786436
  9.7 6.7 %collective-permute-start.3 = (bf16[128,1024]{1,0:T(8,128)(2,1)S(1)}, bf16[128,1024]{1,0:T(8,128)(2,1)S(1)}, u32[]{:S(2)}, u32[]{:S(2)}) collective-permute-start(bf16[128,1024]{1,0:T(8,128)(2,1)S(1)} %collective-permute-done.panel_ref), channel_id=1, source_target_pairs={{12,0},{13,1},{14,2},{15,3},{0,4},{1,5},{2,6},{3,7},{4,8},{5,9},{6... | collective-permute-start | bytes 786440 | tf_op jit(solution)/shard_map/ppermute | solution.py:70
  11.0 11.1 %collective-permute-start.2 = (bf16[128,1024]{1,0:T(8,128)(2,1)S(1)}, bf16[128,1024]{1,0:T(8,128)(2,1)S(1)}, u32[]{:S(2)}, u32[]{:S(2)}) collective-permute-start(bf16[128,1024]{1,0:T(8,128)(2,1)S(1)} %collective-permute-done.panel_ref), channel_id=1, source_target_pairs={{8,0},{9,1},{10,2},{11,3},{12,4},{13,5},{14,6},{15,7},{0,8},{1,9},... | collective-permute-start | bytes 786440 | tf_op jit(solution)/shard_map/ppermute | solution.py:70
  13.4 8.6 %collective-permute-start.1 = (bf16[128,1024]{1,0:T(8,128)(2,1)S(1)}, bf16[128,1024]{1,0:T(8,128)(2,1)S(1)}, u32[]{:S(2)}, u32[]{:S(2)}) collective-permute-start(bf16[128,1024]{1,0:T(8,128)(2,1)S(1)} %collective-permute-done.panel_ref), channel_id=1, source_target_pairs={{4,0},{5,1},{6,2},{7,3},{8,4},{9,5},{10,6},{11,7},{12,8},{13,9},{1... | collective-permute-start | bytes 786440 | tf_op jit(solution)/shard_map/ppermute | solution.py:70
  16.5 6.8 %collective-permute-start.6 = (s32[8,8]{1,0:T(8,128)S(1)}, s32[8,8]{1,0:T(8,128)S(1)}, u32[]{:S(2)}, u32[]{:S(2)}) collective-permute-start(s32[8,8]{1,0:T(8,128)S(1)} %copy-done.9), channel_id=1, source_target_pairs={{0,0},{16,32},{32,16},{48,48},{1,1},{17,33},{33,17},{49,49},{2,2},... | collective-permute-start | bytes 776 | tf_op jit(solution)/shard_map/ppermute | solution.py:32
  23.3 18.0 %collective-permute-start.10 = (bf16[4,128,1024]{2,1,0:T(8,128)(2,1)S(1)}, bf16[4,128,1024]{2,1,0:T(8,128)(2,1)S(1)}, u32[]{:S(2)}, u32[]{:S(2)}) collective-permute-start(bf16[4,128,1024]{2,1,0:T(8,128)(2,1)S(1)} %pad_maximum_fusion.refs_0_), channel_id=1, source_target_pairs={{3,0},{0,1},{1,2},{2,3},{7,4},{4,5},{5,6},{6,7},{11,8},{8,9},{9,10... | collective-permute-start | bytes 3145736 | tf_op jit(solution)/shard_map/ppermute | solution.py:70
  23.5 18.8 %collective-permute-start.9 = (bf16[4,128,1024]{2,1,0:T(8,128)(2,1)S(1)}, bf16[4,128,1024]{2,1,0:T(8,128)(2,1)S(1)}, u32[]{:S(2)}, u32[]{:S(2)}) collective-permute-start(bf16[4,128,1024]{2,1,0:T(8,128)(2,1)S(1)} %pad_maximum_fusion.refs_0_), channel_id=1, source_target_pairs={{1,0},{2,1},{3,2},{0,3},{5,4},{6,5},{7,6},{4,7},{9,8},{10,9},{11,1... | collective-permute-start | bytes 3145736 | tf_op jit(solution)/shard_map/ppermute | solution.py:70
  26.0 15.3 %collective-permute-start.8 = (bf16[8,128,256]{2,1,0:T(8,128)(2,1)S(1)}, bf16[8,128,256]{2,1,0:T(8,128)(2,1)S(1)}, u32[]{:S(2)}, u32[]{:S(2)}) collective-permute-start(bf16[8,128,256]{2,1,0:T(8,128)(2,1)S(1)} %get-tuple-element.29), channel_id=1, source_target_pairs={{0,64},{16,80},{64,0},{80,16},{1,65},{17,81},{65,1},{81,17},{2,66}... | collective-permute-start | bytes 1572872 | tf_op jit(solution)/shard_map/ppermute | solution.py:28
  41.3 1.0 copy-start
  42.3 1.0 copy-start.2
  43.5 6.1 %collective-permute-start.11 = (bf16[32,128,256]{2,1,0:T(8,128)(2,1)S(1)}, bf16[32,128,256]{2,1,0:T(8,128)(2,1)}, u32[]{:S(2)}, u32[]{:S(2)}) collective-permute-start(bf16[32,128,256]{2,1,0:T(8,128)(2,1)S(1)} %constant_dynamic-update-slice_fusion.ref.own), channel_id=1, source_target_pairs={{0,32},{32,0},{1,33},{33,1},{2,34},{34,2},{3,35},{35,3},{4,36},{36... | collective-permute-start | bytes 6291464 | tf_op jit(solution)/shard_map/ppermute | solution.py:28
  44.6 15.6 %collective-permute-start.12 = (bf16[4,128,1024]{2,1,0:T(8,128)(2,1)S(1)}, bf16[4,128,1024]{2,1,0:T(8,128)(2,1)}, u32[]{:S(2)}, u32[]{:S(2)}) collective-permute-start(bf16[4,128,1024]{2,1,0:T(8,128)(2,1)S(1)} %pad_maximum_fusion.refs_0_), channel_id=1, source_target_pairs={{2,0},{3,1},{0,2},{1,3},{6,4},{7,5},{4,6},{5,7},{10,8},{11,9},{8,1... | collective-permute-start | bytes 3145736 | tf_op jit(solution)/shard_map/ppermute | solution.py:70
  45.9 1.8 %collective-permute-start.7 = (s32[8,8]{1,0:T(8,128)S(1)}, s32[8,8]{1,0:T(8,128)S(1)}, u32[]{:S(2)}, u32[]{:S(2)}) collective-permute-start(s32[8,8]{1,0:T(8,128)S(1)} %collective-permute-done.6), channel_id=1, source_target_pairs={{0,32},{32,0},{1,33},{33,1},{2,34},{34,2},{3,35},{35,3},{4,36},{36... | collective-permute-start | bytes 776 | tf_op jit(solution)/shard_map/ppermute | solution.py:28
  49.5 10.7 %copy-start.1 = (bf16[4,128,1024]{2,1,0:T(8,128)(2,1)S(1)}, bf16[4,128,1024]{2,1,0:T(8,128)(2,1)}, u32[]{:S(2)}) copy-start(bf16[4,128,1024]{2,1,0:T(8,128)(2,1)} %copy-done) | copy-start | bytes 3145732
  49.6 10.7 %copy-start.3 = (bf16[4,128,1024]{2,1,0:T(8,128)(2,1)S(1)}, bf16[4,128,1024]{2,1,0:T(8,128)(2,1)}, u32[]{:S(2)}) copy-start(bf16[4,128,1024]{2,1,0:T(8,128)(2,1)} %copy-done.2) | copy-start | bytes 3145732
  69.8 2.5 %collective-permute-start.13 = (f32[48,128]{1,0:T(8,128)S(1)}, f32[48,128]{1,0:T(8,128)S(1)}, u32[]{:S(2)}, u32[]{:S(2)}) collective-permute-start(f32[48,128]{1,0:T(8,128)S(1)} %get-tuple-element.38.mine_ref), channel_id=1, source_target_pairs={{0,32},{32,0},{1,33},{33,1},{2,34},{34,2},{3,35},{35,3},{4,36},{36... | collective-permute-start | bytes 73736 | tf_op jit(solution)/shard_map/ppermute | solution.py:28
  79.6 26.8 %collective-permute-start.14 = (bf16[520,1024]{1,0:T(8,128)(2,1)S(1)}, bf16[520,1024]{1,0:T(8,128)(2,1)S(1)}, u32[]{:S(2)}, u32[]{:S(2)}) collective-permute-start(bf16[520,1024]{1,0:T(8,128)(2,1)S(1)} %get-tuple-element.41), channel_id=1, source_target_pairs={{12,0},{13,1},{14,2},{15,3},{0,4},{1,5},{2,6},{3,7},{4,8},{5,9},{6... | collective-permute-start | bytes 3194888 | tf_op jit(solution)/shard_map/ppermute | solution.py:70
  79.7 26.7 %collective-permute-start.15 = (bf16[520,1024]{1,0:T(8,128)(2,1)S(1)}, bf16[520,1024]{1,0:T(8,128)(2,1)S(1)}, u32[]{:S(2)}, u32[]{:S(2)}) collective-permute-start(bf16[520,1024]{1,0:T(8,128)(2,1)S(1)} %get-tuple-element.42), channel_id=1, source_target_pairs={{8,0},{9,1},{10,2},{11,3},{12,4},{13,5},{14,6},{15,7},{0,8},{1,9},... | collective-permute-start | bytes 3194888 | tf_op jit(solution)/shard_map/ppermute | solution.py:70
  81.9 25.1 %collective-permute-start.16 = (bf16[520,1024]{1,0:T(8,128)(2,1)S(1)}, bf16[520,1024]{1,0:T(8,128)(2,1)S(1)}, u32[]{:S(2)}, u32[]{:S(2)}) collective-permute-start(bf16[520,1024]{1,0:T(8,128)(2,1)S(1)} %get-tuple-element.43), channel_id=1, source_target_pairs={{4,0},{5,1},{6,2},{7,3},{8,4},{9,5},{10,6},{11,7},{12,8},{13,9},{1... | collective-permute-start | bytes 3194888 | tf_op jit(solution)/shard_map/ppermute | solution.py:70
  107.6 0.7 copy-start.4
  108.3 9.9 %collective-permute-start.17 = (bf16[136,1024]{1,0:T(8,128)(2,1)S(1)}, bf16[136,1024]{1,0:T(8,128)(2,1)S(1)}, u32[]{:S(2)}, u32[]{:S(2)}) collective-permute-start(bf16[136,1024]{1,0:T(8,128)(2,1)S(1)} %get-tuple-element.45), channel_id=1, source_target_pairs={{3,0},{0,1},{1,2},{2,3},{7,4},{4,5},{5,6},{6,7},{11,8},{8,9},{9,10... | collective-permute-start | bytes 835592 | tf_op jit(solution)/shard_map/ppermute | solution.py:70
  108.3 9.9 %collective-permute-start.18 = (bf16[136,1024]{1,0:T(8,128)(2,1)S(1)}, bf16[136,1024]{1,0:T(8,128)(2,1)S(1)}, u32[]{:S(2)}, u32[]{:S(2)}) collective-permute-start(bf16[136,1024]{1,0:T(8,128)(2,1)S(1)} %get-tuple-element.46), channel_id=1, source_target_pairs={{2,0},{3,1},{0,2},{1,3},{6,4},{7,5},{4,6},{5,7},{10,8},{11,9},{8,1... | collective-permute-start | bytes 835592 | tf_op jit(solution)/shard_map/ppermute | solution.py:70
  110.7 8.1 %collective-permute-start.19 = (bf16[136,1024]{1,0:T(8,128)(2,1)S(1)}, bf16[136,1024]{1,0:T(8,128)(2,1)S(1)}, u32[]{:S(2)}, u32[]{:S(2)}) collective-permute-start(bf16[136,1024]{1,0:T(8,128)(2,1)S(1)} %get-tuple-element.47), channel_id=1, source_target_pairs={{1,0},{2,1},{3,2},{0,3},{5,4},{6,5},{7,6},{4,7},{9,8},{10,9},{11,1... | collective-permute-start | bytes 835592 | tf_op jit(solution)/shard_map/ppermute | solution.py:70
  118.2 0.7 copy-start.6
  118.2 0.8 copy-start.7
  118.8 0.7 copy-start.8
  121.7 10.6 %collective-permute-start.20 = (bf16[128,1024]{1,0:T(8,128)(2,1)}, bf16[128,1024]{1,0:T(8,128)(2,1)S(1)}, u32[]{:S(2)}, u32[]{:S(2)}) collective-permute-start(bf16[128,1024]{1,0:T(8,128)(2,1)} %finish.1), channel_id=1, source_target_pairs={{0,0},{16,32},{32,16},{48,48},{1,1},{17,33},{33,17},{49,49},{2,2},... | collective-permute-start | bytes 786440 | tf_op jit(solution)/shard_map/ppermute | solution.py:32
  127.3 4.9 %collective-permute-start.21 = (f32[8,128]{1,0:T(8,128)S(1)}, f32[8,128]{1,0:T(8,128)S(1)}, u32[]{:S(2)}, u32[]{:S(2)}) collective-permute-start(f32[8,128]{1,0:T(8,128)S(1)} %constant_dynamic-slice_fusion), channel_id=1, source_target_pairs={{0,0},{16,32},{32,16},{48,48},{1,1},{17,33},{33,17},{49,49},{2,2},... | collective-permute-start | bytes 12296 | tf_op jit(solution)/shard_map/ppermute | solution.py:32

commit v4 on v3

--- a/solution.py
+++ b/solution.py
@@ -1,3 +1,4 @@
+import functools
 import math
 
 import jax
@@ -68,6 +69,18 @@
                 far = ((z + by) % 4, x) if along_z else (z, (x + by) % 4)
                 pairs.append((16 * c + 4 * far[0] + far[1], 16 * c + 4 * z + x))
     return lax.ppermute(value, ("c", "z", "x"), pairs)
+
+
+def homeward(value, by):
+    pairs = []
+    for c in range(2):
+        for yl in range(2):
+            for z in range(4):
+                for x in range(4):
+                    far = (z, (x + by) % 4) if c == 0 else ((z + by) % 4, x)
+                    to = 16 * (2 * yl + c) + 4 * far[0] + far[1]
+                    pairs.append((16 * (2 * c + yl) + 4 * z + x, to))
+    return lax.ppermute(value, ("c", "yl", "z", "x"), pairs)
 
 
 def turn_kernel(ref, out):
@@ -129,9 +142,9 @@
 
 
 def sum_kernel(
-    here_ref, count_ref, list_ref, place_ref, own, oth, l_ref, top_ref, mine_ref, other_ref, *refs
+    wanted, here_ref, count_ref, list_ref, place_ref, own, oth, l_ref, top_ref, mine_ref, other_ref, *refs
 ):
-    outs, norm_ref, full_ref, mass_ref = refs[0:4], refs[4], refs[5], refs[6]
+    outs, norm_ref, full_ref, mass_ref = dict(zip(wanted, refs[0:2])), refs[2], refs[3], refs[4]
     parts = points_of(own, oth, here_ref[1])
     m0, s0 = mine_ref[0:STATS, :], mine_ref[STATS : 2 * STATS, :]
     m1, s1 = other_ref[0:STATS, :], other_ref[STATS : 2 * STATS, :]
@@ -170,7 +183,7 @@
         by_turns(turns, run)
         return 0
 
-    for d in range(4):
+    for d in wanted:
         lax.fori_loop(0, 4, lambda k, _, d=d: panel_step(k, _, d), 0)
         outs[d][4 * PANEL :, :] = jnp.zeros((8, DIM), jnp.bfloat16)
         outs[d][4 * PANEL :, 0:PANEL] = mass_ref[8 * d : 8 * d + 8, :].astype(jnp.bfloat16)
@@ -200,7 +213,7 @@
     column = jnp.sum(jnp.where(row == lane, mass, 0.0), axis=1, keepdims=True)
     sums = sum(ref[0:PANEL, :].astype(jnp.float32) for ref in ins)
     panel = panel_ref[...].astype(jnp.float32)
-    out_ref[...] = ((sums + panel) / (column + 1.0)).astype(jnp.bfloat16)
+    out_ref[...] = ((sums + panel) * (1.0 / (column + 1.0))).astype(jnp.bfloat16)
 
 
 def shards(coarse_cluster_means, fine_cluster_means, block_panel_candidates, softmax_heat):
@@ -244,7 +257,7 @@
         in_specs=[vmem],
         out_specs=vmem,
         out_shape=jax.ShapeDtypeStruct((32, SLICE, BLOCK), jnp.bfloat16),
-        compiler_params=pltpu.CompilerParams(vmem_limit_bytes=16 << 20),
+        compiler_params=pltpu.CompilerParams(vmem_limit_bytes=8 << 20),
         name="turn",
     )
     power, top, stat = pl.pallas_call(
@@ -256,45 +269,50 @@
             jax.ShapeDtypeStruct((PANELS, 8, SLOTS * BLOCK), jnp.float32),
             jax.ShapeDtypeStruct((2 * STATS, BLOCK), jnp.float32),
         ],
-        compiler_params=pltpu.CompilerParams(vmem_limit_bytes=24 << 20),
+        compiler_params=pltpu.CompilerParams(vmem_limit_bytes=8 << 20),
         name="scores",
     )(here, count, table, place, scale, turn(own), turn(oth), *stacks)
     stat_other = moved(stat, "c", 1)
 
-    sums = pl.pallas_call(
-        sum_kernel,
-        in_specs=[smem] * 4 + [vmem] * 6,
-        out_specs=[vmem] * 5,
-        out_shape=[jax.ShapeDtypeStruct((PACK, DIM), jnp.bfloat16)] * 4
-        + [jax.ShapeDtypeStruct((BLOCKS, BLOCK), jnp.float32)],
-        scratch_shapes=[
-            pltpu.VMEM((STATS, BLOCK), jnp.float32),
-            pltpu.VMEM((32, PANEL), jnp.float32),
-        ],
-        compiler_params=pltpu.CompilerParams(vmem_limit_bytes=24 << 20),
-        name="sums",
-    )(here, count, table, place, own, oth, power, top, stat, stat_other)
-    packs, norm = sums[0:4], sums[4]
+    def sums_of(wanted):
+        return pl.pallas_call(
+            functools.partial(sum_kernel, wanted),
+            in_specs=[smem] * 4 + [vmem] * 6,
+            out_specs=[vmem] * 3,
+            out_shape=[jax.ShapeDtypeStruct((PACK, DIM), jnp.bfloat16)] * 2
+            + [jax.ShapeDtypeStruct((BLOCKS, BLOCK), jnp.float32)],
+            scratch_shapes=[
+                pltpu.VMEM((STATS, BLOCK), jnp.float32),
+                pltpu.VMEM((32, PANEL), jnp.float32),
+            ],
+            compiler_params=pltpu.CompilerParams(vmem_limit_bytes=8 << 20),
+            name="sums",
+        )(here, count, table, place, own, oth, power, top, stat, stat_other)
+
+    pack_far, pack_next, norm = sums_of((2, 1))
+    pack_last, pack_own, _ = sums_of((3, 0))
+    packs = [pack_own, pack_next, pack_far, pack_last]
     got = [packs[0]] + [shifted(packs[d], True, -d) for d in (1, 2, 3)]
     chunks = pl.pallas_call(
         fold_kernel,
         in_specs=[vmem] * 4,
         out_specs=[vmem] * 4,
         out_shape=[jax.ShapeDtypeStruct((CHUNK, DIM), jnp.bfloat16)] * 4,
-        compiler_params=pltpu.CompilerParams(vmem_limit_bytes=16 << 20),
+        compiler_params=pltpu.CompilerParams(vmem_limit_bytes=8 << 20),
         name="fold",
     )(*got)
-    last = [chunks[0]] + [shifted(chunks[d], False, -d) for d in (1, 2, 3)]
+    norm, chunks = lax.optimization_barrier((norm, chunks))
+    last = [homeward(chunks[d], d) for d in range(4)]
+    part_norm = lax.dynamic_slice_in_dim(norm, c * 8, 8, axis=0)
+    log_norm = swapped(part_norm).reshape(8 * BLOCK)
     revised = pl.pallas_call(
         finish_kernel,
         in_specs=[vmem] * 5,
         out_specs=vmem,
         out_shape=jax.ShapeDtypeStruct((PANEL, DIM), jnp.bfloat16),
         name="finish",
-    )(panel, *last)
-    norm, revised = lax.optimization_barrier((norm, revised))
-    part_norm = lax.dynamic_slice_in_dim(norm, c * 8, 8, axis=0)
-    return (swapped(revised), swapped(part_norm).reshape(8 * BLOCK))
+    )(fine_cluster_means, *last)
+    return (revised, log_norm)
 
 
 def solution(mesh):

time: 133 us -> 128 us (0.962)
  waiting for transfers between devices: 60.1 us -> 50.9 us
  Pallas kernels: 23.2 us -> 26.3 us
    ppermute x12 -> x9, waiting for transfers between devices: 41.1 us -> 28.6 us  [shifted(): return lax.ppermute(value, ('c', 'z', 'x'), pairs)]
    ppermute x0 -> x4, starting transfers between devices: none -> 10.2 us  [homeward(): return lax.ppermute(value, ('c', 'yl', 'z', 'x'), pairs)]
    ppermute x4 -> x3, starting transfers between devices: 17.7 us -> 12.1 us  [swapped(): return lax.ppermute(value, ('c', 'yl'), [(0, 0), (1, 2), (2, 1), (3, 3)])]
    ppermute x12 -> x9, starting transfers between devices: 15.4 us -> 12.2 us  [shifted(): return lax.ppermute(value, ('c', 'z', 'x'), pairs)]
    pallas_call x1 -> x2, Pallas kernels: 7.31 us -> 10 us  [sums_of(): pl.pallas_call(functools.partial(sum_kernel, wanted), in_specs=[smem] * 4...]
    ppermute x0 -> x4, waiting for transfers between devices: none -> 2.19 us  [homeward(): return lax.ppermute(value, ('c', 'yl', 'z', 'x'), pairs)]
    ppermute x4 -> x3, waiting for transfers between devices: 4.12 us -> 5.28 us  [swapped(): return lax.ppermute(value, ('c', 'yl'), [(0, 0), (1, 2), (2, 1), (3, 3)])]
    unnamed x25 -> x22, local copies, waits for them, and re-layouts: 4.79 us -> 4.09 us
  transfers between devices with their start and end apart: 22 -> 22, of which waited for: 11 -> 10; matrix products, arithmetic and copies ran while one was open for 2% -> 2% of each run, Pallas kernels for 3% -> 7%
where the time goes in v4:
time: 128 us; the launch traced here: 127 us
  waiting for transfers between devices  50.9 us (40%)
  starting transfers between devices  41.7 us (33%)
  Pallas kernels  26.3 us (21%)
  local copies, waits for them, and re-layouts  5.86 us (5%)
  between operations  1.64 us (1%)
    ppermute x9, waiting for transfers between devices, shifted(): return lax.ppermute(value, ('c', 'z', 'x'), pairs)  28.6 us
    ppermute x6, waiting for transfers between devices, moved(): lax.ppermute(value, axis, [(i, (i - by) % size) for i in range(size)])  14.9 us
    ppermute x9, starting transfers between devices, shifted(): return lax.ppermute(value, ('c', 'z', 'x'), pairs)  12.2 us
    ppermute x3, starting transfers between devices, swapped(): return lax.ppermute(value, ('c', 'yl'), [(0, 0), (1, 2), (2, 1), (3, 3)])  12.1 us
    ppermute x4, starting transfers between devices, homeward(): return lax.ppermute(value, ('c', 'yl', 'z', 'x'), pairs)  10.2 us
    pallas_call x2, Pallas kernels, sums_of(): pl.pallas_call(functools.partial(sum_kernel, wanted), in_specs=[smem] * 4...  10 us
    pallas_call x1, Pallas kernels, shards(): pl.pallas_call(score_kernel, in_specs=[smem] * 5 + [vmem] * 6, out_specs=...  9.93 us
    ppermute x6, starting transfers between devices, moved(): lax.ppermute(value, axis, [(i, (i - by) % size) for i in range(size)])  7.31 us
  transfers between devices with their start and end apart: 22, of which 10 were waited for; matrix products, arithmetic and copies ran while one was open for 2% of the time, Pallas kernels for 7%

profile of v4, /device:TPU:1, one launch (start us, length us, event | category | flops | bytes accessed | tf_op | source)
XLA Modules:
  0.0 127.5 jit_solution(16766206055720978880)
XLA Ops:
  0.6 4.6 %collective-permute-start = (bf16[128,1024]{1,0:T(8,128)(2,1)}, bf16[128,1024]{1,0:T(8,128)(2,1)S(1)}, u32[]{:S(2)}, u32[]{:S(2)}) collective-permute-start(bf16[128,1024]{1,0:T(8,128)(2,1)} %panel_ref.1), channel_id=1, source_target_pairs={{0,0},{16,32},{32,16},{48,48},{1,1},{17,33},{33,17},{49,49},{2,2},... | collective-permute-start | bytes 786440 | tf_op jit(solution)/shard_map/ppermute | solution.py:33
  5.3 1.7 %dynamic-slice_bitcast_fusion = (bf16[8,128,256]{2,1,0:T(8,128)(2,1)S(1)}, bf16[8,128,256]{2,1,0:T(8,128)(2,1)S(1)}, bf16[8,128,256]{2,1,0:T(8,128)(2,1)S(1)}, bf16[8,128,256]{2,1,0:T(8,128)(2,1)S(1)}) fusion(bf16[4,8,128,256]{3,2,1,0:T(8,128)(2,1)} %bitcast.22, s32[]{:T(128)S(6)} %select_n.144, s32[]{:T(128)S(6)} %select_n.142, s32[]{:T(128)S(6)} %select_n.140, ...), kind=kLoop, calls=%fused_computation.1 | loop fusion | bytes 4194320 | tf_op jit(solution)/shard_map/jit(dynamic_index_in_dim)/squeeze | solution.py:231
  7.0 0.1 collective-permute-start.5
  7.1 2.7 %collective-permute-start.4 = (bf16[8,128,256]{2,1,0:T(8,128)(2,1)S(1)}, bf16[8,128,256]{2,1,0:T(8,128)(2,1)S(1)}, u32[]{:S(2)}, u32[]{:S(2)}) collective-permute-start(bf16[8,128,256]{2,1,0:T(8,128)(2,1)S(1)} %get-tuple-element.58), channel_id=1, source_target_pairs={{0,80},{16,0},{64,16},{80,64},{1,81},{17,1},{65,17},{81,65},{2,82}... | collective-permute-start | bytes 1572872 | tf_op jit(solution)/shard_map/ppermute | solution.py:29
  9.7 0.0 collective-permute-done
  9.7 1.2 collective-permute-start.3
  11.0 2.5 %collective-permute-start.2 = (bf16[128,1024]{1,0:T(8,128)(2,1)S(1)}, bf16[128,1024]{1,0:T(8,128)(2,1)S(1)}, u32[]{:S(2)}, u32[]{:S(2)}) collective-permute-start(bf16[128,1024]{1,0:T(8,128)(2,1)S(1)} %collective-permute-done), channel_id=1, source_target_pairs={{8,0},{9,1},{10,2},{11,3},{12,4},{13,5},{14,6},{15,7},{0,8},{1,9},... | collective-permute-start | bytes 786440 | tf_op jit(solution)/shard_map/ppermute | solution.py:71
  13.4 1.2 collective-permute-start.1
  14.6 1.9 %collective-permute-done.3 = bf16[128,1024]{1,0:T(8,128)(2,1)S(1)} collective-permute-done((bf16[128,1024]{1,0:T(8,128)(2,1)S(1)}, bf16[128,1024]{1,0:T(8,128)(2,1)S(1)}, u32[]{:S(2)}, u32[]{:S(2)}) %collective-permute-start.3) | collective-permute-done | bytes 262176 | tf_op jit(solution)/shard_map/ppermute | solution.py:71
  16.5 5.5 %collective-permute-start.6 = (s32[8,8]{1,0:T(8,128)S(1)}, s32[8,8]{1,0:T(8,128)S(1)}, u32[]{:S(2)}, u32[]{:S(2)}) collective-permute-start(s32[8,8]{1,0:T(8,128)S(1)} %copy-done.8), channel_id=1, source_target_pairs={{0,0},{16,32},{32,16},{48,48},{1,1},{17,33},{33,17},{49,49},{2,2},... | collective-permute-start | bytes 776 | tf_op jit(solution)/shard_map/ppermute | solution.py:33
  22.0 0.0 collective-permute-done.2
  22.0 0.0 collective-permute-done.1
  22.1 0.1 pad_maximum_fusion.refs_0_
  22.2 1.1 collective-permute-done.6
  23.3 0.0 collective-permute-done.5
  23.3 0.0 collective-permute-done.4
  23.3 0.2 collective-permute-start.10
  23.5 2.5 %collective-permute-start.9 = (bf16[4,128,1024]{2,1,0:T(8,128)(2,1)S(1)}, bf16[4,128,1024]{2,1,0:T(8,128)(2,1)S(1)}, u32[]{:S(2)}, u32[]{:S(2)}) collective-permute-start(bf16[4,128,1024]{2,1,0:T(8,128)(2,1)S(1)} %pad_maximum_fusion.refs_0_), channel_id=1, source_target_pairs={{1,0},{2,1},{3,2},{0,3},{5,4},{6,5},{7,6},{4,7},{9,8},{10,9},{11,1... | collective-permute-start | bytes 3145736 | tf_op jit(solution)/shard_map/ppermute | solution.py:71
  26.0 2.5 %collective-permute-start.8 = (bf16[8,128,256]{2,1,0:T(8,128)(2,1)S(1)}, bf16[8,128,256]{2,1,0:T(8,128)(2,1)S(1)}, u32[]{:S(2)}, u32[]{:S(2)}) collective-permute-start(bf16[8,128,256]{2,1,0:T(8,128)(2,1)S(1)} %get-tuple-element.32), channel_id=1, source_target_pairs={{0,64},{16,80},{64,0},{80,16},{1,65},{17,81},{65,1},{81,17},{2,66}... | collective-permute-start | bytes 1572872 | tf_op jit(solution)/shard_map/ppermute | solution.py:29
  28.4 12.9 %collective-permute-done.8 = bf16[8,128,256]{2,1,0:T(8,128)(2,1)S(1)} collective-permute-done((bf16[8,128,256]{2,1,0:T(8,128)(2,1)S(1)}, bf16[8,128,256]{2,1,0:T(8,128)(2,1)S(1)}, u32[]{:S(2)}, u32[]{:S(2)}) %collective-permute-start.8) | collective-permute-done | bytes 524320 | tf_op jit(solution)/shard_map/ppermute | solution.py:29
  41.3 0.0 collective-permute-done.10.refs_3_
  41.3 1.0 copy-done
  42.3 0.0 collective-permute-done.9.refs_1_
  42.3 1.0 copy-done.2
  43.5 0.5 collective-permute-start.11
  44.6 1.1 collective-permute-start.12
  45.8 0.1 pad_maximum_fusion.1.scale_ref
  45.8 0.1 pad_add_fusion.here_ref
  45.9 0.7 collective-permute-start.7
  46.6 1.2 collective-permute-done.7
  47.8 0.1 copy.16
  47.9 0.2 reduce_window_sum.11
  48.1 0.1 convert_reduce_fusion.count_ref
  48.2 0.4 select_reduce_fusion
  48.6 1.0 turn.2.own
  49.6 0.0 collective-permute-done.11.ref.oth
  49.6 2.7 %turn.3.oth = bf16[32,256,128]{2,1,0:T(8,128)(2,1)S(1)} custom-call(bf16[32,128,256]{2,1,0:T(8,128)(2,1)} %collective-permute-done.11.ref.oth), custom_call_target="tpu_custom_call" | custom-call | tf_op jit(solution)/shard_map/turn/pallas_call | solution.py:274
  52.3 8.0 %collective-permute-done.12.refs_2_ = bf16[4,128,1024]{2,1,0:T(8,128)(2,1)} collective-permute-done((bf16[4,128,1024]{2,1,0:T(8,128)(2,1)S(1)}, bf16[4,128,1024]{2,1,0:T(8,128)(2,1)}, u32[]{:S(2)}, u32[]{:S(2)}) %collective-permute-start.12) | collective-permute-done | bytes 1048608 | tf_op jit(solution)/shard_map/ppermute | solution.py:71
  60.3 9.9 %scores.1 = (f32[16,128,1024]{2,1,0:T(8,128)S(1)}, f32[16,8,1024]{2,1,0:T(8,128)S(1)}, f32[48,128]{1,0:T(8,128)S(1)}) custom-call(s32[2]{0:T(128)S(1)} %pad_add_fusion.here_ref, s32[16]{0:T(128)S(1)} %convert_reduce_fusion.count_ref, s32[16,8]{1,0:T(8,128)S(1)} %get-tuple-element.61.list_ref, s32[16,8]{1,0:T(8,128)S(1)} %get-tuple-element.60.place_ref, ...), custom_call_target="tpu_custom_call" | custom-call | tf_op jit(solution)/shard_map/scores/pallas_call | solution.py:263
  70.2 1.0 collective-permute-start.13
  71.2 0.8 collective-permute-done.13.other_ref
  72.1 4.8 %sums.2 = (bf16[520,1024]{1,0:T(8,128)(2,1)S(1)}, bf16[520,1024]{1,0:T(8,128)(2,1)S(1)}, f32[16,128]{1,0:T(8,128)S(1)}) custom-call(s32[2]{0:T(128)S(1)} %pad_add_fusion.here_ref, s32[16]{0:T(128)S(1)} %convert_reduce_fusion.count_ref, s32[16,8]{1,0:T(8,128)S(1)} %get-tuple-element.61.list_ref, s32[16,8]{1,0:T(8,128)S(1)} %get-tuple-element.60.place_ref, ...), custom_call_target="tpu_custom_call" | custom-call | tf_op jit(solution)/shard_map/sums/pallas_call | solution.py:278
  76.9 0.1 collective-permute-start.14
  76.9 2.0 %collective-permute-start.15 = (bf16[520,1024]{1,0:T(8,128)(2,1)S(1)}, bf16[520,1024]{1,0:T(8,128)(2,1)S(1)}, u32[]{:S(2)}, u32[]{:S(2)}) collective-permute-start(bf16[520,1024]{1,0:T(8,128)(2,1)S(1)} %get-tuple-element.45), channel_id=1, source_target_pairs={{8,0},{9,1},{10,2},{11,3},{12,4},{13,5},{14,6},{15,7},{0,8},{1,9},... | collective-permute-start | bytes 3194888 | tf_op jit(solution)/shard_map/ppermute | solution.py:71
  78.9 5.2 %sums.3 = (bf16[520,1024]{1,0:T(8,128)(2,1)S(1)}, bf16[520,1024]{1,0:T(8,128)(2,1)S(1)}, f32[16,128]{1,0:T(8,128)}) custom-call(s32[2]{0:T(128)S(1)} %pad_add_fusion.here_ref, s32[16]{0:T(128)S(1)} %convert_reduce_fusion.count_ref, s32[16,8]{1,0:T(8,128)S(1)} %get-tuple-element.61.list_ref, s32[16,8]{1,0:T(8,128)S(1)} %get-tuple-element.60.place_ref, ...), custom_call_target="tpu_custom_call" | custom-call | tf_op jit(solution)/shard_map/sums/pallas_call | solution.py:278
  84.1 1.5 %collective-permute-start.16 = (bf16[520,1024]{1,0:T(8,128)(2,1)S(1)}, bf16[520,1024]{1,0:T(8,128)(2,1)S(1)}, u32[]{:S(2)}, u32[]{:S(2)}) collective-permute-start(bf16[520,1024]{1,0:T(8,128)(2,1)S(1)} %get-tuple-element.46), channel_id=1, source_target_pairs={{4,0},{5,1},{6,2},{7,3},{8,4},{9,5},{10,6},{11,7},{12,8},{13,9},{1... | collective-permute-start | bytes 3194888 | tf_op jit(solution)/shard_map/ppermute | solution.py:71
  85.6 18.0 %collective-permute-done.14.refs_1_ = bf16[520,1024]{1,0:T(8,128)(2,1)S(1)} collective-permute-done((bf16[520,1024]{1,0:T(8,128)(2,1)S(1)}, bf16[520,1024]{1,0:T(8,128)(2,1)S(1)}, u32[]{:S(2)}, u32[]{:S(2)}) %collective-permute-start.14) | collective-permute-done | bytes 1064992 | tf_op jit(solution)/shard_map/ppermute | solution.py:71
  103.7 0.0 collective-permute-done.15.refs_2_
  103.7 0.6 collective-permute-done.16.refs_3_
  104.3 0.5 fold.1
  104.8 3.5 %collective-permute-start.17 = (bf16[136,1024]{1,0:T(8,128)(2,1)S(1)}, bf16[136,1024]{1,0:T(8,128)(2,1)S(1)}, u32[]{:S(2)}, u32[]{:S(2)}) collective-permute-start(bf16[136,1024]{1,0:T(8,128)(2,1)S(1)} %get-tuple-element.51), channel_id=1, source_target_pairs={{0,0},{1,1},{2,2},{3,3},{4,4},{5,5},{6,6},{7,7},{8,8},{9,9},{10,10... | collective-permute-start | bytes 835592 | tf_op jit(solution)/shard_map/ppermute | solution.py:83
  108.3 0.4 collective-permute-start.18
  108.7 3.3 %collective-permute-start.19 = (bf16[136,1024]{1,0:T(8,128)(2,1)S(1)}, bf16[136,1024]{1,0:T(8,128)(2,1)S(1)}, u32[]{:S(2)}, u32[]{:S(2)}) collective-permute-start(bf16[136,1024]{1,0:T(8,128)(2,1)S(1)} %get-tuple-element.53), channel_id=1, source_target_pairs={{0,2},{1,3},{2,0},{3,1},{4,6},{5,7},{6,4},{7,5},{8,10},{9,11},{10,... | collective-permute-start | bytes 835592 | tf_op jit(solution)/shard_map/ppermute | solution.py:83
  112.1 2.9 %collective-permute-start.20 = (bf16[136,1024]{1,0:T(8,128)(2,1)S(1)}, bf16[136,1024]{1,0:T(8,128)(2,1)S(1)}, u32[]{:S(2)}, u32[]{:S(2)}) collective-permute-start(bf16[136,1024]{1,0:T(8,128)(2,1)S(1)} %get-tuple-element.54), channel_id=1, source_target_pairs={{0,3},{1,0},{2,1},{3,2},{4,7},{5,4},{6,5},{7,6},{8,11},{9,8},{10,9... | collective-permute-start | bytes 835592 | tf_op jit(solution)/shard_map/ppermute | solution.py:83
  115.0 1.9 %collective-permute-start.21 = (f32[8,128]{1,0:T(8,128)S(1)}, f32[8,128]{1,0:T(8,128)S(1)}, u32[]{:S(2)}, u32[]{:S(2)}) collective-permute-start(f32[8,128]{1,0:T(8,128)S(1)} %constant_dynamic-slice_fusion), channel_id=1, source_target_pairs={{0,0},{16,32},{32,16},{48,48},{1,1},{17,33},{33,17},{49,49},{2,2},... | collective-permute-start | bytes 12296 | tf_op jit(solution)/shard_map/ppermute | solution.py:33
  116.9 4.2 %collective-permute-done.21 = f32[8,128]{1,0:T(8,128)S(1)} collective-permute-done((f32[8,128]{1,0:T(8,128)S(1)}, f32[8,128]{1,0:T(8,128)S(1)}, u32[]{:S(2)}, u32[]{:S(2)}) %collective-permute-start.21) | collective-permute-done | bytes 4128 | tf_op jit(solution)/shard_map/ppermute | solution.py:33
  121.1 0.0 collective-permute-done.17.refs_0_
  121.1 0.0 collective-permute-done.18.refs_1_
  121.1 2.2 %collective-permute-done.19.refs_2_ = bf16[136,1024]{1,0:T(8,128)(2,1)S(1)} collective-permute-done((bf16[136,1024]{1,0:T(8,128)(2,1)S(1)}, bf16[136,1024]{1,0:T(8,128)(2,1)S(1)}, u32[]{:S(2)}, u32[]{:S(2)}) %collective-permute-start.19) | collective-permute-done | bytes 278560 | tf_op jit(solution)/shard_map/ppermute | solution.py:83
  123.3 0.0 collective-permute-done.20.refs_3_
  123.3 0.7 copy-done.6
  124.0 0.7 copy-done.7
  124.7 2.2 %finish.1 = bf16[128,1024]{1,0:T(8,128)(2,1)} custom-call(bf16[128,1024]{1,0:T(8,128)(2,1)} %panel_ref.1, bf16[136,1024]{1,0:T(8,128)(2,1)} %copy-done.4, bf16[136,1024]{1,0:T(8,128)(2,1)} %copy-done.5, bf16[136,1024]{1,0:T(8,128)(2,1)} %copy-done.6, bf16[136,1024]{1,0:T(8,128)(2,1)} %copy-done.7), custom_call_target="tpu_custom_call" | custom-call | tf_op jit(solution)/shard_map/finish/pallas_call | solution.py:308
  126.9 0.6 copy.23
  (25 shorter events, 0.3 us)
Async XLA Ops:
  0.6 9.1 %collective-permute-start = (bf16[128,1024]{1,0:T(8,128)(2,1)}, bf16[128,1024]{1,0:T(8,128)(2,1)S(1)}, u32[]{:S(2)}, u32[]{:S(2)}) collective-permute-start(bf16[128,1024]{1,0:T(8,128)(2,1)} %panel_ref.1), channel_id=1, source_target_pairs={{0,0},{16,32},{32,16},{48,48},{1,1},{17,33},{33,17},{49,49},{2,2},... | collective-permute-start | bytes 786440 | tf_op jit(solution)/shard_map/ppermute | solution.py:33
  5.3 11.2 %copy-start.8 = (s32[8,8]{1,0:T(8,128)S(1)}, s32[8,8]{1,0:T(8,128)}, u32[]{:S(2)}) copy-start(s32[8,8]{1,0:T(8,128)} %param.6) | copy-start | bytes 772
  7.0 16.3 %collective-permute-start.5 = (bf16[8,128,256]{2,1,0:T(8,128)(2,1)S(1)}, bf16[8,128,256]{2,1,0:T(8,128)(2,1)S(1)}, u32[]{:S(2)}, u32[]{:S(2)}) collective-permute-start(bf16[8,128,256]{2,1,0:T(8,128)(2,1)S(1)} %get-tuple-element.56), channel_id=1, source_target_pairs={{0,16},{16,64},{64,80},{80,0},{1,17},{17,65},{65,81},{81,1},{2,18}... | collective-permute-start | bytes 1572872 | tf_op jit(solution)/shard_map/ppermute | solution.py:29
  7.1 16.2 %collective-permute-start.4 = (bf16[8,128,256]{2,1,0:T(8,128)(2,1)S(1)}, bf16[8,128,256]{2,1,0:T(8,128)(2,1)S(1)}, u32[]{:S(2)}, u32[]{:S(2)}) collective-permute-start(bf16[8,128,256]{2,1,0:T(8,128)(2,1)S(1)} %get-tuple-element.58), channel_id=1, source_target_pairs={{0,80},{16,0},{64,16},{80,64},{1,81},{17,1},{65,17},{81,65},{2,82}... | collective-permute-start | bytes 1572872 | tf_op jit(solution)/shard_map/ppermute | solution.py:29
  9.7 6.7 %collective-permute-start.3 = (bf16[128,1024]{1,0:T(8,128)(2,1)S(1)}, bf16[128,1024]{1,0:T(8,128)(2,1)S(1)}, u32[]{:S(2)}, u32[]{:S(2)}) collective-permute-start(bf16[128,1024]{1,0:T(8,128)(2,1)S(1)} %collective-permute-done), channel_id=1, source_target_pairs={{12,0},{13,1},{14,2},{15,3},{0,4},{1,5},{2,6},{3,7},{4,8},{5,9},{6... | collective-permute-start | bytes 786440 | tf_op jit(solution)/shard_map/ppermute | solution.py:71
  11.0 11.1 %collective-permute-start.2 = (bf16[128,1024]{1,0:T(8,128)(2,1)S(1)}, bf16[128,1024]{1,0:T(8,128)(2,1)S(1)}, u32[]{:S(2)}, u32[]{:S(2)}) collective-permute-start(bf16[128,1024]{1,0:T(8,128)(2,1)S(1)} %collective-permute-done), channel_id=1, source_target_pairs={{8,0},{9,1},{10,2},{11,3},{12,4},{13,5},{14,6},{15,7},{0,8},{1,9},... | collective-permute-start | bytes 786440 | tf_op jit(solution)/shard_map/ppermute | solution.py:71
  13.4 8.6 %collective-permute-start.1 = (bf16[128,1024]{1,0:T(8,128)(2,1)S(1)}, bf16[128,1024]{1,0:T(8,128)(2,1)S(1)}, u32[]{:S(2)}, u32[]{:S(2)}) collective-permute-start(bf16[128,1024]{1,0:T(8,128)(2,1)S(1)} %collective-permute-done), channel_id=1, source_target_pairs={{4,0},{5,1},{6,2},{7,3},{8,4},{9,5},{10,6},{11,7},{12,8},{13,9},{1... | collective-permute-start | bytes 786440 | tf_op jit(solution)/shard_map/ppermute | solution.py:71
  16.5 6.8 %collective-permute-start.6 = (s32[8,8]{1,0:T(8,128)S(1)}, s32[8,8]{1,0:T(8,128)S(1)}, u32[]{:S(2)}, u32[]{:S(2)}) collective-permute-start(s32[8,8]{1,0:T(8,128)S(1)} %copy-done.8), channel_id=1, source_target_pairs={{0,0},{16,32},{32,16},{48,48},{1,1},{17,33},{33,17},{49,49},{2,2},... | collective-permute-start | bytes 776 | tf_op jit(solution)/shard_map/ppermute | solution.py:33
  23.3 18.0 %collective-permute-start.10 = (bf16[4,128,1024]{2,1,0:T(8,128)(2,1)S(1)}, bf16[4,128,1024]{2,1,0:T(8,128)(2,1)S(1)}, u32[]{:S(2)}, u32[]{:S(2)}) collective-permute-start(bf16[4,128,1024]{2,1,0:T(8,128)(2,1)S(1)} %pad_maximum_fusion.refs_0_), channel_id=1, source_target_pairs={{3,0},{0,1},{1,2},{2,3},{7,4},{4,5},{5,6},{6,7},{11,8},{8,9},{9,10... | collective-permute-start | bytes 3145736 | tf_op jit(solution)/shard_map/ppermute | solution.py:71
  23.5 18.8 %collective-permute-start.9 = (bf16[4,128,1024]{2,1,0:T(8,128)(2,1)S(1)}, bf16[4,128,1024]{2,1,0:T(8,128)(2,1)S(1)}, u32[]{:S(2)}, u32[]{:S(2)}) collective-permute-start(bf16[4,128,1024]{2,1,0:T(8,128)(2,1)S(1)} %pad_maximum_fusion.refs_0_), channel_id=1, source_target_pairs={{1,0},{2,1},{3,2},{0,3},{5,4},{6,5},{7,6},{4,7},{9,8},{10,9},{11,1... | collective-permute-start | bytes 3145736 | tf_op jit(solution)/shard_map/ppermute | solution.py:71
  26.0 15.3 %collective-permute-start.8 = (bf16[8,128,256]{2,1,0:T(8,128)(2,1)S(1)}, bf16[8,128,256]{2,1,0:T(8,128)(2,1)S(1)}, u32[]{:S(2)}, u32[]{:S(2)}) collective-permute-start(bf16[8,128,256]{2,1,0:T(8,128)(2,1)S(1)} %get-tuple-element.32), channel_id=1, source_target_pairs={{0,64},{16,80},{64,0},{80,16},{1,65},{17,81},{65,1},{81,17},{2,66}... | collective-permute-start | bytes 1572872 | tf_op jit(solution)/shard_map/ppermute | solution.py:29
  41.3 1.0 copy-start
  42.3 1.0 copy-start.2
  43.5 6.1 %collective-permute-start.11 = (bf16[32,128,256]{2,1,0:T(8,128)(2,1)S(1)}, bf16[32,128,256]{2,1,0:T(8,128)(2,1)}, u32[]{:S(2)}, u32[]{:S(2)}) collective-permute-start(bf16[32,128,256]{2,1,0:T(8,128)(2,1)S(1)} %constant_dynamic-update-slice_fusion.ref.own), channel_id=1, source_target_pairs={{0,32},{32,0},{1,33},{33,1},{2,34},{34,2},{3,35},{35,3},{4,36},{36... | collective-permute-start | bytes 6291464 | tf_op jit(solution)/shard_map/ppermute | solution.py:29
  44.6 15.6 %collective-permute-start.12 = (bf16[4,128,1024]{2,1,0:T(8,128)(2,1)S(1)}, bf16[4,128,1024]{2,1,0:T(8,128)(2,1)}, u32[]{:S(2)}, u32[]{:S(2)}) collective-permute-start(bf16[4,128,1024]{2,1,0:T(8,128)(2,1)S(1)} %pad_maximum_fusion.refs_0_), channel_id=1, source_target_pairs={{2,0},{3,1},{0,2},{1,3},{6,4},{7,5},{4,6},{5,7},{10,8},{11,9},{8,1... | collective-permute-start | bytes 3145736 | tf_op jit(solution)/shard_map/ppermute | solution.py:71
  45.9 1.8 %collective-permute-start.7 = (s32[8,8]{1,0:T(8,128)S(1)}, s32[8,8]{1,0:T(8,128)S(1)}, u32[]{:S(2)}, u32[]{:S(2)}) collective-permute-start(s32[8,8]{1,0:T(8,128)S(1)} %collective-permute-done.6), channel_id=1, source_target_pairs={{0,32},{32,0},{1,33},{33,1},{2,34},{34,2},{3,35},{35,3},{4,36},{36... | collective-permute-start | bytes 776 | tf_op jit(solution)/shard_map/ppermute | solution.py:29
  49.5 10.7 %copy-start.1 = (bf16[4,128,1024]{2,1,0:T(8,128)(2,1)S(1)}, bf16[4,128,1024]{2,1,0:T(8,128)(2,1)}, u32[]{:S(2)}) copy-start(bf16[4,128,1024]{2,1,0:T(8,128)(2,1)} %copy-done) | copy-start | bytes 3145732
  49.5 10.7 %copy-start.3 = (bf16[4,128,1024]{2,1,0:T(8,128)(2,1)S(1)}, bf16[4,128,1024]{2,1,0:T(8,128)(2,1)}, u32[]{:S(2)}) copy-start(bf16[4,128,1024]{2,1,0:T(8,128)(2,1)} %copy-done.2) | copy-start | bytes 3145732
  70.2 1.8 %collective-permute-start.13 = (f32[48,128]{1,0:T(8,128)S(1)}, f32[48,128]{1,0:T(8,128)S(1)}, u32[]{:S(2)}, u32[]{:S(2)}) collective-permute-start(f32[48,128]{1,0:T(8,128)S(1)} %get-tuple-element.41.mine_ref), channel_id=1, source_target_pairs={{0,32},{32,0},{1,33},{33,1},{2,34},{34,2},{3,35},{35,3},{4,36},{36... | collective-permute-start | bytes 73736 | tf_op jit(solution)/shard_map/ppermute | solution.py:29
  76.9 26.8 %collective-permute-start.14 = (bf16[520,1024]{1,0:T(8,128)(2,1)S(1)}, bf16[520,1024]{1,0:T(8,128)(2,1)S(1)}, u32[]{:S(2)}, u32[]{:S(2)}) collective-permute-start(bf16[520,1024]{1,0:T(8,128)(2,1)S(1)} %get-tuple-element.44), channel_id=1, source_target_pairs={{12,0},{13,1},{14,2},{15,3},{0,4},{1,5},{2,6},{3,7},{4,8},{5,9},{6... | collective-permute-start | bytes 3194888 | tf_op jit(solution)/shard_map/ppermute | solution.py:71
  76.9 26.7 %collective-permute-start.15 = (bf16[520,1024]{1,0:T(8,128)(2,1)S(1)}, bf16[520,1024]{1,0:T(8,128)(2,1)S(1)}, u32[]{:S(2)}, u32[]{:S(2)}) collective-permute-start(bf16[520,1024]{1,0:T(8,128)(2,1)S(1)} %get-tuple-element.45), channel_id=1, source_target_pairs={{8,0},{9,1},{10,2},{11,3},{12,4},{13,5},{14,6},{15,7},{0,8},{1,9},... | collective-permute-start | bytes 3194888 | tf_op jit(solution)/shard_map/ppermute | solution.py:71
  84.1 20.2 %collective-permute-start.16 = (bf16[520,1024]{1,0:T(8,128)(2,1)S(1)}, bf16[520,1024]{1,0:T(8,128)(2,1)S(1)}, u32[]{:S(2)}, u32[]{:S(2)}) collective-permute-start(bf16[520,1024]{1,0:T(8,128)(2,1)S(1)} %get-tuple-element.46), channel_id=1, source_target_pairs={{4,0},{5,1},{6,2},{7,3},{8,4},{9,5},{10,6},{11,7},{12,8},{13,9},{1... | collective-permute-start | bytes 3194888 | tf_op jit(solution)/shard_map/ppermute | solution.py:71
  104.8 16.3 %collective-permute-start.17 = (bf16[136,1024]{1,0:T(8,128)(2,1)S(1)}, bf16[136,1024]{1,0:T(8,128)(2,1)S(1)}, u32[]{:S(2)}, u32[]{:S(2)}) collective-permute-start(bf16[136,1024]{1,0:T(8,128)(2,1)S(1)} %get-tuple-element.51), channel_id=1, source_target_pairs={{0,0},{1,1},{2,2},{3,3},{4,4},{5,5},{6,6},{7,7},{8,8},{9,9},{10,10... | collective-permute-start | bytes 835592 | tf_op jit(solution)/shard_map/ppermute | solution.py:83
  108.3 12.8 %collective-permute-start.18 = (bf16[136,1024]{1,0:T(8,128)(2,1)S(1)}, bf16[136,1024]{1,0:T(8,128)(2,1)S(1)}, u32[]{:S(2)}, u32[]{:S(2)}) collective-permute-start(bf16[136,1024]{1,0:T(8,128)(2,1)S(1)} %get-tuple-element.52), channel_id=1, source_target_pairs={{0,1},{1,2},{2,3},{3,0},{4,5},{5,6},{6,7},{7,4},{8,9},{9,10},{10,1... | collective-permute-start | bytes 835592 | tf_op jit(solution)/shard_map/ppermute | solution.py:83
  108.7 14.5 %collective-permute-start.19 = (bf16[136,1024]{1,0:T(8,128)(2,1)S(1)}, bf16[136,1024]{1,0:T(8,128)(2,1)S(1)}, u32[]{:S(2)}, u32[]{:S(2)}) collective-permute-start(bf16[136,1024]{1,0:T(8,128)(2,1)S(1)} %get-tuple-element.53), channel_id=1, source_target_pairs={{0,2},{1,3},{2,0},{3,1},{4,6},{5,7},{6,4},{7,5},{8,10},{9,11},{10,... | collective-permute-start | bytes 835592 | tf_op jit(solution)/shard_map/ppermute | solution.py:83
  112.1 11.2 %collective-permute-start.20 = (bf16[136,1024]{1,0:T(8,128)(2,1)S(1)}, bf16[136,1024]{1,0:T(8,128)(2,1)S(1)}, u32[]{:S(2)}, u32[]{:S(2)}) collective-permute-start(bf16[136,1024]{1,0:T(8,128)(2,1)S(1)} %get-tuple-element.54), channel_id=1, source_target_pairs={{0,3},{1,0},{2,1},{3,2},{4,7},{5,4},{6,5},{7,6},{8,11},{9,8},{10,9... | collective-permute-start | bytes 835592 | tf_op jit(solution)/shard_map/ppermute | solution.py:83
  115.0 6.1 %collective-permute-start.21 = (f32[8,128]{1,0:T(8,128)S(1)}, f32[8,128]{1,0:T(8,128)S(1)}, u32[]{:S(2)}, u32[]{:S(2)}) collective-permute-start(f32[8,128]{1,0:T(8,128)S(1)} %constant_dynamic-slice_fusion), channel_id=1, source_target_pairs={{0,0},{16,32},{32,16},{48,48},{1,1},{17,33},{33,17},{49,49},{2,2},... | collective-permute-start | bytes 12296 | tf_op jit(solution)/shard_map/ppermute | solution.py:33
  121.1 2.2 %copy-start.4 = (bf16[136,1024]{1,0:T(8,128)(2,1)}, bf16[136,1024]{1,0:T(8,128)(2,1)S(1)}, u32[]{:S(2)}) copy-start(bf16[136,1024]{1,0:T(8,128)(2,1)S(1)} %collective-permute-done.17.refs_0_) | copy-start | bytes 835588
  121.1 2.2 %copy-start.5 = (bf16[136,1024]{1,0:T(8,128)(2,1)}, bf16[136,1024]{1,0:T(8,128)(2,1)S(1)}, u32[]{:S(2)}) copy-start(bf16[136,1024]{1,0:T(8,128)(2,1)S(1)} %collective-permute-done.18.refs_1_) | copy-start | bytes 835588
  123.3 0.7 copy-start.6
  124.0 0.7 copy-start.7

commit v5 on v4

--- a/solution.py
+++ b/solution.py
@@ -16,6 +16,7 @@
 PANELS = 16
 SLOTS = 8
 Y = ("yh", "yl")
+ORDER = (0, 1, 3, 2)
 LOW = -1e30
 HIGH = 1e30
 LN2 = math.log(2.0)
@@ -91,16 +92,17 @@
     lax.fori_loop(0, 32, one, 0, unroll=4)
 
 
-def score_kernel(here_ref, count_ref, list_ref, place_ref, scale_ref, own, oth, *refs):
-    p_in = refs[0:4]
-    l_ref, top_ref, stat_ref = refs[4:7]
+def score_kernel(
+    base, here_ref, count_ref, list_ref, place_ref, scale_ref, own, oth, before_ref, *refs
+):
+    p_in, (l_ref, top_ref, stat_ref) = refs[:-3], refs[-3:]
     twice, once = scale_ref[0], scale_ref[1]
     parts = points_of(own, oth, here_ref[1])
-    stat_ref[0:STATS, :] = jnp.full((STATS, BLOCK), LOW, jnp.float32)
-    stat_ref[STATS : 2 * STATS, :] = jnp.zeros((STATS, BLOCK), jnp.float32)
-
-    def panel_step(i, p_ref, base):
-        r = base + i
+    stat_ref[...] = before_ref[...]
+
+    def panel_step(i, p_ref, start):
+        r = start + i
+        row = r - 4 * base
         panel32 = p_ref[i].astype(jnp.float32)
         sqnorm = jnp.sum(panel32 * panel32, axis=1, keepdims=True) * once
 
@@ -119,12 +121,12 @@
                 logit = jnp.dot(lhs, rhs, preferred_element_type=jnp.float32) * twice - sqnorm
                 top = jnp.maximum(old[:, lanes], jnp.max(logit, axis=0, keepdims=True))
                 power = jnp.exp2(logit - top)
-                l_ref[r, :, lanes] = power
+                l_ref[row, :, lanes] = power
                 tops.append(top)
                 adds.append(jnp.sum(power, axis=0, keepdims=True))
             new = jnp.concatenate(tops, axis=1)
             total = total * jnp.exp2(old - new) + jnp.concatenate(adds, axis=1)
-            top_ref[r, :, 0 : 2 * turns * BLOCK] = jnp.broadcast_to(new, (8, 2 * turns * BLOCK))
+            top_ref[row, :, 0 : 2 * turns * BLOCK] = jnp.broadcast_to(new, (8, 2 * turns * BLOCK))
             for j, block in enumerate(blocks):
                 lanes = slice(j * BLOCK, (j + 1) * BLOCK)
                 stat_ref[pl.ds(block, 1), :] = new[:, lanes]
@@ -132,18 +134,19 @@
 
         by_turns((count_ref[r] + 1) // 2, run)
 
-    for k in range(4):
-
-        def step(i, _, k=k):
-            panel_step(i, p_in[k], 4 * k)
+    for k, p_ref in enumerate(p_in):
+
+        def step(i, _, k=k, p_ref=p_ref):
+            panel_step(i, p_ref, 4 * (base + k))
             return 0
 
         lax.fori_loop(0, 4, step, 0)
 
 
 def sum_kernel(
-    wanted, here_ref, count_ref, list_ref, place_ref, own, oth, l_ref, top_ref, mine_ref, other_ref, *refs
+    wanted, here_ref, count_ref, list_ref, place_ref, own, oth, mine_ref, other_ref, *refs
 ):
+    scored, refs = ((refs[0], refs[1], 0), (refs[2], refs[3], 3)), refs[4:]
     outs, norm_ref, full_ref, mass_ref = dict(zip(wanted, refs[0:2])), refs[2], refs[3], refs[4]
     parts = points_of(own, oth, here_ref[1])
     m0, s0 = mine_ref[0:STATS, :], mine_ref[STATS : 2 * STATS, :]
@@ -155,8 +158,9 @@
     full_ref[...] = jnp.where(row < BLOCKS, norm, HIGH)
     mass_ref[...] = jnp.zeros_like(mass_ref)
 
-    def panel_step(k, _, d):
+    def panel_step(k, d, l_ref, top_ref, base):
         r = 4 * k + d
+        row = r - 4 * base
         rows = pl.multiple_of(k * PANEL, PANEL)
         turns = (count_ref[r] + 1) // 2
 
@@ -169,8 +173,8 @@
             places = [place_ref[r, n] for n in range(2 * turns)]
             norm = jnp.concatenate([full_ref[pl.ds(block, 1), :] for block in blocks], axis=1)
             lanes = slice(0, 2 * turns * BLOCK)
-            factor = jnp.exp2(top_ref[r, 0:1, lanes] - norm)
-            weight = (l_ref[r, :, lanes] * factor).astype(jnp.bfloat16)
+            factor = jnp.exp2(top_ref[row, 0:1, lanes] - norm)
+            weight = (l_ref[row, :, lanes] * factor).astype(jnp.bfloat16)
             sums = jnp.dot(weight, rows_of(parts, places, 1), preferred_element_type=jnp.float32)
             sums = sums.astype(jnp.bfloat16)
             for i, (_, _, offset) in enumerate(parts):
@@ -184,7 +188,12 @@
         return 0
 
     for d in wanted:
-        lax.fori_loop(0, 4, lambda k, _, d=d: panel_step(k, _, d), 0)
+        for l_ref, top_ref, base in scored:
+
+            def step(k, _, d=d, l_ref=l_ref, top_ref=top_ref, base=base):
+                return panel_step(k, d, l_ref, top_ref, base)
+
+            lax.fori_loop(base, 3 if base == 0 else 4, step, 0)
         outs[d][4 * PANEL :, :] = jnp.zeros((8, DIM), jnp.bfloat16)
         outs[d][4 * PANEL :, 0:PANEL] = mass_ref[8 * d : 8 * d + 8, :].astype(jnp.bfloat16)
 
@@ -235,13 +244,14 @@
     stack, own, mine = lax.optimization_barrier((stack, own, mine))
     own[2] = moved(own[2], Y, 2)
     other = moved(mine, "c", 1)
-    stacks = [stack] + [shifted(stack, False, d) for d in (1, 2, 3)]
-    own = jnp.concatenate(lax.optimization_barrier((own, stacks[1], stacks[3]))[0])
+    stacks = [stack] + [shifted(stack, False, d) for d in ORDER[1:]]
+    own = jnp.concatenate(lax.optimization_barrier((own, stacks[1], stacks[2]))[0])
     oth = moved(own, "c", 1)
 
     cands = jnp.where(c == 0, jnp.stack([mine, other]), jnp.stack([other, mine])).reshape(BLOCKS, 8)
     dz, dx = (cands // 4 % 4 - z) % 4, (cands % 4 - x) % 4
-    spot = jnp.where(c == 0, 4 * dx + dz, 4 * dz + dx)
+    d1, d2 = jnp.where(c == 0, dz, dx), jnp.where(c == 0, dx, dz)
+    spot = 4 * jnp.where(d2 >= 2, 5 - d2, d2) + d1
     spot = jnp.where(cands // 16 == c, spot, -1)
     hits = jnp.any(spot[None] == jnp.arange(PANELS, dtype=jnp.int32)[:, None, None], axis=2)
     order = jnp.cumsum(hits.astype(jnp.int32), axis=1) - 1
@@ -260,24 +270,30 @@
         compiler_params=pltpu.CompilerParams(vmem_limit_bytes=8 << 20),
         name="turn",
     )
-    power, top, stat = pl.pallas_call(
-        score_kernel,
-        in_specs=[smem] * 5 + [vmem] * 6,
-        out_specs=[vmem] * 3,
-        out_shape=[
-            jax.ShapeDtypeStruct((PANELS, PANEL, SLOTS * BLOCK), jnp.float32),
-            jax.ShapeDtypeStruct((PANELS, 8, SLOTS * BLOCK), jnp.float32),
-            jax.ShapeDtypeStruct((2 * STATS, BLOCK), jnp.float32),
-        ],
-        compiler_params=pltpu.CompilerParams(vmem_limit_bytes=8 << 20),
-        name="scores",
-    )(here, count, table, place, scale, turn(own), turn(oth), *stacks)
+    def scores_of(base, stat, held):
+        return pl.pallas_call(
+            functools.partial(score_kernel, base),
+            in_specs=[smem] * 5 + [vmem] * (3 + len(held)),
+            out_specs=[vmem] * 3,
+            out_shape=[
+                jax.ShapeDtypeStruct((4 * len(held), PANEL, SLOTS * BLOCK), jnp.float32),
+                jax.ShapeDtypeStruct((4 * len(held), 8, SLOTS * BLOCK), jnp.float32),
+                jax.ShapeDtypeStruct((2 * STATS, BLOCK), jnp.float32),
+            ],
+            compiler_params=pltpu.CompilerParams(vmem_limit_bytes=8 << 20),
+            name="scores",
+        )(here, count, table, place, scale, own_t, oth_t, stat, *held)
+
+    own_t, oth_t = turn(own), turn(oth)
+    low = jnp.full((STATS, BLOCK), LOW, jnp.float32)
+    *near, stat = scores_of(0, jnp.concatenate([low, jnp.zeros_like(low)]), stacks[0:3])
+    *far, stat = scores_of(3, stat, stacks[3:4])
     stat_other = moved(stat, "c", 1)
 
-    def sums_of(wanted):
+    def sums_of(wanted, stat):
         return pl.pallas_call(
             functools.partial(sum_kernel, wanted),
-            in_specs=[smem] * 4 + [vmem] * 6,
+            in_specs=[smem] * 4 + [vmem] * 8,
             out_specs=[vmem] * 3,
             out_shape=[jax.ShapeDtypeStruct((PACK, DIM), jnp.bfloat16)] * 2
             + [jax.ShapeDtypeStruct((BLOCKS, BLOCK), jnp.float32)],
@@ -286,11 +302,14 @@
                 pltpu.VMEM((32, PANEL), jnp.float32),
             ],
             compiler_params=pltpu.CompilerParams(vmem_limit_bytes=8 << 20),
+            cost_estimate=pl.CostEstimate(
+                flops=4_000_000_000, transcendentals=0, bytes_accessed=16_000_000
+            ),
             name="sums",
-        )(here, count, table, place, own, oth, power, top, stat, stat_other)
-
-    pack_far, pack_next, norm = sums_of((2, 1))
-    pack_last, pack_own, _ = sums_of((3, 0))
+        )(here, count, table, place, own, oth, stat, stat_other, *near, *far)
+
+    pack_last, pack_own, norm = sums_of((3, 0), stat)
+    pack_far, pack_next, _ = sums_of((2, 1), stat)
     packs = [pack_own, pack_next, pack_far, pack_last]
     got = [packs[0]] + [shifted(packs[d], True, -d) for d in (1, 2, 3)]
     chunks = pl.pallas_call(
@@ -302,7 +321,7 @@
         name="fold",
     )(*got)
     norm, chunks = lax.optimization_barrier((norm, chunks))
-    last = [homeward(chunks[d], d) for d in range(4)]
+    last = [homeward(chunk, d) for chunk, d in zip(chunks, ORDER)]
     part_norm = lax.dynamic_slice_in_dim(norm, c * 8, 8, axis=0)
     log_norm = swapped(part_norm).reshape(8 * BLOCK)
     revised = pl.pallas_call(
@@ -310,6 +329,7 @@
         in_specs=[vmem] * 5,
         out_specs=vmem,
         out_shape=jax.ShapeDtypeStruct((PANEL, DIM), jnp.bfloat16),
+        compiler_params=pltpu.CompilerParams(vmem_limit_bytes=4 << 20),
         name="finish",
     )(fine_cluster_means, *last)
     return (revised, log_norm)

time: 128 us -> 120 us (0.938)
  waiting for transfers between devices: 50.9 us -> 43.4 us
  starting transfers between devices: 41.7 us -> 43.2 us
  local copies, waits for them, and re-layouts: 5.86 us -> 4.46 us
    ppermute x9, waiting for transfers between devices: 28.6 us -> 24.3 us  [shifted(): return lax.ppermute(value, ('c', 'z', 'x'), pairs)]
    ppermute x4, waiting for transfers between devices: 2.19 us -> 0.01 us  [homeward(): return lax.ppermute(value, ('c', 'yl', 'z', 'x'), pairs)]
    ppermute x6, waiting for transfers between devices: 14.9 us -> 13.2 us  [moved(): lax.ppermute(value, axis, [(i, (i - by) % size) for i in range(size)])]
    ppermute x6, starting transfers between devices: 7.31 us -> 5.63 us  [moved(): lax.ppermute(value, axis, [(i, (i - by) % size) for i in range(size)])]
    ppermute x9, starting transfers between devices: 12.2 us -> 13.6 us  [shifted(): return lax.ppermute(value, ('c', 'z', 'x'), pairs)]
    unnamed x22 -> x18, local copies, waits for them, and re-layouts: 4.09 us -> 2.69 us
    pallas_call x1, Pallas kernels: 2.19 us -> 0.9 us  [shards(): pl.pallas_call(finish_kernel, in_specs=[vmem] * 5, out_specs=vmem, out_sh...]
    pallas_call x3 -> x4, Pallas kernels: 13.6 us -> 14.2 us  [the longest x2 10.5 us: scores_of(): pl.pallas_call(functools.partial(score_kernel, base), in_specs=[smem] * 5...]
  transfers between devices with their start and end apart: 22 -> 22, of which waited for: 10 -> 9; matrix products, arithmetic and copies ran while one was open for 2% -> 2% of each run, Pallas kernels for 7% -> 13%
where the time goes in v5:
time: 120 us; the launch traced here: 119 us
  waiting for transfers between devices  43.4 us (36%)
  starting transfers between devices  43.2 us (36%)
  Pallas kernels  25.3 us (21%)
  local copies, waits for them, and re-layouts  4.46 us (4%)
  between operations  1.7 us (1%)
    ppermute x9, waiting for transfers between devices, shifted(): return lax.ppermute(value, ('c', 'z', 'x'), pairs)  24.3 us
    ppermute x9, starting transfers between devices, shifted(): return lax.ppermute(value, ('c', 'z', 'x'), pairs)  13.6 us
    ppermute x3, starting transfers between devices, swapped(): return lax.ppermute(value, ('c', 'yl'), [(0, 0), (1, 2), (2, 1), (3, 3)])  13.3 us
    ppermute x6, waiting for transfers between devices, moved(): lax.ppermute(value, axis, [(i, (i - by) % size) for i in range(size)])  13.2 us
    ppermute x4, starting transfers between devices, homeward(): return lax.ppermute(value, ('c', 'yl', 'z', 'x'), pairs)  10.7 us
    pallas_call x2, Pallas kernels, scores_of(): pl.pallas_call(functools.partial(score_kernel, base), in_specs=[smem] * 5...  10.5 us
    pallas_call x2, Pallas kernels, sums_of(): pl.pallas_call(functools.partial(sum_kernel, wanted), in_specs=[smem] * 4...  9.72 us
    ppermute x3, waiting for transfers between devices, swapped(): return lax.ppermute(value, ('c', 'yl'), [(0, 0), (1, 2), (2, 1), (3, 3)])  5.95 us
  transfers between devices with their start and end apart: 22, of which 9 were waited for; matrix products, arithmetic and copies ran while one was open for 2% of the time, Pallas kernels for 13%

profile of v5, /device:TPU:1, one launch (start us, length us, event | category | flops | bytes accessed | tf_op | source)
XLA Modules:
  0.0 119.2 jit_solution(11733703224373151233)
XLA Ops:
  0.6 4.6 %collective-permute-start = (bf16[128,1024]{1,0:T(8,128)(2,1)}, bf16[128,1024]{1,0:T(8,128)(2,1)S(1)}, u32[]{:S(2)}, u32[]{:S(2)}) collective-permute-start(bf16[128,1024]{1,0:T(8,128)(2,1)} %panel_ref.1), channel_id=1, source_target_pairs={{0,0},{16,32},{32,16},{48,48},{1,1},{17,33},{33,17},{49,49},{2,2},... | collective-permute-start | bytes 786440 | tf_op jit(solution)/shard_map/ppermute | solution.py:34
  5.3 1.7 %dynamic-slice_bitcast_fusion = (bf16[8,128,256]{2,1,0:T(8,128)(2,1)S(1)}, bf16[8,128,256]{2,1,0:T(8,128)(2,1)S(1)}, bf16[8,128,256]{2,1,0:T(8,128)(2,1)S(1)}, bf16[8,128,256]{2,1,0:T(8,128)(2,1)S(1)}) fusion(bf16[4,8,128,256]{3,2,1,0:T(8,128)(2,1)} %bitcast.22, s32[]{:T(128)S(6)} %select_n.159, s32[]{:T(128)S(6)} %select_n.157, s32[]{:T(128)S(6)} %select_n.155, ...), kind=kLoop, calls=%fused_computation.1 | loop fusion | bytes 4194320 | tf_op jit(solution)/shard_map/jit(dynamic_index_in_dim)/squeeze | solution.py:240
  7.0 0.6 collective-permute-start.4
  7.5 1.0 collective-permute-start.5
  8.5 1.0 collective-permute-done
  9.5 2.5 %collective-permute-start.1 = (bf16[128,1024]{1,0:T(8,128)(2,1)S(1)}, bf16[128,1024]{1,0:T(8,128)(2,1)S(1)}, u32[]{:S(2)}, u32[]{:S(2)}) collective-permute-start(bf16[128,1024]{1,0:T(8,128)(2,1)S(1)} %collective-permute-done), channel_id=1, source_target_pairs={{4,0},{5,1},{6,2},{7,3},{8,4},{9,5},{10,6},{11,7},{12,8},{13,9},{1... | collective-permute-start | bytes 786440 | tf_op jit(solution)/shard_map/ppermute | solution.py:72
  12.0 0.5 collective-permute-start.2
  12.5 0.6 collective-permute-start.3
  13.1 5.0 %collective-permute-done.1 = bf16[128,1024]{1,0:T(8,128)(2,1)S(1)} collective-permute-done((bf16[128,1024]{1,0:T(8,128)(2,1)S(1)}, bf16[128,1024]{1,0:T(8,128)(2,1)S(1)}, u32[]{:S(2)}, u32[]{:S(2)}) %collective-permute-start.1) | collective-permute-done | bytes 262176 | tf_op jit(solution)/shard_map/ppermute | solution.py:72
  18.1 5.8 %collective-permute-start.6 = (s32[8,8]{1,0:T(8,128)S(1)}, s32[8,8]{1,0:T(8,128)S(1)}, u32[]{:S(2)}, u32[]{:S(2)}) collective-permute-start(s32[8,8]{1,0:T(8,128)S(1)} %copy-done.6), channel_id=1, source_target_pairs={{0,0},{16,32},{32,16},{48,48},{1,1},{17,33},{33,17},{49,49},{2,2},... | collective-permute-start | bytes 776 | tf_op jit(solution)/shard_map/ppermute | solution.py:34
  23.9 0.0 collective-permute-done.2
  23.9 0.0 collective-permute-done.3
  23.9 0.1 pad_maximum_fusion.refs_0_
  24.0 1.1 collective-permute-done.6
  25.1 0.0 collective-permute-done.4
  25.1 0.0 collective-permute-done.5
  25.1 0.0 collective-permute-start.10
  25.2 3.5 %collective-permute-start.9 = (bf16[4,128,1024]{2,1,0:T(8,128)(2,1)S(1)}, bf16[4,128,1024]{2,1,0:T(8,128)(2,1)S(1)}, u32[]{:S(2)}, u32[]{:S(2)}) collective-permute-start(bf16[4,128,1024]{2,1,0:T(8,128)(2,1)S(1)} %pad_maximum_fusion.refs_0_), channel_id=1, source_target_pairs={{1,0},{2,1},{3,2},{0,3},{5,4},{6,5},{7,6},{4,7},{9,8},{10,9},{11,1... | collective-permute-start | bytes 3145736 | tf_op jit(solution)/shard_map/ppermute | solution.py:72
  28.6 2.8 %collective-permute-start.8 = (bf16[8,128,256]{2,1,0:T(8,128)(2,1)S(1)}, bf16[8,128,256]{2,1,0:T(8,128)(2,1)S(1)}, u32[]{:S(2)}, u32[]{:S(2)}) collective-permute-start(bf16[8,128,256]{2,1,0:T(8,128)(2,1)S(1)} %get-tuple-element.35), channel_id=1, source_target_pairs={{0,64},{16,80},{64,0},{80,16},{1,65},{17,81},{65,1},{81,17},{2,66}... | collective-permute-start | bytes 1572872 | tf_op jit(solution)/shard_map/ppermute | solution.py:30
  31.4 11.2 %collective-permute-done.8 = bf16[8,128,256]{2,1,0:T(8,128)(2,1)S(1)} collective-permute-done((bf16[8,128,256]{2,1,0:T(8,128)(2,1)S(1)}, bf16[8,128,256]{2,1,0:T(8,128)(2,1)S(1)}, u32[]{:S(2)}, u32[]{:S(2)}) %collective-permute-start.8) | collective-permute-done | bytes 524320 | tf_op jit(solution)/shard_map/ppermute | solution.py:30
  42.6 0.0 collective-permute-done.10.refs_2_
  42.6 1.0 copy-done
  43.6 0.0 collective-permute-done.9.refs_1_
  43.6 1.0 copy-done.2
  44.8 0.1 collective-permute-start.11
  45.5 3.1 %collective-permute-start.12 = (bf16[4,128,1024]{2,1,0:T(8,128)(2,1)S(1)}, bf16[4,128,1024]{2,1,0:T(8,128)(2,1)}, u32[]{:S(2)}, u32[]{:S(2)}) collective-permute-start(bf16[4,128,1024]{2,1,0:T(8,128)(2,1)S(1)} %pad_maximum_fusion.refs_0_), channel_id=1, source_target_pairs={{2,0},{3,1},{0,2},{1,3},{6,4},{7,5},{4,6},{5,7},{10,8},{11,9},{8,1... | collective-permute-start | bytes 3145736 | tf_op jit(solution)/shard_map/ppermute | solution.py:72
  48.6 0.1 pad_maximum_fusion.1.scale_ref
  48.7 0.1 pad_add_fusion.here_ref
  48.8 0.0 collective-permute-start.7
  48.8 1.1 collective-permute-done.7
  50.0 0.1 copy.16
  50.1 0.2 reduce_window_sum.11
  50.3 0.1 convert_reduce_fusion.count_ref
  50.4 0.4 select_reduce_fusion
  50.8 1.0 turn.2.own
  51.8 0.0 copy-start.5
  51.8 0.0 collective-permute-done.11.ref.oth
  51.8 2.7 %turn.3.oth = bf16[32,256,128]{2,1,0:T(8,128)(2,1)S(1)} custom-call(bf16[32,128,256]{2,1,0:T(8,128)(2,1)} %collective-permute-done.11.ref.oth), custom_call_target="tpu_custom_call" | custom-call | tf_op jit(solution)/shard_map/turn/pallas_call | solution.py:287
  54.5 7.2 %scores.2 = (f32[12,128,1024]{2,1,0:T(8,128)S(1)}, f32[12,8,1024]{2,1,0:T(8,128)S(1)}, f32[48,128]{1,0:T(8,128)S(1)}) custom-call(s32[2]{0:T(128)S(1)} %pad_add_fusion.here_ref, s32[16]{0:T(128)S(1)} %convert_reduce_fusion.count_ref, s32[16,8]{1,0:T(8,128)S(1)} %get-tuple-element.67.list_ref, s32[16,8]{1,0:T(8,128)S(1)} %get-tuple-element.66.place_ref, ...), custom_call_target="tpu_custom_call" | custom-call | tf_op jit(solution)/shard_map/scores/pallas_call | solution.py:274
  61.7 0.0 collective-permute-done.12.refs_0_
  61.7 3.4 %scores.3 = (f32[4,128,1024]{2,1,0:T(8,128)S(1)}, f32[4,8,1024]{2,1,0:T(8,128)S(1)}, f32[48,128]{1,0:T(8,128)S(1)}) custom-call(s32[2]{0:T(128)S(1)} %pad_add_fusion.here_ref, s32[16]{0:T(128)S(1)} %convert_reduce_fusion.count_ref, s32[16,8]{1,0:T(8,128)S(1)} %get-tuple-element.67.list_ref, s32[16,8]{1,0:T(8,128)S(1)} %get-tuple-element.66.place_ref, ...), custom_call_target="tpu_custom_call" | custom-call | tf_op jit(solution)/shard_map/scores/pallas_call | solution.py:274
  65.1 1.2 %collective-permute-start.13 = (f32[48,128]{1,0:T(8,128)S(1)}, f32[48,128]{1,0:T(8,128)S(1)}, u32[]{:S(2)}, u32[]{:S(2)}) collective-permute-start(f32[48,128]{1,0:T(8,128)S(1)} %get-tuple-element.43.mine_ref), channel_id=1, source_target_pairs={{0,32},{32,0},{1,33},{33,1},{2,34},{34,2},{3,35},{35,3},{4,36},{36... | collective-permute-start | bytes 73736 | tf_op jit(solution)/shard_map/ppermute | solution.py:30
  66.3 0.8 collective-permute-done.13.other_ref
  67.1 5.1 %sums.3 = (bf16[520,1024]{1,0:T(8,128)(2,1)S(1)}, bf16[520,1024]{1,0:T(8,128)(2,1)S(1)}, f32[16,128]{1,0:T(8,128)}) custom-call(s32[2]{0:T(128)S(1)} %pad_add_fusion.here_ref, s32[16]{0:T(128)S(1)} %convert_reduce_fusion.count_ref, s32[16,8]{1,0:T(8,128)S(1)} %get-tuple-element.67.list_ref, s32[16,8]{1,0:T(8,128)S(1)} %get-tuple-element.66.place_ref, ...), custom_call_target="tpu_custom_call" | custom-call | flops 4000000000 | bytes 16000000 | tf_op jit(solution)/shard_map/sums/pallas_call | solution.py:294
  72.2 0.0 collective-permute-start.14
  72.2 2.5 %collective-permute-start.15 = (bf16[520,1024]{1,0:T(8,128)(2,1)S(1)}, bf16[520,1024]{1,0:T(8,128)(2,1)S(1)}, u32[]{:S(2)}, u32[]{:S(2)}) collective-permute-start(bf16[520,1024]{1,0:T(8,128)(2,1)S(1)} %get-tuple-element.51), channel_id=1, source_target_pairs={{8,0},{9,1},{10,2},{11,3},{12,4},{13,5},{14,6},{15,7},{0,8},{1,9},... | collective-permute-start | bytes 3194888 | tf_op jit(solution)/shard_map/ppermute | solution.py:72
  74.7 4.6 %sums.2 = (bf16[520,1024]{1,0:T(8,128)(2,1)S(1)}, bf16[520,1024]{1,0:T(8,128)(2,1)S(1)}, f32[16,128]{1,0:T(8,128)S(1)}) custom-call(s32[2]{0:T(128)S(1)} %pad_add_fusion.here_ref, s32[16]{0:T(128)S(1)} %convert_reduce_fusion.count_ref, s32[16,8]{1,0:T(8,128)S(1)} %get-tuple-element.67.list_ref, s32[16,8]{1,0:T(8,128)S(1)} %get-tuple-element.66.place_ref, ...), custom_call_target="tpu_custom_call" | custom-call | flops 4000000000 | bytes 16000000 | tf_op jit(solution)/shard_map/sums/pallas_call | solution.py:294
  79.3 1.0 collective-permute-start.16
  80.3 18.7 %collective-permute-done.14.refs_1_ = bf16[520,1024]{1,0:T(8,128)(2,1)S(1)} collective-permute-done((bf16[520,1024]{1,0:T(8,128)(2,1)S(1)}, bf16[520,1024]{1,0:T(8,128)(2,1)S(1)}, u32[]{:S(2)}, u32[]{:S(2)}) %collective-permute-start.14) | collective-permute-done | bytes 1064992 | tf_op jit(solution)/shard_map/ppermute | solution.py:72
  99.0 0.0 collective-permute-done.15.refs_2_
  99.0 0.6 collective-permute-done.16.refs_3_
  99.6 0.5 fold.1
  100.1 4.3 %collective-permute-start.17 = (bf16[136,1024]{1,0:T(8,128)(2,1)S(1)}, bf16[136,1024]{1,0:T(8,128)(2,1)S(1)}, u32[]{:S(2)}, u32[]{:S(2)}) collective-permute-start(bf16[136,1024]{1,0:T(8,128)(2,1)S(1)} %get-tuple-element.57), channel_id=1, source_target_pairs={{0,0},{1,1},{2,2},{3,3},{4,4},{5,5},{6,6},{7,7},{8,8},{9,9},{10,10... | collective-permute-start | bytes 835592 | tf_op jit(solution)/shard_map/ppermute | solution.py:84
  104.4 0.1 collective-permute-start.18
  104.5 3.2 %collective-permute-start.19 = (bf16[136,1024]{1,0:T(8,128)(2,1)S(1)}, bf16[136,1024]{1,0:T(8,128)(2,1)S(1)}, u32[]{:S(2)}, u32[]{:S(2)}) collective-permute-start(bf16[136,1024]{1,0:T(8,128)(2,1)S(1)} %get-tuple-element.59), channel_id=1, source_target_pairs={{0,3},{1,0},{2,1},{3,2},{4,7},{5,4},{6,5},{7,6},{8,11},{9,8},{10,9... | collective-permute-start | bytes 835592 | tf_op jit(solution)/shard_map/ppermute | solution.py:84
  107.7 3.1 %collective-permute-start.20 = (bf16[136,1024]{1,0:T(8,128)(2,1)S(1)}, bf16[136,1024]{1,0:T(8,128)(2,1)S(1)}, u32[]{:S(2)}, u32[]{:S(2)}) collective-permute-start(bf16[136,1024]{1,0:T(8,128)(2,1)S(1)} %get-tuple-element.60), channel_id=1, source_target_pairs={{0,2},{1,3},{2,0},{3,1},{4,6},{5,7},{6,4},{7,5},{8,10},{9,11},{10,... | collective-permute-start | bytes 835592 | tf_op jit(solution)/shard_map/ppermute | solution.py:84
  110.8 2.9 %collective-permute-start.21 = (f32[8,128]{1,0:T(8,128)S(1)}, f32[8,128]{1,0:T(8,128)S(1)}, u32[]{:S(2)}, u32[]{:S(2)}) collective-permute-start(f32[8,128]{1,0:T(8,128)S(1)} %constant_dynamic-slice_fusion), channel_id=1, source_target_pairs={{0,0},{16,32},{32,16},{48,48},{1,1},{17,33},{33,17},{49,49},{2,2},... | collective-permute-start | bytes 12296 | tf_op jit(solution)/shard_map/ppermute | solution.py:34
  113.8 3.9 %collective-permute-done.21 = f32[8,128]{1,0:T(8,128)S(1)} collective-permute-done((f32[8,128]{1,0:T(8,128)S(1)}, f32[8,128]{1,0:T(8,128)S(1)}, u32[]{:S(2)}, u32[]{:S(2)}) %collective-permute-start.21) | collective-permute-done | bytes 4128 | tf_op jit(solution)/shard_map/ppermute | solution.py:34
  117.7 0.0 collective-permute-done.17.refs_0_
  117.7 0.0 collective-permute-done.18.refs_1_
  117.7 0.0 collective-permute-done.19.refs_2_
  117.7 0.0 collective-permute-done.20.refs_3_
  117.7 0.9 finish.1
  118.6 0.6 copy.23
  (22 shorter events, 0.3 us)
Async XLA Ops:
  0.6 8.9 %collective-permute-start = (bf16[128,1024]{1,0:T(8,128)(2,1)}, bf16[128,1024]{1,0:T(8,128)(2,1)S(1)}, u32[]{:S(2)}, u32[]{:S(2)}) collective-permute-start(bf16[128,1024]{1,0:T(8,128)(2,1)} %panel_ref.1), channel_id=1, source_target_pairs={{0,0},{16,32},{32,16},{48,48},{1,1},{17,33},{33,17},{49,49},{2,2},... | collective-permute-start | bytes 786440 | tf_op jit(solution)/shard_map/ppermute | solution.py:34
  5.3 12.8 %copy-start.6 = (s32[8,8]{1,0:T(8,128)S(1)}, s32[8,8]{1,0:T(8,128)}, u32[]{:S(2)}) copy-start(s32[8,8]{1,0:T(8,128)} %param.6) | copy-start | bytes 772
  7.0 18.2 %collective-permute-start.4 = (bf16[8,128,256]{2,1,0:T(8,128)(2,1)S(1)}, bf16[8,128,256]{2,1,0:T(8,128)(2,1)S(1)}, u32[]{:S(2)}, u32[]{:S(2)}) collective-permute-start(bf16[8,128,256]{2,1,0:T(8,128)(2,1)S(1)} %get-tuple-element.64), channel_id=1, source_target_pairs={{0,80},{16,0},{64,16},{80,64},{1,81},{17,1},{65,17},{81,65},{2,82}... | collective-permute-start | bytes 1572872 | tf_op jit(solution)/shard_map/ppermute | solution.py:30
  7.5 17.6 %collective-permute-start.5 = (bf16[8,128,256]{2,1,0:T(8,128)(2,1)S(1)}, bf16[8,128,256]{2,1,0:T(8,128)(2,1)S(1)}, u32[]{:S(2)}, u32[]{:S(2)}) collective-permute-start(bf16[8,128,256]{2,1,0:T(8,128)(2,1)S(1)} %get-tuple-element.62), channel_id=1, source_target_pairs={{0,16},{16,64},{64,80},{80,0},{1,17},{17,65},{65,81},{81,1},{2,18}... | collective-permute-start | bytes 1572872 | tf_op jit(solution)/shard_map/ppermute | solution.py:30
  9.5 8.6 %collective-permute-start.1 = (bf16[128,1024]{1,0:T(8,128)(2,1)S(1)}, bf16[128,1024]{1,0:T(8,128)(2,1)S(1)}, u32[]{:S(2)}, u32[]{:S(2)}) collective-permute-start(bf16[128,1024]{1,0:T(8,128)(2,1)S(1)} %collective-permute-done), channel_id=1, source_target_pairs={{4,0},{5,1},{6,2},{7,3},{8,4},{9,5},{10,6},{11,7},{12,8},{13,9},{1... | collective-permute-start | bytes 786440 | tf_op jit(solution)/shard_map/ppermute | solution.py:72
  12.0 11.9 %collective-permute-start.2 = (bf16[128,1024]{1,0:T(8,128)(2,1)S(1)}, bf16[128,1024]{1,0:T(8,128)(2,1)S(1)}, u32[]{:S(2)}, u32[]{:S(2)}) collective-permute-start(bf16[128,1024]{1,0:T(8,128)(2,1)S(1)} %collective-permute-done), channel_id=1, source_target_pairs={{8,0},{9,1},{10,2},{11,3},{12,4},{13,5},{14,6},{15,7},{0,8},{1,9},... | collective-permute-start | bytes 786440 | tf_op jit(solution)/shard_map/ppermute | solution.py:72
  12.5 11.4 %collective-permute-start.3 = (bf16[128,1024]{1,0:T(8,128)(2,1)S(1)}, bf16[128,1024]{1,0:T(8,128)(2,1)S(1)}, u32[]{:S(2)}, u32[]{:S(2)}) collective-permute-start(bf16[128,1024]{1,0:T(8,128)(2,1)S(1)} %collective-permute-done), channel_id=1, source_target_pairs={{12,0},{13,1},{14,2},{15,3},{0,4},{1,5},{2,6},{3,7},{4,8},{5,9},{6... | collective-permute-start | bytes 786440 | tf_op jit(solution)/shard_map/ppermute | solution.py:72
  18.1 7.0 %collective-permute-start.6 = (s32[8,8]{1,0:T(8,128)S(1)}, s32[8,8]{1,0:T(8,128)S(1)}, u32[]{:S(2)}, u32[]{:S(2)}) collective-permute-start(s32[8,8]{1,0:T(8,128)S(1)} %copy-done.6), channel_id=1, source_target_pairs={{0,0},{16,32},{32,16},{48,48},{1,1},{17,33},{33,17},{49,49},{2,2},... | collective-permute-start | bytes 776 | tf_op jit(solution)/shard_map/ppermute | solution.py:34
  25.1 17.5 %collective-permute-start.10 = (bf16[4,128,1024]{2,1,0:T(8,128)(2,1)S(1)}, bf16[4,128,1024]{2,1,0:T(8,128)(2,1)S(1)}, u32[]{:S(2)}, u32[]{:S(2)}) collective-permute-start(bf16[4,128,1024]{2,1,0:T(8,128)(2,1)S(1)} %pad_maximum_fusion.refs_0_), channel_id=1, source_target_pairs={{3,0},{0,1},{1,2},{2,3},{7,4},{4,5},{5,6},{6,7},{11,8},{8,9},{9,10... | collective-permute-start | bytes 3145736 | tf_op jit(solution)/shard_map/ppermute | solution.py:72
  25.2 18.4 %collective-permute-start.9 = (bf16[4,128,1024]{2,1,0:T(8,128)(2,1)S(1)}, bf16[4,128,1024]{2,1,0:T(8,128)(2,1)S(1)}, u32[]{:S(2)}, u32[]{:S(2)}) collective-permute-start(bf16[4,128,1024]{2,1,0:T(8,128)(2,1)S(1)} %pad_maximum_fusion.refs_0_), channel_id=1, source_target_pairs={{1,0},{2,1},{3,2},{0,3},{5,4},{6,5},{7,6},{4,7},{9,8},{10,9},{11,1... | collective-permute-start | bytes 3145736 | tf_op jit(solution)/shard_map/ppermute | solution.py:72
  28.6 14.0 %collective-permute-start.8 = (bf16[8,128,256]{2,1,0:T(8,128)(2,1)S(1)}, bf16[8,128,256]{2,1,0:T(8,128)(2,1)S(1)}, u32[]{:S(2)}, u32[]{:S(2)}) collective-permute-start(bf16[8,128,256]{2,1,0:T(8,128)(2,1)S(1)} %get-tuple-element.35), channel_id=1, source_target_pairs={{0,64},{16,80},{64,0},{80,16},{1,65},{17,81},{65,1},{81,17},{2,66}... | collective-permute-start | bytes 1572872 | tf_op jit(solution)/shard_map/ppermute | solution.py:30
  42.6 1.0 copy-start
  43.6 1.0 copy-start.2
  44.8 7.0 %collective-permute-start.11 = (bf16[32,128,256]{2,1,0:T(8,128)(2,1)S(1)}, bf16[32,128,256]{2,1,0:T(8,128)(2,1)}, u32[]{:S(2)}, u32[]{:S(2)}) collective-permute-start(bf16[32,128,256]{2,1,0:T(8,128)(2,1)S(1)} %constant_dynamic-update-slice_fusion.ref.own), channel_id=1, source_target_pairs={{0,32},{32,0},{1,33},{33,1},{2,34},{34,2},{3,35},{35,3},{4,36},{36... | collective-permute-start | bytes 6291464 | tf_op jit(solution)/shard_map/ppermute | solution.py:30
  45.5 16.2 %collective-permute-start.12 = (bf16[4,128,1024]{2,1,0:T(8,128)(2,1)S(1)}, bf16[4,128,1024]{2,1,0:T(8,128)(2,1)}, u32[]{:S(2)}, u32[]{:S(2)}) collective-permute-start(bf16[4,128,1024]{2,1,0:T(8,128)(2,1)S(1)} %pad_maximum_fusion.refs_0_), channel_id=1, source_target_pairs={{2,0},{3,1},{0,2},{1,3},{6,4},{7,5},{4,6},{5,7},{10,8},{11,9},{8,1... | collective-permute-start | bytes 3145736 | tf_op jit(solution)/shard_map/ppermute | solution.py:72
  48.8 1.2 collective-permute-start.7
  51.7 2.8 %copy-start.1 = (bf16[4,128,1024]{2,1,0:T(8,128)(2,1)S(1)}, bf16[4,128,1024]{2,1,0:T(8,128)(2,1)}, u32[]{:S(2)}) copy-start(bf16[4,128,1024]{2,1,0:T(8,128)(2,1)} %copy-done) | copy-start | bytes 3145732
  51.8 2.8 %copy-start.3 = (bf16[4,128,1024]{2,1,0:T(8,128)(2,1)S(1)}, bf16[4,128,1024]{2,1,0:T(8,128)(2,1)}, u32[]{:S(2)}) copy-start(bf16[4,128,1024]{2,1,0:T(8,128)(2,1)} %copy-done.2) | copy-start | bytes 3145732
  51.8 2.8 %copy-start.5 = (f32[48,128]{1,0:T(8,128)S(1)}, f32[48,128]{1,0:T(8,128)}, u32[]{:S(2)}) copy-start(f32[48,128]{1,0:T(8,128)} %constant.160.clone.1.before_ref) | copy-start | bytes 73732
  65.1 2.1 %collective-permute-start.13 = (f32[48,128]{1,0:T(8,128)S(1)}, f32[48,128]{1,0:T(8,128)S(1)}, u32[]{:S(2)}, u32[]{:S(2)}) collective-permute-start(f32[48,128]{1,0:T(8,128)S(1)} %get-tuple-element.43.mine_ref), channel_id=1, source_target_pairs={{0,32},{32,0},{1,33},{33,1},{2,34},{34,2},{3,35},{35,3},{4,36},{36... | collective-permute-start | bytes 73736 | tf_op jit(solution)/shard_map/ppermute | solution.py:30
  72.2 26.7 %collective-permute-start.14 = (bf16[520,1024]{1,0:T(8,128)(2,1)S(1)}, bf16[520,1024]{1,0:T(8,128)(2,1)S(1)}, u32[]{:S(2)}, u32[]{:S(2)}) collective-permute-start(bf16[520,1024]{1,0:T(8,128)(2,1)S(1)} %get-tuple-element.50), channel_id=1, source_target_pairs={{12,0},{13,1},{14,2},{15,3},{0,4},{1,5},{2,6},{3,7},{4,8},{5,9},{6... | collective-permute-start | bytes 3194888 | tf_op jit(solution)/shard_map/ppermute | solution.py:72
  72.2 26.7 %collective-permute-start.15 = (bf16[520,1024]{1,0:T(8,128)(2,1)S(1)}, bf16[520,1024]{1,0:T(8,128)(2,1)S(1)}, u32[]{:S(2)}, u32[]{:S(2)}) collective-permute-start(bf16[520,1024]{1,0:T(8,128)(2,1)S(1)} %get-tuple-element.51), channel_id=1, source_target_pairs={{8,0},{9,1},{10,2},{11,3},{12,4},{13,5},{14,6},{15,7},{0,8},{1,9},... | collective-permute-start | bytes 3194888 | tf_op jit(solution)/shard_map/ppermute | solution.py:72
  79.3 20.3 %collective-permute-start.16 = (bf16[520,1024]{1,0:T(8,128)(2,1)S(1)}, bf16[520,1024]{1,0:T(8,128)(2,1)S(1)}, u32[]{:S(2)}, u32[]{:S(2)}) collective-permute-start(bf16[520,1024]{1,0:T(8,128)(2,1)S(1)} %get-tuple-element.52), channel_id=1, source_target_pairs={{4,0},{5,1},{6,2},{7,3},{8,4},{9,5},{10,6},{11,7},{12,8},{13,9},{1... | collective-permute-start | bytes 3194888 | tf_op jit(solution)/shard_map/ppermute | solution.py:72
  99.6 18.1 %copy-start.4 = (bf16[128,1024]{1,0:T(8,128)(2,1)S(1)}, bf16[128,1024]{1,0:T(8,128)(2,1)}, u32[]{:S(2)}) copy-start(bf16[128,1024]{1,0:T(8,128)(2,1)} %panel_ref.1) | copy-start | bytes 786436
  100.1 17.5 %collective-permute-start.17 = (bf16[136,1024]{1,0:T(8,128)(2,1)S(1)}, bf16[136,1024]{1,0:T(8,128)(2,1)S(1)}, u32[]{:S(2)}, u32[]{:S(2)}) collective-permute-start(bf16[136,1024]{1,0:T(8,128)(2,1)S(1)} %get-tuple-element.57), channel_id=1, source_target_pairs={{0,0},{1,1},{2,2},{3,3},{4,4},{5,5},{6,6},{7,7},{8,8},{9,9},{10,10... | collective-permute-start | bytes 835592 | tf_op jit(solution)/shard_map/ppermute | solution.py:84
  104.4 13.2 %collective-permute-start.18 = (bf16[136,1024]{1,0:T(8,128)(2,1)S(1)}, bf16[136,1024]{1,0:T(8,128)(2,1)S(1)}, u32[]{:S(2)}, u32[]{:S(2)}) collective-permute-start(bf16[136,1024]{1,0:T(8,128)(2,1)S(1)} %get-tuple-element.58), channel_id=1, source_target_pairs={{0,1},{1,2},{2,3},{3,0},{4,5},{5,6},{6,7},{7,4},{8,9},{9,10},{10,1... | collective-permute-start | bytes 835592 | tf_op jit(solution)/shard_map/ppermute | solution.py:84
  104.5 13.1 %collective-permute-start.19 = (bf16[136,1024]{1,0:T(8,128)(2,1)S(1)}, bf16[136,1024]{1,0:T(8,128)(2,1)S(1)}, u32[]{:S(2)}, u32[]{:S(2)}) collective-permute-start(bf16[136,1024]{1,0:T(8,128)(2,1)S(1)} %get-tuple-element.59), channel_id=1, source_target_pairs={{0,3},{1,0},{2,1},{3,2},{4,7},{5,4},{6,5},{7,6},{8,11},{9,8},{10,9... | collective-permute-start | bytes 835592 | tf_op jit(solution)/shard_map/ppermute | solution.py:84
  107.7 9.9 %collective-permute-start.20 = (bf16[136,1024]{1,0:T(8,128)(2,1)S(1)}, bf16[136,1024]{1,0:T(8,128)(2,1)S(1)}, u32[]{:S(2)}, u32[]{:S(2)}) collective-permute-start(bf16[136,1024]{1,0:T(8,128)(2,1)S(1)} %get-tuple-element.60), channel_id=1, source_target_pairs={{0,2},{1,3},{2,0},{3,1},{4,6},{5,7},{6,4},{7,5},{8,10},{9,11},{10,... | collective-permute-start | bytes 835592 | tf_op jit(solution)/shard_map/ppermute | solution.py:84
  110.8 6.8 %collective-permute-start.21 = (f32[8,128]{1,0:T(8,128)S(1)}, f32[8,128]{1,0:T(8,128)S(1)}, u32[]{:S(2)}, u32[]{:S(2)}) collective-permute-start(f32[8,128]{1,0:T(8,128)S(1)} %constant_dynamic-slice_fusion), channel_id=1, source_target_pairs={{0,0},{16,32},{32,16},{48,48},{1,1},{17,33},{33,17},{49,49},{2,2},... | collective-permute-start | bytes 12296 | tf_op jit(solution)/shard_map/ppermute | solution.py:34

commit v6 on v5

--- a/solution.py
+++ b/solution.py
@@ -82,6 +82,11 @@
                     to = 16 * (2 * yl + c) + 4 * far[0] + far[1]
                     pairs.append((16 * (2 * c + yl) + 4 * z + x, to))
     return lax.ppermute(value, ("c", "yl", "z", "x"), pairs)
+
+
+def join_kernel(*refs):
+    for d in range(4):
+        refs[6][8 * d : 8 * d + 8] = refs[d][...]
 
 
 def turn_kernel(ref, out):
@@ -147,7 +152,7 @@
     wanted, here_ref, count_ref, list_ref, place_ref, own, oth, mine_ref, other_ref, *refs
 ):
     scored, refs = ((refs[0], refs[1], 0), (refs[2], refs[3], 3)), refs[4:]
-    outs, norm_ref, full_ref, mass_ref = dict(zip(wanted, refs[0:2])), refs[2], refs[3], refs[4]
+    outs, (norm_ref, full_ref, mass_ref) = dict(zip(wanted, refs)), refs[len(wanted) :]
     parts = points_of(own, oth, here_ref[1])
     m0, s0 = mine_ref[0:STATS, :], mine_ref[STATS : 2 * STATS, :]
     m1, s1 = other_ref[0:STATS, :], other_ref[STATS : 2 * STATS, :]
@@ -245,7 +250,14 @@
     own[2] = moved(own[2], Y, 2)
     other = moved(mine, "c", 1)
     stacks = [stack] + [shifted(stack, False, d) for d in ORDER[1:]]
-    own = jnp.concatenate(lax.optimization_barrier((own, stacks[1], stacks[2]))[0])
+    own = pl.pallas_call(
+        join_kernel,
+        in_specs=[vmem] * 4 + [pl.BlockSpec(memory_space=pl.ANY)] * 2,
+        out_specs=vmem,
+        out_shape=jax.ShapeDtypeStruct((32, BLOCK, SLICE), jnp.bfloat16),
+        compiler_params=pltpu.CompilerParams(vmem_limit_bytes=8 << 20),
+        name="join",
+    )(*own, stacks[1], stacks[2])
     oth = moved(own, "c", 1)
 
     cands = jnp.where(c == 0, jnp.stack([mine, other]), jnp.stack([other, mine])).reshape(BLOCKS, 8)
@@ -294,8 +306,8 @@
         return pl.pallas_call(
             functools.partial(sum_kernel, wanted),
             in_specs=[smem] * 4 + [vmem] * 8,
-            out_specs=[vmem] * 3,
-            out_shape=[jax.ShapeDtypeStruct((PACK, DIM), jnp.bfloat16)] * 2
+            out_specs=[vmem] * (len(wanted) + 1),
+            out_shape=[jax.ShapeDtypeStruct((PACK, DIM), jnp.bfloat16)] * len(wanted)
             + [jax.ShapeDtypeStruct((BLOCKS, BLOCK), jnp.float32)],
             scratch_shapes=[
                 pltpu.VMEM((STATS, BLOCK), jnp.float32),
@@ -308,8 +320,8 @@
             name="sums",
         )(here, count, table, place, own, oth, stat, stat_other, *near, *far)
 
-    pack_last, pack_own, norm = sums_of((3, 0), stat)
-    pack_far, pack_next, _ = sums_of((2, 1), stat)
+    pack_next, pack_last, pack_own, norm = sums_of((1, 3, 0), stat)
+    pack_far, _ = sums_of((2,), stat)
     packs = [pack_own, pack_next, pack_far, pack_last]
     got = [packs[0]] + [shifted(packs[d], True, -d) for d in (1, 2, 3)]
     chunks = pl.pallas_call(

time: 120 us -> 117 us (0.975)
  waiting for transfers between devices: 43.4 us -> 40 us
  Pallas kernels: 25.3 us -> 26.7 us
    ppermute x9, waiting for transfers between devices: 24.3 us -> 21.6 us  [shifted(): return lax.ppermute(value, ('c', 'z', 'x'), pairs)]
    ppermute x3, waiting for transfers between devices: 5.95 us -> 3.89 us  [swapped(): return lax.ppermute(value, ('c', 'yl'), [(0, 0), (1, 2), (2, 1), (3, 3)])]
    unnamed x18 -> x15, local copies, waits for them, and re-layouts: 2.69 us -> 1.76 us
  transfers between devices with their start and end apart: 22 -> 22, of which waited for: 9 -> 10; matrix products, arithmetic and copies ran while one was open for 2% -> 2% of each run, Pallas kernels for 13% -> 15%
where the time goes in v6:
time: 117 us; the launch traced here: 116 us
  starting transfers between devices  43.4 us (37%)
  waiting for transfers between devices  40 us (34%)
  Pallas kernels  26.7 us (23%)
  local copies, waits for them, and re-layouts  3.5 us (3%)
  between operations  1.67 us (1%)
    ppermute x9, waiting for transfers between devices, shifted(): return lax.ppermute(value, ('c', 'z', 'x'), pairs)  21.6 us
    ppermute x9, starting transfers between devices, shifted(): return lax.ppermute(value, ('c', 'z', 'x'), pairs)  14.2 us
    ppermute x3, starting transfers between devices, swapped(): return lax.ppermute(value, ('c', 'yl'), [(0, 0), (1, 2), (2, 1), (3, 3)])  14 us
    ppermute x6, waiting for transfers between devices, moved(): lax.ppermute(value, axis, [(i, (i - by) % size) for i in range(size)])  13.3 us
    pallas_call x2, Pallas kernels, scores_of(): pl.pallas_call(functools.partial(score_kernel, base), in_specs=[smem] * 5...  11.1 us
    ppermute x4, starting transfers between devices, homeward(): return lax.ppermute(value, ('c', 'yl', 'z', 'x'), pairs)  10.5 us
    pallas_call x2, Pallas kernels, sums_of(): pl.pallas_call(functools.partial(sum_kernel, wanted), in_specs=[smem] * 4...  10.3 us
    ppermute x6, starting transfers between devices, moved(): lax.ppermute(value, axis, [(i, (i - by) % size) for i in range(size)])  4.78 us
  transfers between devices with their start and end apart: 22, of which 10 were waited for; matrix products, arithmetic and copies ran while one was open for 2% of the time, Pallas kernels for 15%

profile of v6, /device:TPU:1, one launch (start us, length us, event | category | flops | bytes accessed | tf_op | source)
XLA Modules:
  0.0 116.3 jit_solution(17813370694670635174)
XLA Ops:
  0.6 4.6 %collective-permute-start = (bf16[128,1024]{1,0:T(8,128)(2,1)}, bf16[128,1024]{1,0:T(8,128)(2,1)S(1)}, u32[]{:S(2)}, u32[]{:S(2)}) collective-permute-start(bf16[128,1024]{1,0:T(8,128)(2,1)} %panel_ref.1), channel_id=1, source_target_pairs={{0,0},{16,32},{32,16},{48,48},{1,1},{17,33},{33,17},{49,49},{2,2},... | collective-permute-start | bytes 786440 | tf_op jit(solution)/shard_map/ppermute | solution.py:34
  5.3 1.7 %dynamic-slice_bitcast_fusion = (bf16[8,128,256]{2,1,0:T(8,128)(2,1)S(1)}, bf16[8,128,256]{2,1,0:T(8,128)(2,1)S(1)}, bf16[8,128,256]{2,1,0:T(8,128)(2,1)S(1)}, bf16[8,128,256]{2,1,0:T(8,128)(2,1)S(1)}) fusion(bf16[4,8,128,256]{3,2,1,0:T(8,128)(2,1)} %bitcast.22, s32[]{:T(128)S(6)} %select_n.159, s32[]{:T(128)S(6)} %select_n.157, s32[]{:T(128)S(6)} %select_n.155, ...), kind=kLoop, calls=%fused_computation.1 | loop fusion | bytes 4194320 | tf_op jit(solution)/shard_map/jit(dynamic_index_in_dim)/squeeze | solution.py:245
  7.0 0.6 collective-permute-start.4
  7.5 1.0 collective-permute-start.5
  8.5 1.0 collective-permute-done
  9.5 2.5 %collective-permute-start.1 = (bf16[128,1024]{1,0:T(8,128)(2,1)S(1)}, bf16[128,1024]{1,0:T(8,128)(2,1)S(1)}, u32[]{:S(2)}, u32[]{:S(2)}) collective-permute-start(bf16[128,1024]{1,0:T(8,128)(2,1)S(1)} %collective-permute-done), channel_id=1, source_target_pairs={{4,0},{5,1},{6,2},{7,3},{8,4},{9,5},{10,6},{11,7},{12,8},{13,9},{1... | collective-permute-start | bytes 786440 | tf_op jit(solution)/shard_map/ppermute | solution.py:72
  12.0 0.5 collective-permute-start.2
  12.5 0.6 collective-permute-start.3
  13.1 5.0 %collective-permute-done.1 = bf16[128,1024]{1,0:T(8,128)(2,1)S(1)} collective-permute-done((bf16[128,1024]{1,0:T(8,128)(2,1)S(1)}, bf16[128,1024]{1,0:T(8,128)(2,1)S(1)}, u32[]{:S(2)}, u32[]{:S(2)}) %collective-permute-start.1) | collective-permute-done | bytes 262176 | tf_op jit(solution)/shard_map/ppermute | solution.py:72
  18.1 5.8 %collective-permute-start.6 = (s32[8,8]{1,0:T(8,128)S(1)}, s32[8,8]{1,0:T(8,128)S(1)}, u32[]{:S(2)}, u32[]{:S(2)}) collective-permute-start(s32[8,8]{1,0:T(8,128)S(1)} %copy-done.6), channel_id=1, source_target_pairs={{0,0},{16,32},{32,16},{48,48},{1,1},{17,33},{33,17},{49,49},{2,2},... | collective-permute-start | bytes 776 | tf_op jit(solution)/shard_map/ppermute | solution.py:34
  23.9 0.0 collective-permute-done.2
  23.9 0.0 collective-permute-done.3
  23.9 0.1 pad_maximum_fusion.refs_0_
  24.0 1.1 collective-permute-done.6
  25.1 0.0 collective-permute-done.4.refs_1_
  25.1 0.0 collective-permute-done.5.refs_3_
  25.1 0.0 collective-permute-start.10
  25.2 3.5 %collective-permute-start.9 = (bf16[4,128,1024]{2,1,0:T(8,128)(2,1)S(1)}, bf16[4,128,1024]{2,1,0:T(8,128)(2,1)S(1)}, u32[]{:S(2)}, u32[]{:S(2)}) collective-permute-start(bf16[4,128,1024]{2,1,0:T(8,128)(2,1)S(1)} %pad_maximum_fusion.refs_0_), channel_id=1, source_target_pairs={{1,0},{2,1},{3,2},{0,3},{5,4},{6,5},{7,6},{4,7},{9,8},{10,9},{11,1... | collective-permute-start | bytes 3145736 | tf_op jit(solution)/shard_map/ppermute | solution.py:72
  28.6 2.8 %collective-permute-start.8 = (bf16[8,128,256]{2,1,0:T(8,128)(2,1)S(1)}, bf16[8,128,256]{2,1,0:T(8,128)(2,1)S(1)}, u32[]{:S(2)}, u32[]{:S(2)}) collective-permute-start(bf16[8,128,256]{2,1,0:T(8,128)(2,1)S(1)} %get-tuple-element.31), channel_id=1, source_target_pairs={{0,64},{16,80},{64,0},{80,16},{1,65},{17,81},{65,1},{81,17},{2,66}... | collective-permute-start | bytes 1572872 | tf_op jit(solution)/shard_map/ppermute | solution.py:30
  31.4 11.2 %collective-permute-done.8.refs_2_ = bf16[8,128,256]{2,1,0:T(8,128)(2,1)S(1)} collective-permute-done((bf16[8,128,256]{2,1,0:T(8,128)(2,1)S(1)}, bf16[8,128,256]{2,1,0:T(8,128)(2,1)S(1)}, u32[]{:S(2)}, u32[]{:S(2)}) %collective-permute-start.8) | collective-permute-done | bytes 524320 | tf_op jit(solution)/shard_map/ppermute | solution.py:30
  42.6 0.0 collective-permute-done.10.refs_5_.refs_2_
  42.6 0.0 collective-permute-done.9.refs_4_.refs_1_
  42.6 0.1 join.1.ref.own
  42.8 0.8 copy-done
  43.6 0.3 copy-done.2
  43.9 0.0 collective-permute-start.11
  44.6 3.1 %collective-permute-start.12 = (bf16[4,128,1024]{2,1,0:T(8,128)(2,1)S(1)}, bf16[4,128,1024]{2,1,0:T(8,128)(2,1)}, u32[]{:S(2)}, u32[]{:S(2)}) collective-permute-start(bf16[4,128,1024]{2,1,0:T(8,128)(2,1)S(1)} %pad_maximum_fusion.refs_0_), channel_id=1, source_target_pairs={{2,0},{3,1},{0,2},{1,3},{6,4},{7,5},{4,6},{5,7},{10,8},{11,9},{8,1... | collective-permute-start | bytes 3145736 | tf_op jit(solution)/shard_map/ppermute | solution.py:72
  47.7 0.1 pad_maximum_fusion.1.scale_ref
  47.8 0.1 pad_add_fusion.here_ref
  47.8 0.0 collective-permute-start.7
  47.9 1.1 collective-permute-done.7
  49.1 0.1 copy.16
  49.2 0.2 reduce_window_sum.11
  49.3 0.1 convert_reduce_fusion.count_ref
  49.5 0.4 select_reduce_fusion
  49.8 1.0 turn.2.own
  50.8 0.0 copy-start.5
  50.9 0.0 collective-permute-done.11.ref.oth
  50.9 2.7 %turn.3.oth = bf16[32,256,128]{2,1,0:T(8,128)(2,1)S(1)} custom-call(bf16[32,128,256]{2,1,0:T(8,128)(2,1)} %collective-permute-done.11.ref.oth), custom_call_target="tpu_custom_call" | custom-call | tf_op jit(solution)/shard_map/turn/pallas_call | solution.py:299
  53.6 7.7 %scores.2 = (f32[12,128,1024]{2,1,0:T(8,128)S(1)}, f32[12,8,1024]{2,1,0:T(8,128)S(1)}, f32[48,128]{1,0:T(8,128)S(1)}) custom-call(s32[2]{0:T(128)S(1)} %pad_add_fusion.here_ref, s32[16]{0:T(128)S(1)} %convert_reduce_fusion.count_ref, s32[16,8]{1,0:T(8,128)S(1)} %get-tuple-element.59.list_ref, s32[16,8]{1,0:T(8,128)S(1)} %get-tuple-element.58.place_ref, ...), custom_call_target="tpu_custom_call" | custom-call | tf_op jit(solution)/shard_map/scores/pallas_call | solution.py:286
  61.3 0.0 collective-permute-done.12.refs_0_
  61.4 3.4 %scores.3 = (f32[4,128,1024]{2,1,0:T(8,128)S(1)}, f32[4,8,1024]{2,1,0:T(8,128)S(1)}, f32[48,128]{1,0:T(8,128)S(1)}) custom-call(s32[2]{0:T(128)S(1)} %pad_add_fusion.here_ref, s32[16]{0:T(128)S(1)} %convert_reduce_fusion.count_ref, s32[16,8]{1,0:T(8,128)S(1)} %get-tuple-element.59.list_ref, s32[16,8]{1,0:T(8,128)S(1)} %get-tuple-element.58.place_ref, ...), custom_call_target="tpu_custom_call" | custom-call | tf_op jit(solution)/shard_map/scores/pallas_call | solution.py:286
  64.7 0.4 collective-permute-start.13
  65.2 1.0 collective-permute-done.13.other_ref
  66.2 4.0 %sums.3 = (bf16[520,1024]{1,0:T(8,128)(2,1)S(1)}, f32[16,128]{1,0:T(8,128)}) custom-call(s32[2]{0:T(128)S(1)} %pad_add_fusion.here_ref, s32[16]{0:T(128)S(1)} %convert_reduce_fusion.count_ref, s32[16,8]{1,0:T(8,128)S(1)} %get-tuple-element.59.list_ref, s32[16,8]{1,0:T(8,128)S(1)} %get-tuple-element.58.place_ref, bf16[32,128,256]{2,1,0:T(8,128)(2,1)S(1)} %join.1.ref.own, ...), custom_call_target="tpu_custom_call" | custom-call | flops 4000000000 | bytes 16000000 | tf_op jit(solution)/shard_map/sums/pallas_call | solution.py:306
  70.2 1.3 %collective-permute-start.15 = (bf16[520,1024]{1,0:T(8,128)(2,1)S(1)}, bf16[520,1024]{1,0:T(8,128)(2,1)S(1)}, u32[]{:S(2)}, u32[]{:S(2)}) collective-permute-start(bf16[520,1024]{1,0:T(8,128)(2,1)S(1)} %get-tuple-element.43), channel_id=1, source_target_pairs={{8,0},{9,1},{10,2},{11,3},{12,4},{13,5},{14,6},{15,7},{0,8},{1,9},... | collective-permute-start | bytes 3194888 | tf_op jit(solution)/shard_map/ppermute | solution.py:72
  71.5 6.4 %sums.2 = (bf16[520,1024]{1,0:T(8,128)(2,1)S(1)}, bf16[520,1024]{1,0:T(8,128)(2,1)S(1)}, bf16[520,1024]{1,0:T(8,128)(2,1)S(1)}, f32[16,128]{1,0:T(8,128)S(1)}) custom-call(s32[2]{0:T(128)S(1)} %pad_add_fusion.here_ref, s32[16]{0:T(128)S(1)} %convert_reduce_fusion.count_ref, s32[16,8]{1,0:T(8,128)S(1)} %get-tuple-element.59.list_ref, ...), custom_call_target="tpu_custom_call" | custom-call | flops 4000000000 | bytes 16000000 | tf_op jit(solution)/shard_map/sums/pallas_call | solution.py:306
  77.8 0.5 collective-permute-start.14
  78.3 2.3 %collective-permute-start.16 = (bf16[520,1024]{1,0:T(8,128)(2,1)S(1)}, bf16[520,1024]{1,0:T(8,128)(2,1)S(1)}, u32[]{:S(2)}, u32[]{:S(2)}) collective-permute-start(bf16[520,1024]{1,0:T(8,128)(2,1)S(1)} %get-tuple-element.44), channel_id=1, source_target_pairs={{4,0},{5,1},{6,2},{7,3},{8,4},{9,5},{10,6},{11,7},{12,8},{13,9},{1... | collective-permute-start | bytes 3194888 | tf_op jit(solution)/shard_map/ppermute | solution.py:72
  80.6 5.2 %collective-permute-done.15.refs_2_ = bf16[520,1024]{1,0:T(8,128)(2,1)S(1)} collective-permute-done((bf16[520,1024]{1,0:T(8,128)(2,1)S(1)}, bf16[520,1024]{1,0:T(8,128)(2,1)S(1)}, u32[]{:S(2)}, u32[]{:S(2)}) %collective-permute-start.15) | collective-permute-done | bytes 1064992 | tf_op jit(solution)/shard_map/ppermute | solution.py:72
  85.8 11.4 %collective-permute-done.14.refs_1_ = bf16[520,1024]{1,0:T(8,128)(2,1)S(1)} collective-permute-done((bf16[520,1024]{1,0:T(8,128)(2,1)S(1)}, bf16[520,1024]{1,0:T(8,128)(2,1)S(1)}, u32[]{:S(2)}, u32[]{:S(2)}) %collective-permute-start.14) | collective-permute-done | bytes 1064992 | tf_op jit(solution)/shard_map/ppermute | solution.py:72
  97.2 0.0 collective-permute-done.16.refs_3_
  97.2 0.5 fold.1
  97.7 3.4 %collective-permute-start.17 = (bf16[136,1024]{1,0:T(8,128)(2,1)S(1)}, bf16[136,1024]{1,0:T(8,128)(2,1)S(1)}, u32[]{:S(2)}, u32[]{:S(2)}) collective-permute-start(bf16[136,1024]{1,0:T(8,128)(2,1)S(1)} %get-tuple-element.49), channel_id=1, source_target_pairs={{0,0},{1,1},{2,2},{3,3},{4,4},{5,5},{6,6},{7,7},{8,8},{9,9},{10,10... | collective-permute-start | bytes 835592 | tf_op jit(solution)/shard_map/ppermute | solution.py:84
  101.2 0.5 collective-permute-start.18
  101.7 4.3 %collective-permute-start.19 = (bf16[136,1024]{1,0:T(8,128)(2,1)S(1)}, bf16[136,1024]{1,0:T(8,128)(2,1)S(1)}, u32[]{:S(2)}, u32[]{:S(2)}) collective-permute-start(bf16[136,1024]{1,0:T(8,128)(2,1)S(1)} %get-tuple-element.51), channel_id=1, source_target_pairs={{0,3},{1,0},{2,1},{3,2},{4,7},{5,4},{6,5},{7,6},{8,11},{9,8},{10,9... | collective-permute-start | bytes 835592 | tf_op jit(solution)/shard_map/ppermute | solution.py:84
  105.9 2.3 %collective-permute-start.20 = (bf16[136,1024]{1,0:T(8,128)(2,1)S(1)}, bf16[136,1024]{1,0:T(8,128)(2,1)S(1)}, u32[]{:S(2)}, u32[]{:S(2)}) collective-permute-start(bf16[136,1024]{1,0:T(8,128)(2,1)S(1)} %get-tuple-element.52), channel_id=1, source_target_pairs={{0,2},{1,3},{2,0},{3,1},{4,6},{5,7},{6,4},{7,5},{8,10},{9,11},{10,... | collective-permute-start | bytes 835592 | tf_op jit(solution)/shard_map/ppermute | solution.py:84
  108.2 3.6 %collective-permute-start.21 = (f32[8,128]{1,0:T(8,128)S(1)}, f32[8,128]{1,0:T(8,128)S(1)}, u32[]{:S(2)}, u32[]{:S(2)}) collective-permute-start(f32[8,128]{1,0:T(8,128)S(1)} %constant_dynamic-slice_fusion), channel_id=1, source_target_pairs={{0,0},{16,32},{32,16},{48,48},{1,1},{17,33},{33,17},{49,49},{2,2},... | collective-permute-start | bytes 12296 | tf_op jit(solution)/shard_map/ppermute | solution.py:34
  111.9 1.8 %collective-permute-done.21 = f32[8,128]{1,0:T(8,128)S(1)} collective-permute-done((f32[8,128]{1,0:T(8,128)S(1)}, f32[8,128]{1,0:T(8,128)S(1)}, u32[]{:S(2)}, u32[]{:S(2)}) %collective-permute-start.21) | collective-permute-done | bytes 4128 | tf_op jit(solution)/shard_map/ppermute | solution.py:34
  113.7 0.0 collective-permute-done.17.refs_0_
  113.7 0.0 collective-permute-done.19.refs_2_
  113.7 1.1 collective-permute-done.20.refs_3_
  114.8 0.9 finish.1
  115.7 0.6 copy.20
  (19 shorter events, 0.1 us)
Async XLA Ops:
  0.6 8.9 %collective-permute-start = (bf16[128,1024]{1,0:T(8,128)(2,1)}, bf16[128,1024]{1,0:T(8,128)(2,1)S(1)}, u32[]{:S(2)}, u32[]{:S(2)}) collective-permute-start(bf16[128,1024]{1,0:T(8,128)(2,1)} %panel_ref.1), channel_id=1, source_target_pairs={{0,0},{16,32},{32,16},{48,48},{1,1},{17,33},{33,17},{49,49},{2,2},... | collective-permute-start | bytes 786440 | tf_op jit(solution)/shard_map/ppermute | solution.py:34
  5.3 12.8 %copy-start.6 = (s32[8,8]{1,0:T(8,128)S(1)}, s32[8,8]{1,0:T(8,128)}, u32[]{:S(2)}) copy-start(s32[8,8]{1,0:T(8,128)} %param.6) | copy-start | bytes 772
  7.0 18.2 %collective-permute-start.4 = (bf16[8,128,256]{2,1,0:T(8,128)(2,1)S(1)}, bf16[8,128,256]{2,1,0:T(8,128)(2,1)S(1)}, u32[]{:S(2)}, u32[]{:S(2)}) collective-permute-start(bf16[8,128,256]{2,1,0:T(8,128)(2,1)S(1)} %get-tuple-element.56), channel_id=1, source_target_pairs={{0,80},{16,0},{64,16},{80,64},{1,81},{17,1},{65,17},{81,65},{2,82}... | collective-permute-start | bytes 1572872 | tf_op jit(solution)/shard_map/ppermute | solution.py:30
  7.5 17.6 %collective-permute-start.5 = (bf16[8,128,256]{2,1,0:T(8,128)(2,1)S(1)}, bf16[8,128,256]{2,1,0:T(8,128)(2,1)S(1)}, u32[]{:S(2)}, u32[]{:S(2)}) collective-permute-start(bf16[8,128,256]{2,1,0:T(8,128)(2,1)S(1)} %get-tuple-element.54), channel_id=1, source_target_pairs={{0,16},{16,64},{64,80},{80,0},{1,17},{17,65},{65,81},{81,1},{2,18}... | collective-permute-start | bytes 1572872 | tf_op jit(solution)/shard_map/ppermute | solution.py:30
  9.5 8.6 %collective-permute-start.1 = (bf16[128,1024]{1,0:T(8,128)(2,1)S(1)}, bf16[128,1024]{1,0:T(8,128)(2,1)S(1)}, u32[]{:S(2)}, u32[]{:S(2)}) collective-permute-start(bf16[128,1024]{1,0:T(8,128)(2,1)S(1)} %collective-permute-done), channel_id=1, source_target_pairs={{4,0},{5,1},{6,2},{7,3},{8,4},{9,5},{10,6},{11,7},{12,8},{13,9},{1... | collective-permute-start | bytes 786440 | tf_op jit(solution)/shard_map/ppermute | solution.py:72
  12.0 11.9 %collective-permute-start.2 = (bf16[128,1024]{1,0:T(8,128)(2,1)S(1)}, bf16[128,1024]{1,0:T(8,128)(2,1)S(1)}, u32[]{:S(2)}, u32[]{:S(2)}) collective-permute-start(bf16[128,1024]{1,0:T(8,128)(2,1)S(1)} %collective-permute-done), channel_id=1, source_target_pairs={{8,0},{9,1},{10,2},{11,3},{12,4},{13,5},{14,6},{15,7},{0,8},{1,9},... | collective-permute-start | bytes 786440 | tf_op jit(solution)/shard_map/ppermute | solution.py:72
  12.5 11.4 %collective-permute-start.3 = (bf16[128,1024]{1,0:T(8,128)(2,1)S(1)}, bf16[128,1024]{1,0:T(8,128)(2,1)S(1)}, u32[]{:S(2)}, u32[]{:S(2)}) collective-permute-start(bf16[128,1024]{1,0:T(8,128)(2,1)S(1)} %collective-permute-done), channel_id=1, source_target_pairs={{12,0},{13,1},{14,2},{15,3},{0,4},{1,5},{2,6},{3,7},{4,8},{5,9},{6... | collective-permute-start | bytes 786440 | tf_op jit(solution)/shard_map/ppermute | solution.py:72
  18.1 7.0 %collective-permute-start.6 = (s32[8,8]{1,0:T(8,128)S(1)}, s32[8,8]{1,0:T(8,128)S(1)}, u32[]{:S(2)}, u32[]{:S(2)}) collective-permute-start(s32[8,8]{1,0:T(8,128)S(1)} %copy-done.6), channel_id=1, source_target_pairs={{0,0},{16,32},{32,16},{48,48},{1,1},{17,33},{33,17},{49,49},{2,2},... | collective-permute-start | bytes 776 | tf_op jit(solution)/shard_map/ppermute | solution.py:34
  25.1 17.5 %collective-permute-start.10 = (bf16[4,128,1024]{2,1,0:T(8,128)(2,1)S(1)}, bf16[4,128,1024]{2,1,0:T(8,128)(2,1)S(1)}, u32[]{:S(2)}, u32[]{:S(2)}) collective-permute-start(bf16[4,128,1024]{2,1,0:T(8,128)(2,1)S(1)} %pad_maximum_fusion.refs_0_), channel_id=1, source_target_pairs={{3,0},{0,1},{1,2},{2,3},{7,4},{4,5},{5,6},{6,7},{11,8},{8,9},{9,10... | collective-permute-start | bytes 3145736 | tf_op jit(solution)/shard_map/ppermute | solution.py:72
  25.2 17.5 %collective-permute-start.9 = (bf16[4,128,1024]{2,1,0:T(8,128)(2,1)S(1)}, bf16[4,128,1024]{2,1,0:T(8,128)(2,1)S(1)}, u32[]{:S(2)}, u32[]{:S(2)}) collective-permute-start(bf16[4,128,1024]{2,1,0:T(8,128)(2,1)S(1)} %pad_maximum_fusion.refs_0_), channel_id=1, source_target_pairs={{1,0},{2,1},{3,2},{0,3},{5,4},{6,5},{7,6},{4,7},{9,8},{10,9},{11,1... | collective-permute-start | bytes 3145736 | tf_op jit(solution)/shard_map/ppermute | solution.py:72
  28.6 14.0 %collective-permute-start.8 = (bf16[8,128,256]{2,1,0:T(8,128)(2,1)S(1)}, bf16[8,128,256]{2,1,0:T(8,128)(2,1)S(1)}, u32[]{:S(2)}, u32[]{:S(2)}) collective-permute-start(bf16[8,128,256]{2,1,0:T(8,128)(2,1)S(1)} %get-tuple-element.31), channel_id=1, source_target_pairs={{0,64},{16,80},{64,0},{80,16},{1,65},{17,81},{65,1},{81,17},{2,66}... | collective-permute-start | bytes 1572872 | tf_op jit(solution)/shard_map/ppermute | solution.py:30
  42.6 1.0 copy-start
  42.6 1.3 %copy-start.2 = (bf16[4,128,1024]{2,1,0:T(8,128)(2,1)}, bf16[4,128,1024]{2,1,0:T(8,128)(2,1)S(1)}, u32[]{:S(2)}) copy-start(bf16[4,128,1024]{2,1,0:T(8,128)(2,1)S(1)} %collective-permute-done.9.refs_4_.refs_1_) | copy-start | bytes 3145732
  43.9 6.9 %collective-permute-start.11 = (bf16[32,128,256]{2,1,0:T(8,128)(2,1)S(1)}, bf16[32,128,256]{2,1,0:T(8,128)(2,1)}, u32[]{:S(2)}, u32[]{:S(2)}) collective-permute-start(bf16[32,128,256]{2,1,0:T(8,128)(2,1)S(1)} %join.1.ref.own), channel_id=1, source_target_pairs={{0,32},{32,0},{1,33},{33,1},{2,34},{34,2},{3,35},{35,3},{4,36},{36... | collective-permute-start | bytes 6291464 | tf_op jit(solution)/shard_map/ppermute | solution.py:30
  44.6 16.7 %collective-permute-start.12 = (bf16[4,128,1024]{2,1,0:T(8,128)(2,1)S(1)}, bf16[4,128,1024]{2,1,0:T(8,128)(2,1)}, u32[]{:S(2)}, u32[]{:S(2)}) collective-permute-start(bf16[4,128,1024]{2,1,0:T(8,128)(2,1)S(1)} %pad_maximum_fusion.refs_0_), channel_id=1, source_target_pairs={{2,0},{3,1},{0,2},{1,3},{6,4},{7,5},{4,6},{5,7},{10,8},{11,9},{8,1... | collective-permute-start | bytes 3145736 | tf_op jit(solution)/shard_map/ppermute | solution.py:72
  47.8 1.2 %collective-permute-start.7 = (s32[8,8]{1,0:T(8,128)S(1)}, s32[8,8]{1,0:T(8,128)S(1)}, u32[]{:S(2)}, u32[]{:S(2)}) collective-permute-start(s32[8,8]{1,0:T(8,128)S(1)} %collective-permute-done.6), channel_id=1, source_target_pairs={{0,32},{32,0},{1,33},{33,1},{2,34},{34,2},{3,35},{35,3},{4,36},{36... | collective-permute-start | bytes 776 | tf_op jit(solution)/shard_map/ppermute | solution.py:30
  50.8 2.8 %copy-start.1 = (bf16[4,128,1024]{2,1,0:T(8,128)(2,1)S(1)}, bf16[4,128,1024]{2,1,0:T(8,128)(2,1)}, u32[]{:S(2)}) copy-start(bf16[4,128,1024]{2,1,0:T(8,128)(2,1)} %copy-done) | copy-start | bytes 3145732
  50.8 2.8 %copy-start.3 = (bf16[4,128,1024]{2,1,0:T(8,128)(2,1)S(1)}, bf16[4,128,1024]{2,1,0:T(8,128)(2,1)}, u32[]{:S(2)}) copy-start(bf16[4,128,1024]{2,1,0:T(8,128)(2,1)} %copy-done.2) | copy-start | bytes 3145732
  50.8 2.8 %copy-start.5 = (f32[48,128]{1,0:T(8,128)S(1)}, f32[48,128]{1,0:T(8,128)}, u32[]{:S(2)}) copy-start(f32[48,128]{1,0:T(8,128)} %constant.160.clone.1.before_ref) | copy-start | bytes 73732
  64.7 1.5 %collective-permute-start.13 = (f32[48,128]{1,0:T(8,128)S(1)}, f32[48,128]{1,0:T(8,128)S(1)}, u32[]{:S(2)}, u32[]{:S(2)}) collective-permute-start(f32[48,128]{1,0:T(8,128)S(1)} %get-tuple-element.35.mine_ref), channel_id=1, source_target_pairs={{0,32},{32,0},{1,33},{33,1},{2,34},{34,2},{3,35},{35,3},{4,36},{36... | collective-permute-start | bytes 73736 | tf_op jit(solution)/shard_map/ppermute | solution.py:30
  70.2 15.7 %collective-permute-start.15 = (bf16[520,1024]{1,0:T(8,128)(2,1)S(1)}, bf16[520,1024]{1,0:T(8,128)(2,1)S(1)}, u32[]{:S(2)}, u32[]{:S(2)}) collective-permute-start(bf16[520,1024]{1,0:T(8,128)(2,1)S(1)} %get-tuple-element.43), channel_id=1, source_target_pairs={{8,0},{9,1},{10,2},{11,3},{12,4},{13,5},{14,6},{15,7},{0,8},{1,9},... | collective-permute-start | bytes 3194888 | tf_op jit(solution)/shard_map/ppermute | solution.py:72
  77.8 19.4 %collective-permute-start.14 = (bf16[520,1024]{1,0:T(8,128)(2,1)S(1)}, bf16[520,1024]{1,0:T(8,128)(2,1)S(1)}, u32[]{:S(2)}, u32[]{:S(2)}) collective-permute-start(bf16[520,1024]{1,0:T(8,128)(2,1)S(1)} %get-tuple-element.42), channel_id=1, source_target_pairs={{12,0},{13,1},{14,2},{15,3},{0,4},{1,5},{2,6},{3,7},{4,8},{5,9},{6... | collective-permute-start | bytes 3194888 | tf_op jit(solution)/shard_map/ppermute | solution.py:72
  78.3 18.9 %collective-permute-start.16 = (bf16[520,1024]{1,0:T(8,128)(2,1)S(1)}, bf16[520,1024]{1,0:T(8,128)(2,1)S(1)}, u32[]{:S(2)}, u32[]{:S(2)}) collective-permute-start(bf16[520,1024]{1,0:T(8,128)(2,1)S(1)} %get-tuple-element.44), channel_id=1, source_target_pairs={{4,0},{5,1},{6,2},{7,3},{8,4},{9,5},{10,6},{11,7},{12,8},{13,9},{1... | collective-permute-start | bytes 3194888 | tf_op jit(solution)/shard_map/ppermute | solution.py:72
  97.2 17.6 %copy-start.4 = (bf16[128,1024]{1,0:T(8,128)(2,1)S(1)}, bf16[128,1024]{1,0:T(8,128)(2,1)}, u32[]{:S(2)}) copy-start(bf16[128,1024]{1,0:T(8,128)(2,1)} %panel_ref.1) | copy-start | bytes 786436
  97.7 16.0 %collective-permute-start.17 = (bf16[136,1024]{1,0:T(8,128)(2,1)S(1)}, bf16[136,1024]{1,0:T(8,128)(2,1)S(1)}, u32[]{:S(2)}, u32[]{:S(2)}) collective-permute-start(bf16[136,1024]{1,0:T(8,128)(2,1)S(1)} %get-tuple-element.49), channel_id=1, source_target_pairs={{0,0},{1,1},{2,2},{3,3},{4,4},{5,5},{6,6},{7,7},{8,8},{9,9},{10,10... | collective-permute-start | bytes 835592 | tf_op jit(solution)/shard_map/ppermute | solution.py:84
  101.2 12.5 %collective-permute-start.18 = (bf16[136,1024]{1,0:T(8,128)(2,1)S(1)}, bf16[136,1024]{1,0:T(8,128)(2,1)S(1)}, u32[]{:S(2)}, u32[]{:S(2)}) collective-permute-start(bf16[136,1024]{1,0:T(8,128)(2,1)S(1)} %get-tuple-element.50), channel_id=1, source_target_pairs={{0,1},{1,2},{2,3},{3,0},{4,5},{5,6},{6,7},{7,4},{8,9},{9,10},{10,1... | collective-permute-start | bytes 835592 | tf_op jit(solution)/shard_map/ppermute | solution.py:84
  101.7 12.0 %collective-permute-start.19 = (bf16[136,1024]{1,0:T(8,128)(2,1)S(1)}, bf16[136,1024]{1,0:T(8,128)(2,1)S(1)}, u32[]{:S(2)}, u32[]{:S(2)}) collective-permute-start(bf16[136,1024]{1,0:T(8,128)(2,1)S(1)} %get-tuple-element.51), channel_id=1, source_target_pairs={{0,3},{1,0},{2,1},{3,2},{4,7},{5,4},{6,5},{7,6},{8,11},{9,8},{10,9... | collective-permute-start | bytes 835592 | tf_op jit(solution)/shard_map/ppermute | solution.py:84
  105.9 8.9 %collective-permute-start.20 = (bf16[136,1024]{1,0:T(8,128)(2,1)S(1)}, bf16[136,1024]{1,0:T(8,128)(2,1)S(1)}, u32[]{:S(2)}, u32[]{:S(2)}) collective-permute-start(bf16[136,1024]{1,0:T(8,128)(2,1)S(1)} %get-tuple-element.52), channel_id=1, source_target_pairs={{0,2},{1,3},{2,0},{3,1},{4,6},{5,7},{6,4},{7,5},{8,10},{9,11},{10,... | collective-permute-start | bytes 835592 | tf_op jit(solution)/shard_map/ppermute | solution.py:84
  108.2 5.5 %collective-permute-start.21 = (f32[8,128]{1,0:T(8,128)S(1)}, f32[8,128]{1,0:T(8,128)S(1)}, u32[]{:S(2)}, u32[]{:S(2)}) collective-permute-start(f32[8,128]{1,0:T(8,128)S(1)} %constant_dynamic-slice_fusion), channel_id=1, source_target_pairs={{0,0},{16,32},{32,16},{48,48},{1,1},{17,33},{33,17},{49,49},{2,2},... | collective-permute-start | bytes 12296 | tf_op jit(solution)/shard_map/ppermute | solution.py:34

commit v7 on v6

--- a/solution.py
+++ b/solution.py
@@ -89,9 +89,11 @@
         refs[6][8 * d : 8 * d + 8] = refs[d][...]
 
 
-def turn_kernel(ref, out):
+def turn_kernel(ref, out, *kept):
     def one(i, _):
         out[i] = ref[i].T
+        for copy in kept:
+            copy[i] = ref[i]
         return 0
 
     lax.fori_loop(0, 32, one, 0, unroll=4)
@@ -274,14 +276,17 @@
     )
     place = (table // 8 - y) % 4 * 8 + table % 8
 
-    turn = pl.pallas_call(
-        turn_kernel,
-        in_specs=[vmem],
-        out_specs=vmem,
-        out_shape=jax.ShapeDtypeStruct((32, SLICE, BLOCK), jnp.bfloat16),
-        compiler_params=pltpu.CompilerParams(vmem_limit_bytes=8 << 20),
-        name="turn",
-    )
+    def turn(points, kept):
+        straight = [jax.ShapeDtypeStruct((32, BLOCK, SLICE), jnp.bfloat16)] * kept
+        return pl.pallas_call(
+            turn_kernel,
+            in_specs=[vmem],
+            out_specs=[vmem] * (1 + kept),
+            out_shape=[jax.ShapeDtypeStruct((32, SLICE, BLOCK), jnp.bfloat16), *straight],
+            compiler_params=pltpu.CompilerParams(vmem_limit_bytes=8 << 20),
+            name="turn",
+        )(points)
+
     def scores_of(base, stat, held):
         return pl.pallas_call(
             functools.partial(score_kernel, base),
@@ -296,7 +301,7 @@
             name="scores",
         )(here, count, table, place, scale, own_t, oth_t, stat, *held)
 
-    own_t, oth_t = turn(own), turn(oth)
+    (own_t,), (oth_t, oth) = turn(own, 0), turn(oth, 1)
     low = jnp.full((STATS, BLOCK), LOW, jnp.float32)
     *near, stat = scores_of(0, jnp.concatenate([low, jnp.zeros_like(low)]), stacks[0:3])
     *far, stat = scores_of(3, stat, stacks[3:4])
@@ -320,8 +325,9 @@
             name="sums",
         )(here, count, table, place, own, oth, stat, stat_other, *near, *far)
 
-    pack_next, pack_last, pack_own, norm = sums_of((1, 3, 0), stat)
-    pack_far, _ = sums_of((2,), stat)
+    pack_far, norm = sums_of((2,), stat)
+    after = lax.optimization_barrier((stat, pack_far))[0]
+    pack_next, pack_last, pack_own, _ = sums_of((1, 3, 0), after)
     packs = [pack_own, pack_next, pack_far, pack_last]
     got = [packs[0]] + [shifted(packs[d], True, -d) for d in (1, 2, 3)]
     chunks = pl.pallas_call(

time: 117 us -> 115 us (0.983)
  Pallas kernels: 26.7 us -> 23.9 us
  starting transfers between devices: 43.4 us -> 44.8 us
    pallas_call x2, Pallas kernels: 10.3 us -> 8.16 us  [sums_of(): pl.pallas_call(functools.partial(sum_kernel, wanted), in_specs=[smem] * 4...]
    ppermute x6, starting transfers between devices: 4.78 us -> 6.58 us  [moved(): lax.ppermute(value, axis, [(i, (i - by) % size) for i in range(size)])]
    ppermute x9, waiting for transfers between devices: 21.6 us -> 19.9 us  [shifted(): return lax.ppermute(value, ('c', 'z', 'x'), pairs)]
where the time goes in v7:
time: 115 us; the launch traced here: 114 us
  starting transfers between devices  44.8 us (39%)
  waiting for transfers between devices  39.4 us (34%)
  Pallas kernels  23.9 us (21%)
  local copies, waits for them, and re-layouts  3.17 us (3%)
  between operations  1.65 us (1%)
    ppermute x9, waiting for transfers between devices, shifted(): return lax.ppermute(value, ('c', 'z', 'x'), pairs)  19.9 us
    ppermute x9, starting transfers between devices, shifted(): return lax.ppermute(value, ('c', 'z', 'x'), pairs)  15 us
    ppermute x3, starting transfers between devices, swapped(): return lax.ppermute(value, ('c', 'yl'), [(0, 0), (1, 2), (2, 1), (3, 3)])  13.5 us
    ppermute x6, waiting for transfers between devices, moved(): lax.ppermute(value, axis, [(i, (i - by) % size) for i in range(size)])  13.4 us
    pallas_call x2, Pallas kernels, scores_of(): pl.pallas_call(functools.partial(score_kernel, base), in_specs=[smem] * 5...  10.5 us
    ppermute x4, starting transfers between devices, homeward(): return lax.ppermute(value, ('c', 'yl', 'z', 'x'), pairs)  9.75 us
    pallas_call x2, Pallas kernels, sums_of(): pl.pallas_call(functools.partial(sum_kernel, wanted), in_specs=[smem] * 4...  8.16 us
    ppermute x6, starting transfers between devices, moved(): lax.ppermute(value, axis, [(i, (i - by) % size) for i in range(size)])  6.58 us
  transfers between devices with their start and end apart: 22, of which 10 were waited for; matrix products, arithmetic and copies ran while one was open for 2% of the time, Pallas kernels for 15%

profile of v7, /device:TPU:1, one launch (start us, length us, event | category | flops | bytes accessed | tf_op | source)
XLA Modules:
  0.0 114.0 jit_solution(2911033133883970391)
XLA Ops:
  0.6 4.6 %collective-permute-start = (bf16[128,1024]{1,0:T(8,128)(2,1)}, bf16[128,1024]{1,0:T(8,128)(2,1)S(1)}, u32[]{:S(2)}, u32[]{:S(2)}) collective-permute-start(bf16[128,1024]{1,0:T(8,128)(2,1)} %panel_ref.1), channel_id=1, source_target_pairs={{0,0},{16,32},{32,16},{48,48},{1,1},{17,33},{33,17},{49,49},{2,2},... | collective-permute-start | bytes 786440 | tf_op jit(solution)/shard_map/ppermute | solution.py:34
  5.3 1.7 %dynamic-slice_bitcast_fusion = (bf16[8,128,256]{2,1,0:T(8,128)(2,1)S(1)}, bf16[8,128,256]{2,1,0:T(8,128)(2,1)S(1)}, bf16[8,128,256]{2,1,0:T(8,128)(2,1)S(1)}, bf16[8,128,256]{2,1,0:T(8,128)(2,1)S(1)}) fusion(bf16[4,8,128,256]{3,2,1,0:T(8,128)(2,1)} %bitcast.22, s32[]{:T(128)S(6)} %select_n.159, s32[]{:T(128)S(6)} %select_n.157, s32[]{:T(128)S(6)} %select_n.155, ...), kind=kLoop, calls=%fused_computation.1 | loop fusion | bytes 4194320 | tf_op jit(solution)/shard_map/jit(dynamic_index_in_dim)/squeeze | solution.py:247
  7.0 0.6 collective-permute-start.4
  7.5 1.0 collective-permute-start.5
  8.5 1.0 collective-permute-done
  9.5 1.2 %collective-permute-start.3 = (bf16[128,1024]{1,0:T(8,128)(2,1)S(1)}, bf16[128,1024]{1,0:T(8,128)(2,1)S(1)}, u32[]{:S(2)}, u32[]{:S(2)}) collective-permute-start(bf16[128,1024]{1,0:T(8,128)(2,1)S(1)} %collective-permute-done), channel_id=1, source_target_pairs={{12,0},{13,1},{14,2},{15,3},{0,4},{1,5},{2,6},{3,7},{4,8},{5,9},{6... | collective-permute-start | bytes 786440 | tf_op jit(solution)/shard_map/ppermute | solution.py:72
  10.7 2.5 %collective-permute-start.2 = (bf16[128,1024]{1,0:T(8,128)(2,1)S(1)}, bf16[128,1024]{1,0:T(8,128)(2,1)S(1)}, u32[]{:S(2)}, u32[]{:S(2)}) collective-permute-start(bf16[128,1024]{1,0:T(8,128)(2,1)S(1)} %collective-permute-done), channel_id=1, source_target_pairs={{8,0},{9,1},{10,2},{11,3},{12,4},{13,5},{14,6},{15,7},{0,8},{1,9},... | collective-permute-start | bytes 786440 | tf_op jit(solution)/shard_map/ppermute | solution.py:72
  13.1 1.2 %collective-permute-start.1 = (bf16[128,1024]{1,0:T(8,128)(2,1)S(1)}, bf16[128,1024]{1,0:T(8,128)(2,1)S(1)}, u32[]{:S(2)}, u32[]{:S(2)}) collective-permute-start(bf16[128,1024]{1,0:T(8,128)(2,1)S(1)} %collective-permute-done), channel_id=1, source_target_pairs={{4,0},{5,1},{6,2},{7,3},{8,4},{9,5},{10,6},{11,7},{12,8},{13,9},{1... | collective-permute-start | bytes 786440 | tf_op jit(solution)/shard_map/ppermute | solution.py:72
  14.3 1.9 %collective-permute-done.3 = bf16[128,1024]{1,0:T(8,128)(2,1)S(1)} collective-permute-done((bf16[128,1024]{1,0:T(8,128)(2,1)S(1)}, bf16[128,1024]{1,0:T(8,128)(2,1)S(1)}, u32[]{:S(2)}, u32[]{:S(2)}) %collective-permute-start.3) | collective-permute-done | bytes 262176 | tf_op jit(solution)/shard_map/ppermute | solution.py:72
  16.2 5.3 %collective-permute-start.6 = (s32[8,8]{1,0:T(8,128)S(1)}, s32[8,8]{1,0:T(8,128)S(1)}, u32[]{:S(2)}, u32[]{:S(2)}) collective-permute-start(s32[8,8]{1,0:T(8,128)S(1)} %copy-done.6), channel_id=1, source_target_pairs={{0,0},{16,32},{32,16},{48,48},{1,1},{17,33},{33,17},{49,49},{2,2},... | collective-permute-start | bytes 776 | tf_op jit(solution)/shard_map/ppermute | solution.py:34
  21.5 0.0 collective-permute-done.2
  21.5 0.0 collective-permute-done.1
  21.5 0.1 pad_maximum_fusion.refs_0_
  21.7 1.1 collective-permute-done.6
  22.8 0.0 collective-permute-done.4.refs_1_
  22.8 0.0 collective-permute-done.5.refs_3_
  22.8 2.4 %collective-permute-start.9 = (bf16[4,128,1024]{2,1,0:T(8,128)(2,1)S(1)}, bf16[4,128,1024]{2,1,0:T(8,128)(2,1)S(1)}, u32[]{:S(2)}, u32[]{:S(2)}) collective-permute-start(bf16[4,128,1024]{2,1,0:T(8,128)(2,1)S(1)} %pad_maximum_fusion.refs_0_), channel_id=1, source_target_pairs={{1,0},{2,1},{3,2},{0,3},{5,4},{6,5},{7,6},{4,7},{9,8},{10,9},{11,1... | collective-permute-start | bytes 3145736 | tf_op jit(solution)/shard_map/ppermute | solution.py:72
  25.2 0.0 collective-permute-start.10
  25.2 2.9 %collective-permute-start.8 = (bf16[8,128,256]{2,1,0:T(8,128)(2,1)S(1)}, bf16[8,128,256]{2,1,0:T(8,128)(2,1)S(1)}, u32[]{:S(2)}, u32[]{:S(2)}) collective-permute-start(bf16[8,128,256]{2,1,0:T(8,128)(2,1)S(1)} %get-tuple-element.34), channel_id=1, source_target_pairs={{0,64},{16,80},{64,0},{80,16},{1,65},{17,81},{65,1},{81,17},{2,66}... | collective-permute-start | bytes 1572872 | tf_op jit(solution)/shard_map/ppermute | solution.py:30
  28.1 11.4 %collective-permute-done.8.refs_2_ = bf16[8,128,256]{2,1,0:T(8,128)(2,1)S(1)} collective-permute-done((bf16[8,128,256]{2,1,0:T(8,128)(2,1)S(1)}, bf16[8,128,256]{2,1,0:T(8,128)(2,1)S(1)}, u32[]{:S(2)}, u32[]{:S(2)}) %collective-permute-start.8) | collective-permute-done | bytes 524320 | tf_op jit(solution)/shard_map/ppermute | solution.py:30
  39.5 0.0 collective-permute-done.9.refs_4_.refs_1_
  39.5 0.8 collective-permute-done.10.refs_5_.refs_2_
  40.4 0.1 join.1.ref.own
  40.5 0.0 copy-done
  40.5 0.8 copy-done.2
  41.3 1.5 %collective-permute-start.11 = (bf16[32,128,256]{2,1,0:T(8,128)(2,1)S(1)}, bf16[32,128,256]{2,1,0:T(8,128)(2,1)}, u32[]{:S(2)}, u32[]{:S(2)}) collective-permute-start(bf16[32,128,256]{2,1,0:T(8,128)(2,1)S(1)} %join.1.ref.own), channel_id=1, source_target_pairs={{0,32},{32,0},{1,33},{33,1},{2,34},{34,2},{3,35},{35,3},{4,36},{36... | collective-permute-start | bytes 6291464 | tf_op jit(solution)/shard_map/ppermute | solution.py:30
  43.5 3.7 %collective-permute-start.12 = (bf16[4,128,1024]{2,1,0:T(8,128)(2,1)S(1)}, bf16[4,128,1024]{2,1,0:T(8,128)(2,1)}, u32[]{:S(2)}, u32[]{:S(2)}) collective-permute-start(bf16[4,128,1024]{2,1,0:T(8,128)(2,1)S(1)} %pad_maximum_fusion.refs_0_), channel_id=1, source_target_pairs={{2,0},{3,1},{0,2},{1,3},{6,4},{7,5},{4,6},{5,7},{10,8},{11,9},{8,1... | collective-permute-start | bytes 3145736 | tf_op jit(solution)/shard_map/ppermute | solution.py:72
  47.2 0.1 pad_maximum_fusion.1.scale_ref
  47.3 0.1 pad_add_fusion.here_ref
  47.4 0.0 collective-permute-start.7
  47.4 1.1 %collective-permute-done.7 = s32[8,8]{1,0:T(8,128)S(1)} collective-permute-done((s32[8,8]{1,0:T(8,128)S(1)}, s32[8,8]{1,0:T(8,128)S(1)}, u32[]{:S(2)}, u32[]{:S(2)}) %collective-permute-start.7) | collective-permute-done | bytes 288 | tf_op jit(solution)/shard_map/ppermute | solution.py:30
  48.6 0.1 copy.16
  48.7 0.2 reduce_window_sum.11
  48.9 0.1 convert_reduce_fusion.count_ref
  49.0 0.4 select_reduce_fusion
  49.4 0.0 copy-start.5
  49.4 1.0 turn.3.own
  50.4 0.0 collective-permute-done.11.ref
  50.4 2.7 %turn.2 = (bf16[32,256,128]{2,1,0:T(8,128)(2,1)S(1)}, bf16[32,128,256]{2,1,0:T(8,128)(2,1)S(1)}) custom-call(bf16[32,128,256]{2,1,0:T(8,128)(2,1)} %collective-permute-done.11.ref), custom_call_target="tpu_custom_call" | custom-call | tf_op jit(solution)/shard_map/turn/pallas_call | solution.py:281
  53.1 6.9 %scores.2 = (f32[12,128,1024]{2,1,0:T(8,128)S(1)}, f32[12,8,1024]{2,1,0:T(8,128)S(1)}, f32[48,128]{1,0:T(8,128)S(1)}) custom-call(s32[2]{0:T(128)S(1)} %pad_add_fusion.here_ref, s32[16]{0:T(128)S(1)} %convert_reduce_fusion.count_ref, s32[16,8]{1,0:T(8,128)S(1)} %get-tuple-element.65.list_ref, s32[16,8]{1,0:T(8,128)S(1)} %get-tuple-element.64.place_ref, ...), custom_call_target="tpu_custom_call" | custom-call | tf_op jit(solution)/shard_map/scores/pallas_call | solution.py:291
  60.1 0.0 collective-permute-done.12.refs_0_
  60.1 3.6 %scores.3 = (f32[4,128,1024]{2,1,0:T(8,128)S(1)}, f32[4,8,1024]{2,1,0:T(8,128)S(1)}, f32[48,128]{1,0:T(8,128)S(1)}) custom-call(s32[2]{0:T(128)S(1)} %pad_add_fusion.here_ref, s32[16]{0:T(128)S(1)} %convert_reduce_fusion.count_ref, s32[16,8]{1,0:T(8,128)S(1)} %get-tuple-element.65.list_ref, s32[16,8]{1,0:T(8,128)S(1)} %get-tuple-element.64.place_ref, ...), custom_call_target="tpu_custom_call" | custom-call | tf_op jit(solution)/shard_map/scores/pallas_call | solution.py:291
  63.7 0.6 collective-permute-start.13
  64.3 0.8 collective-permute-done.13.other_ref
  65.2 2.2 %sums.2 = (bf16[520,1024]{1,0:T(8,128)(2,1)S(1)}, f32[16,128]{1,0:T(8,128)S(1)}) custom-call(s32[2]{0:T(128)S(1)} %pad_add_fusion.here_ref, s32[16]{0:T(128)S(1)} %convert_reduce_fusion.count_ref, s32[16,8]{1,0:T(8,128)S(1)} %get-tuple-element.65.list_ref, s32[16,8]{1,0:T(8,128)S(1)} %get-tuple-element.64.place_ref, bf16[32,128,256]{2,1,0:T(8,128)(2,1)S(1)} %join.1.ref.own, ...), custom_call_target="tpu_custom_call" | custom-call | flops 4000000000 | bytes 16000000 | tf_op jit(solution)/shard_map/sums/pallas_call | solution.py:311
  67.4 1.4 %collective-permute-start.15 = (bf16[520,1024]{1,0:T(8,128)(2,1)S(1)}, bf16[520,1024]{1,0:T(8,128)(2,1)S(1)}, u32[]{:S(2)}, u32[]{:S(2)}) collective-permute-start(bf16[520,1024]{1,0:T(8,128)(2,1)S(1)} %get-tuple-element.46), channel_id=1, source_target_pairs={{8,0},{9,1},{10,2},{11,3},{12,4},{13,5},{14,6},{15,7},{0,8},{1,9},... | collective-permute-start | bytes 3194888 | tf_op jit(solution)/shard_map/ppermute | solution.py:72
  68.8 5.9 %sums.3 = (bf16[520,1024]{1,0:T(8,128)(2,1)S(1)}, bf16[520,1024]{1,0:T(8,128)(2,1)S(1)}, bf16[520,1024]{1,0:T(8,128)(2,1)S(1)}, f32[16,128]{1,0:T(8,128)}) custom-call(s32[2]{0:T(128)S(1)} %pad_add_fusion.here_ref, s32[16]{0:T(128)S(1)} %convert_reduce_fusion.count_ref, s32[16,8]{1,0:T(8,128)S(1)} %get-tuple-element.65.list_ref, ...), custom_call_target="tpu_custom_call" | custom-call | flops 4000000000 | bytes 16000000 | tf_op jit(solution)/shard_map/sums/pallas_call | solution.py:311
  74.7 0.7 collective-permute-start.14
  75.4 2.0 %collective-permute-start.16 = (bf16[520,1024]{1,0:T(8,128)(2,1)S(1)}, bf16[520,1024]{1,0:T(8,128)(2,1)S(1)}, u32[]{:S(2)}, u32[]{:S(2)}) collective-permute-start(bf16[520,1024]{1,0:T(8,128)(2,1)S(1)} %get-tuple-element.50), channel_id=1, source_target_pairs={{4,0},{5,1},{6,2},{7,3},{8,4},{9,5},{10,6},{11,7},{12,8},{13,9},{1... | collective-permute-start | bytes 3194888 | tf_op jit(solution)/shard_map/ppermute | solution.py:72
  77.4 17.1 %collective-permute-done.14.refs_1_ = bf16[520,1024]{1,0:T(8,128)(2,1)S(1)} collective-permute-done((bf16[520,1024]{1,0:T(8,128)(2,1)S(1)}, bf16[520,1024]{1,0:T(8,128)(2,1)S(1)}, u32[]{:S(2)}, u32[]{:S(2)}) %collective-permute-start.14) | collective-permute-done | bytes 1064992 | tf_op jit(solution)/shard_map/ppermute | solution.py:72
  94.5 0.0 collective-permute-done.15.refs_2_
  94.5 0.0 collective-permute-done.16.refs_3_
  94.5 0.5 fold.1
  95.1 3.8 %collective-permute-start.17 = (bf16[136,1024]{1,0:T(8,128)(2,1)S(1)}, bf16[136,1024]{1,0:T(8,128)(2,1)S(1)}, u32[]{:S(2)}, u32[]{:S(2)}) collective-permute-start(bf16[136,1024]{1,0:T(8,128)(2,1)S(1)} %get-tuple-element.55), channel_id=1, source_target_pairs={{0,0},{1,1},{2,2},{3,3},{4,4},{5,5},{6,6},{7,7},{8,8},{9,9},{10,10... | collective-permute-start | bytes 835592 | tf_op jit(solution)/shard_map/ppermute | solution.py:84
  98.9 0.7 collective-permute-start.18
  99.6 3.2 %collective-permute-start.19 = (bf16[136,1024]{1,0:T(8,128)(2,1)S(1)}, bf16[136,1024]{1,0:T(8,128)(2,1)S(1)}, u32[]{:S(2)}, u32[]{:S(2)}) collective-permute-start(bf16[136,1024]{1,0:T(8,128)(2,1)S(1)} %get-tuple-element.57), channel_id=1, source_target_pairs={{0,3},{1,0},{2,1},{3,2},{4,7},{5,4},{6,5},{7,6},{8,11},{9,8},{10,9... | collective-permute-start | bytes 835592 | tf_op jit(solution)/shard_map/ppermute | solution.py:84
  102.7 2.1 %collective-permute-start.20 = (bf16[136,1024]{1,0:T(8,128)(2,1)S(1)}, bf16[136,1024]{1,0:T(8,128)(2,1)S(1)}, u32[]{:S(2)}, u32[]{:S(2)}) collective-permute-start(bf16[136,1024]{1,0:T(8,128)(2,1)S(1)} %get-tuple-element.58), channel_id=1, source_target_pairs={{0,2},{1,3},{2,0},{3,1},{4,6},{5,7},{6,4},{7,5},{8,10},{9,11},{10,... | collective-permute-start | bytes 835592 | tf_op jit(solution)/shard_map/ppermute | solution.py:84
  104.8 3.6 %collective-permute-start.21 = (f32[8,128]{1,0:T(8,128)S(1)}, f32[8,128]{1,0:T(8,128)S(1)}, u32[]{:S(2)}, u32[]{:S(2)}) collective-permute-start(f32[8,128]{1,0:T(8,128)S(1)} %constant_dynamic-slice_fusion), channel_id=1, source_target_pairs={{0,0},{16,32},{32,16},{48,48},{1,1},{17,33},{33,17},{49,49},{2,2},... | collective-permute-start | bytes 12296 | tf_op jit(solution)/shard_map/ppermute | solution.py:34
  108.5 2.9 %collective-permute-done.21 = f32[8,128]{1,0:T(8,128)S(1)} collective-permute-done((f32[8,128]{1,0:T(8,128)S(1)}, f32[8,128]{1,0:T(8,128)S(1)}, u32[]{:S(2)}, u32[]{:S(2)}) %collective-permute-start.21) | collective-permute-done | bytes 4128 | tf_op jit(solution)/shard_map/ppermute | solution.py:34
  111.4 0.0 collective-permute-done.17.refs_0_
  111.4 0.0 collective-permute-done.18.refs_1_
  111.4 1.1 collective-permute-done.20.refs_3_
  112.5 0.9 finish.1
  113.4 0.6 copy.20
  (19 shorter events, 0.1 us)
Async XLA Ops:
  0.6 8.9 %collective-permute-start = (bf16[128,1024]{1,0:T(8,128)(2,1)}, bf16[128,1024]{1,0:T(8,128)(2,1)S(1)}, u32[]{:S(2)}, u32[]{:S(2)}) collective-permute-start(bf16[128,1024]{1,0:T(8,128)(2,1)} %panel_ref.1), channel_id=1, source_target_pairs={{0,0},{16,32},{32,16},{48,48},{1,1},{17,33},{33,17},{49,49},{2,2},... | collective-permute-start | bytes 786440 | tf_op jit(solution)/shard_map/ppermute | solution.py:34
  5.3 10.9 %copy-start.6 = (s32[8,8]{1,0:T(8,128)S(1)}, s32[8,8]{1,0:T(8,128)}, u32[]{:S(2)}) copy-start(s32[8,8]{1,0:T(8,128)} %param.6) | copy-start | bytes 772
  7.0 15.8 %collective-permute-start.4 = (bf16[8,128,256]{2,1,0:T(8,128)(2,1)S(1)}, bf16[8,128,256]{2,1,0:T(8,128)(2,1)S(1)}, u32[]{:S(2)}, u32[]{:S(2)}) collective-permute-start(bf16[8,128,256]{2,1,0:T(8,128)(2,1)S(1)} %get-tuple-element.62), channel_id=1, source_target_pairs={{0,80},{16,0},{64,16},{80,64},{1,81},{17,1},{65,17},{81,65},{2,82}... | collective-permute-start | bytes 1572872 | tf_op jit(solution)/shard_map/ppermute | solution.py:30
  7.5 15.3 %collective-permute-start.5 = (bf16[8,128,256]{2,1,0:T(8,128)(2,1)S(1)}, bf16[8,128,256]{2,1,0:T(8,128)(2,1)S(1)}, u32[]{:S(2)}, u32[]{:S(2)}) collective-permute-start(bf16[8,128,256]{2,1,0:T(8,128)(2,1)S(1)} %get-tuple-element.60), channel_id=1, source_target_pairs={{0,16},{16,64},{64,80},{80,0},{1,17},{17,65},{65,81},{81,1},{2,18}... | collective-permute-start | bytes 1572872 | tf_op jit(solution)/shard_map/ppermute | solution.py:30
  9.5 6.7 %collective-permute-start.3 = (bf16[128,1024]{1,0:T(8,128)(2,1)S(1)}, bf16[128,1024]{1,0:T(8,128)(2,1)S(1)}, u32[]{:S(2)}, u32[]{:S(2)}) collective-permute-start(bf16[128,1024]{1,0:T(8,128)(2,1)S(1)} %collective-permute-done), channel_id=1, source_target_pairs={{12,0},{13,1},{14,2},{15,3},{0,4},{1,5},{2,6},{3,7},{4,8},{5,9},{6... | collective-permute-start | bytes 786440 | tf_op jit(solution)/shard_map/ppermute | solution.py:72
  10.7 10.8 %collective-permute-start.2 = (bf16[128,1024]{1,0:T(8,128)(2,1)S(1)}, bf16[128,1024]{1,0:T(8,128)(2,1)S(1)}, u32[]{:S(2)}, u32[]{:S(2)}) collective-permute-start(bf16[128,1024]{1,0:T(8,128)(2,1)S(1)} %collective-permute-done), channel_id=1, source_target_pairs={{8,0},{9,1},{10,2},{11,3},{12,4},{13,5},{14,6},{15,7},{0,8},{1,9},... | collective-permute-start | bytes 786440 | tf_op jit(solution)/shard_map/ppermute | solution.py:72
  13.1 8.4 %collective-permute-start.1 = (bf16[128,1024]{1,0:T(8,128)(2,1)S(1)}, bf16[128,1024]{1,0:T(8,128)(2,1)S(1)}, u32[]{:S(2)}, u32[]{:S(2)}) collective-permute-start(bf16[128,1024]{1,0:T(8,128)(2,1)S(1)} %collective-permute-done), channel_id=1, source_target_pairs={{4,0},{5,1},{6,2},{7,3},{8,4},{9,5},{10,6},{11,7},{12,8},{13,9},{1... | collective-permute-start | bytes 786440 | tf_op jit(solution)/shard_map/ppermute | solution.py:72
  16.2 6.6 %collective-permute-start.6 = (s32[8,8]{1,0:T(8,128)S(1)}, s32[8,8]{1,0:T(8,128)S(1)}, u32[]{:S(2)}, u32[]{:S(2)}) collective-permute-start(s32[8,8]{1,0:T(8,128)S(1)} %copy-done.6), channel_id=1, source_target_pairs={{0,0},{16,32},{32,16},{48,48},{1,1},{17,33},{33,17},{49,49},{2,2},... | collective-permute-start | bytes 776 | tf_op jit(solution)/shard_map/ppermute | solution.py:34
  22.8 16.7 %collective-permute-start.9 = (bf16[4,128,1024]{2,1,0:T(8,128)(2,1)S(1)}, bf16[4,128,1024]{2,1,0:T(8,128)(2,1)S(1)}, u32[]{:S(2)}, u32[]{:S(2)}) collective-permute-start(bf16[4,128,1024]{2,1,0:T(8,128)(2,1)S(1)} %pad_maximum_fusion.refs_0_), channel_id=1, source_target_pairs={{1,0},{2,1},{3,2},{0,3},{5,4},{6,5},{7,6},{4,7},{9,8},{10,9},{11,1... | collective-permute-start | bytes 3145736 | tf_op jit(solution)/shard_map/ppermute | solution.py:72
  25.2 15.2 %collective-permute-start.10 = (bf16[4,128,1024]{2,1,0:T(8,128)(2,1)S(1)}, bf16[4,128,1024]{2,1,0:T(8,128)(2,1)S(1)}, u32[]{:S(2)}, u32[]{:S(2)}) collective-permute-start(bf16[4,128,1024]{2,1,0:T(8,128)(2,1)S(1)} %pad_maximum_fusion.refs_0_), channel_id=1, source_target_pairs={{3,0},{0,1},{1,2},{2,3},{7,4},{4,5},{5,6},{6,7},{11,8},{8,9},{9,10... | collective-permute-start | bytes 3145736 | tf_op jit(solution)/shard_map/ppermute | solution.py:72
  25.2 14.3 %collective-permute-start.8 = (bf16[8,128,256]{2,1,0:T(8,128)(2,1)S(1)}, bf16[8,128,256]{2,1,0:T(8,128)(2,1)S(1)}, u32[]{:S(2)}, u32[]{:S(2)}) collective-permute-start(bf16[8,128,256]{2,1,0:T(8,128)(2,1)S(1)} %get-tuple-element.34), channel_id=1, source_target_pairs={{0,64},{16,80},{64,0},{80,16},{1,65},{17,81},{65,1},{81,17},{2,66}... | collective-permute-start | bytes 1572872 | tf_op jit(solution)/shard_map/ppermute | solution.py:30
  39.5 1.0 copy-start
  40.3 1.0 copy-start.2
  41.3 9.1 %collective-permute-start.11 = (bf16[32,128,256]{2,1,0:T(8,128)(2,1)S(1)}, bf16[32,128,256]{2,1,0:T(8,128)(2,1)}, u32[]{:S(2)}, u32[]{:S(2)}) collective-permute-start(bf16[32,128,256]{2,1,0:T(8,128)(2,1)S(1)} %join.1.ref.own), channel_id=1, source_target_pairs={{0,32},{32,0},{1,33},{33,1},{2,34},{34,2},{3,35},{35,3},{4,36},{36... | collective-permute-start | bytes 6291464 | tf_op jit(solution)/shard_map/ppermute | solution.py:30
  43.5 16.6 %collective-permute-start.12 = (bf16[4,128,1024]{2,1,0:T(8,128)(2,1)S(1)}, bf16[4,128,1024]{2,1,0:T(8,128)(2,1)}, u32[]{:S(2)}, u32[]{:S(2)}) collective-permute-start(bf16[4,128,1024]{2,1,0:T(8,128)(2,1)S(1)} %pad_maximum_fusion.refs_0_), channel_id=1, source_target_pairs={{2,0},{3,1},{0,2},{1,3},{6,4},{7,5},{4,6},{5,7},{10,8},{11,9},{8,1... | collective-permute-start | bytes 3145736 | tf_op jit(solution)/shard_map/ppermute | solution.py:72
  47.4 1.2 %collective-permute-start.7 = (s32[8,8]{1,0:T(8,128)S(1)}, s32[8,8]{1,0:T(8,128)S(1)}, u32[]{:S(2)}, u32[]{:S(2)}) collective-permute-start(s32[8,8]{1,0:T(8,128)S(1)} %collective-permute-done.6), channel_id=1, source_target_pairs={{0,32},{32,0},{1,33},{33,1},{2,34},{34,2},{3,35},{35,3},{4,36},{36... | collective-permute-start | bytes 776 | tf_op jit(solution)/shard_map/ppermute | solution.py:30
  49.4 3.7 %copy-start.5 = (f32[48,128]{1,0:T(8,128)S(1)}, f32[48,128]{1,0:T(8,128)}, u32[]{:S(2)}) copy-start(f32[48,128]{1,0:T(8,128)} %constant.160.clone.1.before_ref) | copy-start | bytes 73732
  50.4 2.8 %copy-start.1 = (bf16[4,128,1024]{2,1,0:T(8,128)(2,1)S(1)}, bf16[4,128,1024]{2,1,0:T(8,128)(2,1)}, u32[]{:S(2)}) copy-start(bf16[4,128,1024]{2,1,0:T(8,128)(2,1)} %copy-done) | copy-start | bytes 3145732
  50.4 2.8 %copy-start.3 = (bf16[4,128,1024]{2,1,0:T(8,128)(2,1)S(1)}, bf16[4,128,1024]{2,1,0:T(8,128)(2,1)}, u32[]{:S(2)}) copy-start(bf16[4,128,1024]{2,1,0:T(8,128)(2,1)} %copy-done.2) | copy-start | bytes 3145732
  63.7 1.5 %collective-permute-start.13 = (f32[48,128]{1,0:T(8,128)S(1)}, f32[48,128]{1,0:T(8,128)S(1)}, u32[]{:S(2)}, u32[]{:S(2)}) collective-permute-start(f32[48,128]{1,0:T(8,128)S(1)} %get-tuple-element.47.mine_ref), channel_id=1, source_target_pairs={{0,32},{32,0},{1,33},{33,1},{2,34},{34,2},{3,35},{35,3},{4,36},{36... | collective-permute-start | bytes 73736 | tf_op jit(solution)/shard_map/ppermute | solution.py:30
  67.4 27.1 %collective-permute-start.15 = (bf16[520,1024]{1,0:T(8,128)(2,1)S(1)}, bf16[520,1024]{1,0:T(8,128)(2,1)S(1)}, u32[]{:S(2)}, u32[]{:S(2)}) collective-permute-start(bf16[520,1024]{1,0:T(8,128)(2,1)S(1)} %get-tuple-element.46), channel_id=1, source_target_pairs={{8,0},{9,1},{10,2},{11,3},{12,4},{13,5},{14,6},{15,7},{0,8},{1,9},... | collective-permute-start | bytes 3194888 | tf_op jit(solution)/shard_map/ppermute | solution.py:72
  74.7 19.8 %collective-permute-start.14 = (bf16[520,1024]{1,0:T(8,128)(2,1)S(1)}, bf16[520,1024]{1,0:T(8,128)(2,1)S(1)}, u32[]{:S(2)}, u32[]{:S(2)}) collective-permute-start(bf16[520,1024]{1,0:T(8,128)(2,1)S(1)} %get-tuple-element.49), channel_id=1, source_target_pairs={{12,0},{13,1},{14,2},{15,3},{0,4},{1,5},{2,6},{3,7},{4,8},{5,9},{6... | collective-permute-start | bytes 3194888 | tf_op jit(solution)/shard_map/ppermute | solution.py:72
  75.4 19.1 %collective-permute-start.16 = (bf16[520,1024]{1,0:T(8,128)(2,1)S(1)}, bf16[520,1024]{1,0:T(8,128)(2,1)S(1)}, u32[]{:S(2)}, u32[]{:S(2)}) collective-permute-start(bf16[520,1024]{1,0:T(8,128)(2,1)S(1)} %get-tuple-element.50), channel_id=1, source_target_pairs={{4,0},{5,1},{6,2},{7,3},{8,4},{9,5},{10,6},{11,7},{12,8},{13,9},{1... | collective-permute-start | bytes 3194888 | tf_op jit(solution)/shard_map/ppermute | solution.py:72
  94.5 17.9 %copy-start.4 = (bf16[128,1024]{1,0:T(8,128)(2,1)S(1)}, bf16[128,1024]{1,0:T(8,128)(2,1)}, u32[]{:S(2)}) copy-start(bf16[128,1024]{1,0:T(8,128)(2,1)} %panel_ref.1) | copy-start | bytes 786436
  95.1 16.3 %collective-permute-start.17 = (bf16[136,1024]{1,0:T(8,128)(2,1)S(1)}, bf16[136,1024]{1,0:T(8,128)(2,1)S(1)}, u32[]{:S(2)}, u32[]{:S(2)}) collective-permute-start(bf16[136,1024]{1,0:T(8,128)(2,1)S(1)} %get-tuple-element.55), channel_id=1, source_target_pairs={{0,0},{1,1},{2,2},{3,3},{4,4},{5,5},{6,6},{7,7},{8,8},{9,9},{10,10... | collective-permute-start | bytes 835592 | tf_op jit(solution)/shard_map/ppermute | solution.py:84
  98.9 12.5 %collective-permute-start.18 = (bf16[136,1024]{1,0:T(8,128)(2,1)S(1)}, bf16[136,1024]{1,0:T(8,128)(2,1)S(1)}, u32[]{:S(2)}, u32[]{:S(2)}) collective-permute-start(bf16[136,1024]{1,0:T(8,128)(2,1)S(1)} %get-tuple-element.56), channel_id=1, source_target_pairs={{0,1},{1,2},{2,3},{3,0},{4,5},{5,6},{6,7},{7,4},{8,9},{9,10},{10,1... | collective-permute-start | bytes 835592 | tf_op jit(solution)/shard_map/ppermute | solution.py:84
  99.6 11.8 %collective-permute-start.19 = (bf16[136,1024]{1,0:T(8,128)(2,1)S(1)}, bf16[136,1024]{1,0:T(8,128)(2,1)S(1)}, u32[]{:S(2)}, u32[]{:S(2)}) collective-permute-start(bf16[136,1024]{1,0:T(8,128)(2,1)S(1)} %get-tuple-element.57), channel_id=1, source_target_pairs={{0,3},{1,0},{2,1},{3,2},{4,7},{5,4},{6,5},{7,6},{8,11},{9,8},{10,9... | collective-permute-start | bytes 835592 | tf_op jit(solution)/shard_map/ppermute | solution.py:84
  102.7 9.7 %collective-permute-start.20 = (bf16[136,1024]{1,0:T(8,128)(2,1)S(1)}, bf16[136,1024]{1,0:T(8,128)(2,1)S(1)}, u32[]{:S(2)}, u32[]{:S(2)}) collective-permute-start(bf16[136,1024]{1,0:T(8,128)(2,1)S(1)} %get-tuple-element.58), channel_id=1, source_target_pairs={{0,2},{1,3},{2,0},{3,1},{4,6},{5,7},{6,4},{7,5},{8,10},{9,11},{10,... | collective-permute-start | bytes 835592 | tf_op jit(solution)/shard_map/ppermute | solution.py:84
  104.8 6.5 %collective-permute-start.21 = (f32[8,128]{1,0:T(8,128)S(1)}, f32[8,128]{1,0:T(8,128)S(1)}, u32[]{:S(2)}, u32[]{:S(2)}) collective-permute-start(f32[8,128]{1,0:T(8,128)S(1)} %constant_dynamic-slice_fusion), channel_id=1, source_target_pairs={{0,0},{16,32},{32,16},{48,48},{1,1},{17,33},{33,17},{49,49},{2,2},... | collective-permute-start | bytes 12296 | tf_op jit(solution)/shard_map/ppermute | solution.py:34
